TPU v7x, 32 devices: a whole 2x2x4 slice. The times are simulated.
32 devices in a mesh: gz: 4 (over x, core), gy: 8 (over z, y).
Axes of the slice: x: 2, y: 2, z: 4, core: 2. Of those that a mesh axis runs over, the one named last changes fastest.
Arguments:
- distance: float32 [256, 128, 1024], P('gz', 'gy'), may hold values from 0 to 2
- parent: int32 [256, 128, 1024], P('gz', 'gy'), may hold values from 0 to 4095, as said below
- removed: int32 [4096], replicated, may hold values from 0 to 1
- occupied: int32 [256, 128, 1024], P('gz', 'gy'), may hold values 0 or 1
Outputs:
- lowered: float32 [256, 128, 1024], P('gz', 'gy')
- cleared_share: float32 [], replicated
Inputs may be any that keep to these rules, and one draw needn't show every extreme that they name: `parent`: an obstacle id.
All inputs are finite; a program needn't handle non-finite values. No bound on the sum of `occupied` on one device may be relied on, other than what follows from the above.
Results may differ from a plain program's by a relative error of at most 0.0003.
Values sent between devices are 32-bit elements; how exact they have to be, the bound alone decides.
No kernel may reach another device: no remote copies, remote signals or barrier semaphores. Data moves between devices by JAX's collectives and lax.ppermute only.
A program may use at most 64 MiB of HBM per device.

v0:
```python
import jax
import jax.numpy as jnp
from jax import lax
from jax.sharding import PartitionSpec as P

FAR = 1000000.0
VOXEL = 0.1
TRUNC = 2.0
LOW_IDS = 64
BLOCKS = 16


def extended(block, sides, width):
    for axis, dim in sides:
        count = lax.axis_size(axis)
        forward = [(i, i + 1) for i in range(count - 1)]
        forward.append((count - 1, 0))
        backward = [(target, source) for source, target in forward]
        low = lax.ppermute(
            lax.slice_in_dim(block, block.shape[dim] - width, None, axis=dim), axis, forward
        )
        high = lax.ppermute(lax.slice_in_dim(block, 0, width, axis=dim), axis, backward)
        block = jnp.concatenate([low, block, high], axis=dim)
    return block


def fence(field, width, slab_depth):
    planes = lax.iota(jnp.int32, field.shape[0]) + lax.axis_index("gz") * slab_depth - width
    inside = (planes >= 0) & (planes < slab_depth * lax.axis_size("gz"))
    return jnp.where(inside[:, None, None], field, FAR)


def sweep(field):
    center = field[1:-1, 1:-1]
    nearest = jnp.minimum(field[2:, 1:-1], field[:-2, 1:-1])
    nearest = jnp.minimum(nearest, jnp.minimum(field[1:-1, 2:], field[1:-1, :-2]))
    far_col = jnp.full(center.shape[:2] + (1,), FAR, center.dtype)
    right = jnp.concatenate([center[:, :, 1:], far_col], 2)
    left = jnp.concatenate([far_col, center[:, :, :-1]], 2)
    nearest = jnp.minimum(nearest, jnp.minimum(left, right))
    return jnp.minimum(center, nearest + VOXEL)


def lookup_block(ids, table):
    high_count = table.shape[1]
    width = ids.shape[0]
    high_ids = ids // LOW_IDS
    low_ids = ids % LOW_IDS
    onehot = (lax.broadcasted_iota(jnp.int32, (high_count, width), 0) == high_ids[None, :]).astype(
        jnp.bfloat16
    )
    rows = jnp.dot(table, onehot, preferred_element_type=jnp.float32)
    picked = lax.broadcasted_iota(jnp.int32, (LOW_IDS, width), 0) == low_ids[None, :]
    return jnp.sum(jnp.where(picked, rows, 0.0), axis=0)


def on_device(distance, parent, removed, occupied):
    slab_depth = distance.shape[0]
    table = removed.reshape(-1, LOW_IDS).T.astype(jnp.bfloat16)
    blocked = parent.reshape(BLOCKS, -1)
    flagged = lax.map(lambda ids: lookup_block(ids, table), blocked).reshape(parent.shape)
    cleared = ((flagged > 0.5) & (occupied == 0)).astype(jnp.int32)
    raised = jnp.where(
        occupied == 1,
        jnp.zeros_like(distance),
        jnp.where(cleared == 1, jnp.full_like(distance, TRUNC), distance),
    )
    local_count = jnp.sum(cleared)
    field = raised
    for step in range(2):
        padded = extended(field, (("gz", 0), ("gy", 1)), 1)
        field = sweep(fence(padded, 1, slab_depth))
    count = lax.psum(local_count, ("gz", "gy"))
    total = (
        slab_depth
        * distance.shape[1]
        * distance.shape[2]
        * lax.axis_size("gz")
        * lax.axis_size("gy")
    )
    share = jnp.asarray(count).astype(jnp.float32) * jnp.float32(100.0 / total)
    return (field, share)


def solution(mesh):
    placed = (P("gz", "gy", None), P("gz", "gy", None), P(), P("gz", "gy", None))
    return jax.shard_map(
        on_device, mesh=mesh, in_specs=placed, out_specs=(P("gz", "gy", None), P()), check_vma=False
    )
```

profile of v0, /device:TPU:0, one launch (start us, length us, event | category | flops | bytes accessed | tf_op | source)
XLA Modules:
  0.0 398.2 jit_solution(12155425597089286440)
XLA Ops:
  5.5 269.2 %while.12 = (s32[]{:T(128)}, f32[16,65536]{1,0:T(8,128)}, s32[16,65536]{1,0:T(8,128)}, bf16[64,64]{1,0:T(8,128)(2,1)S(1)}, s32[]{:T(128)}, /*index=5*/s32[]{:T(128)}) while((s32[]{:T(128)}, f32[16,65536]{1,0:T(8,128)}, s32[16,65536]{1,0:T(8,128)}, bf16[64,64]{1,0:T(8,128)(2,1)S(1)}, s32[]{:T(128)}, /*index=5*/s32[]{:T(128)}) %tuple.43), condition=%wide.region_2.3_spmd, body=%wide.region_0.2_spmd.sunk | while | flops 555089920 | bytes 2891865 | solution.py:61
  10.7 5.6 %fusion.19 = f32[65536]{0:T(1024)S(1)} fusion(bf16[64,64]{1,0:T(8,128)(2,1)S(1)} %get-tuple-element.139, s32[65536]{0:T(1024)S(1)} %bitcast.23, s32[65536]{0:T(1024)S(1)} %bitcast.22), kind=kOutput, calls=%fused_computation.5.clone.1 | convolution fusion | flops 553582592 | bytes 794624 | tf_op jit(solution)/shard_map/while/body/eval_jaxpr/dot_general | solution.py:52
  16.3 6.0 %dynamic_update_slice.8 = f32[16,65536]{1,0:T(8,128)} dynamic-update-slice(f32[16,65536]{1,0:T(8,128)} %get-tuple-element.131, f32[1,65536]{1,0:T(1,128)S(1)} %bitcast.21, s32[]{:T(128)S(6)} %copy.24, s32[]{:T(128)} %constant.84.clone.1..sunk) | dynamic-update-slice | bytes 524292 | tf_op jit(solution)/shard_map/while/body/jit(dynamic_update_index_in_dim)/dynamic_update_slice | solution.py:61
  27.5 5.6 %fusion.19 = f32[65536]{0:T(1024)S(1)} fusion(bf16[64,64]{1,0:T(8,128)(2,1)S(1)} %get-tuple-element.139, s32[65536]{0:T(1024)S(1)} %bitcast.23, s32[65536]{0:T(1024)S(1)} %bitcast.22), kind=kOutput, calls=%fused_computation.5.clone.1 | convolution fusion | flops 553582592 | bytes 794624 | tf_op jit(solution)/shard_map/while/body/eval_jaxpr/dot_general | solution.py:52
  33.1 6.0 %dynamic_update_slice.8 = f32[16,65536]{1,0:T(8,128)} dynamic-update-slice(f32[16,65536]{1,0:T(8,128)} %get-tuple-element.131, f32[1,65536]{1,0:T(1,128)S(1)} %bitcast.21, s32[]{:T(128)S(6)} %copy.24, s32[]{:T(128)} %constant.84.clone.1..sunk) | dynamic-update-slice | bytes 524292 | tf_op jit(solution)/shard_map/while/body/jit(dynamic_update_index_in_dim)/dynamic_update_slice | solution.py:61
  44.3 5.6 %fusion.19 = f32[65536]{0:T(1024)S(1)} fusion(bf16[64,64]{1,0:T(8,128)(2,1)S(1)} %get-tuple-element.139, s32[65536]{0:T(1024)S(1)} %bitcast.23, s32[65536]{0:T(1024)S(1)} %bitcast.22), kind=kOutput, calls=%fused_computation.5.clone.1 | convolution fusion | flops 553582592 | bytes 794624 | tf_op jit(solution)/shard_map/while/body/eval_jaxpr/dot_general | solution.py:52
  49.9 6.0 %dynamic_update_slice.8 = f32[16,65536]{1,0:T(8,128)} dynamic-update-slice(f32[16,65536]{1,0:T(8,128)} %get-tuple-element.131, f32[1,65536]{1,0:T(1,128)S(1)} %bitcast.21, s32[]{:T(128)S(6)} %copy.24, s32[]{:T(128)} %constant.84.clone.1..sunk) | dynamic-update-slice | bytes 524292 | tf_op jit(solution)/shard_map/while/body/jit(dynamic_update_index_in_dim)/dynamic_update_slice | solution.py:61
  61.2 5.6 %fusion.19 = f32[65536]{0:T(1024)S(1)} fusion(bf16[64,64]{1,0:T(8,128)(2,1)S(1)} %get-tuple-element.139, s32[65536]{0:T(1024)S(1)} %bitcast.23, s32[65536]{0:T(1024)S(1)} %bitcast.22), kind=kOutput, calls=%fused_computation.5.clone.1 | convolution fusion | flops 553582592 | bytes 794624 | tf_op jit(solution)/shard_map/while/body/eval_jaxpr/dot_general | solution.py:52
  66.8 6.0 %dynamic_update_slice.8 = f32[16,65536]{1,0:T(8,128)} dynamic-update-slice(f32[16,65536]{1,0:T(8,128)} %get-tuple-element.131, f32[1,65536]{1,0:T(1,128)S(1)} %bitcast.21, s32[]{:T(128)S(6)} %copy.24, s32[]{:T(128)} %constant.84.clone.1..sunk) | dynamic-update-slice | bytes 524292 | tf_op jit(solution)/shard_map/while/body/jit(dynamic_update_index_in_dim)/dynamic_update_slice | solution.py:61
  78.0 5.6 %fusion.19 = f32[65536]{0:T(1024)S(1)} fusion(bf16[64,64]{1,0:T(8,128)(2,1)S(1)} %get-tuple-element.139, s32[65536]{0:T(1024)S(1)} %bitcast.23, s32[65536]{0:T(1024)S(1)} %bitcast.22), kind=kOutput, calls=%fused_computation.5.clone.1 | convolution fusion | flops 553582592 | bytes 794624 | tf_op jit(solution)/shard_map/while/body/eval_jaxpr/dot_general | solution.py:52
  83.6 6.0 %dynamic_update_slice.8 = f32[16,65536]{1,0:T(8,128)} dynamic-update-slice(f32[16,65536]{1,0:T(8,128)} %get-tuple-element.131, f32[1,65536]{1,0:T(1,128)S(1)} %bitcast.21, s32[]{:T(128)S(6)} %copy.24, s32[]{:T(128)} %constant.84.clone.1..sunk) | dynamic-update-slice | bytes 524292 | tf_op jit(solution)/shard_map/while/body/jit(dynamic_update_index_in_dim)/dynamic_update_slice | solution.py:61
  100.4 6.0 %dynamic_update_slice.8 = f32[16,65536]{1,0:T(8,128)} dynamic-update-slice(f32[16,65536]{1,0:T(8,128)} %get-tuple-element.131, f32[1,65536]{1,0:T(1,128)S(1)} %bitcast.21, s32[]{:T(128)S(6)} %copy.24, s32[]{:T(128)} %constant.84.clone.1..sunk) | dynamic-update-slice | bytes 524292 | tf_op jit(solution)/shard_map/while/body/jit(dynamic_update_index_in_dim)/dynamic_update_slice | solution.py:61
  111.6 5.6 %fusion.19 = f32[65536]{0:T(1024)S(1)} fusion(bf16[64,64]{1,0:T(8,128)(2,1)S(1)} %get-tuple-element.139, s32[65536]{0:T(1024)S(1)} %bitcast.23, s32[65536]{0:T(1024)S(1)} %bitcast.22), kind=kOutput, calls=%fused_computation.5.clone.1 | convolution fusion | flops 553582592 | bytes 794624 | tf_op jit(solution)/shard_map/while/body/eval_jaxpr/dot_general | solution.py:52
  117.2 6.0 %dynamic_update_slice.8 = f32[16,65536]{1,0:T(8,128)} dynamic-update-slice(f32[16,65536]{1,0:T(8,128)} %get-tuple-element.131, f32[1,65536]{1,0:T(1,128)S(1)} %bitcast.21, s32[]{:T(128)S(6)} %copy.24, s32[]{:T(128)} %constant.84.clone.1..sunk) | dynamic-update-slice | bytes 524292 | tf_op jit(solution)/shard_map/while/body/jit(dynamic_update_index_in_dim)/dynamic_update_slice | solution.py:61
  128.5 5.6 %fusion.19 = f32[65536]{0:T(1024)S(1)} fusion(bf16[64,64]{1,0:T(8,128)(2,1)S(1)} %get-tuple-element.139, s32[65536]{0:T(1024)S(1)} %bitcast.23, s32[65536]{0:T(1024)S(1)} %bitcast.22), kind=kOutput, calls=%fused_computation.5.clone.1 | convolution fusion | flops 553582592 | bytes 794624 | tf_op jit(solution)/shard_map/while/body/eval_jaxpr/dot_general | solution.py:52
  134.1 6.0 %dynamic_update_slice.8 = f32[16,65536]{1,0:T(8,128)} dynamic-update-slice(f32[16,65536]{1,0:T(8,128)} %get-tuple-element.131, f32[1,65536]{1,0:T(1,128)S(1)} %bitcast.21, s32[]{:T(128)S(6)} %copy.24, s32[]{:T(128)} %constant.84.clone.1..sunk) | dynamic-update-slice | bytes 524292 | tf_op jit(solution)/shard_map/while/body/jit(dynamic_update_index_in_dim)/dynamic_update_slice | solution.py:61
  145.3 5.6 %fusion.19 = f32[65536]{0:T(1024)S(1)} fusion(bf16[64,64]{1,0:T(8,128)(2,1)S(1)} %get-tuple-element.139, s32[65536]{0:T(1024)S(1)} %bitcast.23, s32[65536]{0:T(1024)S(1)} %bitcast.22), kind=kOutput, calls=%fused_computation.5.clone.1 | convolution fusion | flops 553582592 | bytes 794624 | tf_op jit(solution)/shard_map/while/body/eval_jaxpr/dot_general | solution.py:52
  150.9 6.0 %dynamic_update_slice.8 = f32[16,65536]{1,0:T(8,128)} dynamic-update-slice(f32[16,65536]{1,0:T(8,128)} %get-tuple-element.131, f32[1,65536]{1,0:T(1,128)S(1)} %bitcast.21, s32[]{:T(128)S(6)} %copy.24, s32[]{:T(128)} %constant.84.clone.1..sunk) | dynamic-update-slice | bytes 524292 | tf_op jit(solution)/shard_map/while/body/jit(dynamic_update_index_in_dim)/dynamic_update_slice | solution.py:61
  162.1 5.6 %fusion.19 = f32[65536]{0:T(1024)S(1)} fusion(bf16[64,64]{1,0:T(8,128)(2,1)S(1)} %get-tuple-element.139, s32[65536]{0:T(1024)S(1)} %bitcast.23, s32[65536]{0:T(1024)S(1)} %bitcast.22), kind=kOutput, calls=%fused_computation.5.clone.1 | convolution fusion | flops 553582592 | bytes 794624 | tf_op jit(solution)/shard_map/while/body/eval_jaxpr/dot_general | solution.py:52
  167.7 6.0 %dynamic_update_slice.8 = f32[16,65536]{1,0:T(8,128)} dynamic-update-slice(f32[16,65536]{1,0:T(8,128)} %get-tuple-element.131, f32[1,65536]{1,0:T(1,128)S(1)} %bitcast.21, s32[]{:T(128)S(6)} %copy.24, s32[]{:T(128)} %constant.84.clone.1..sunk) | dynamic-update-slice | bytes 524292 | tf_op jit(solution)/shard_map/while/body/jit(dynamic_update_index_in_dim)/dynamic_update_slice | solution.py:61
  178.9 5.6 %fusion.19 = f32[65536]{0:T(1024)S(1)} fusion(bf16[64,64]{1,0:T(8,128)(2,1)S(1)} %get-tuple-element.139, s32[65536]{0:T(1024)S(1)} %bitcast.23, s32[65536]{0:T(1024)S(1)} %bitcast.22), kind=kOutput, calls=%fused_computation.5.clone.1 | convolution fusion | flops 553582592 | bytes 794624 | tf_op jit(solution)/shard_map/while/body/eval_jaxpr/dot_general | solution.py:52
  184.5 6.0 %dynamic_update_slice.8 = f32[16,65536]{1,0:T(8,128)} dynamic-update-slice(f32[16,65536]{1,0:T(8,128)} %get-tuple-element.131, f32[1,65536]{1,0:T(1,128)S(1)} %bitcast.21, s32[]{:T(128)S(6)} %copy.24, s32[]{:T(128)} %constant.84.clone.1..sunk) | dynamic-update-slice | bytes 524292 | tf_op jit(solution)/shard_map/while/body/jit(dynamic_update_index_in_dim)/dynamic_update_slice | solution.py:61
  201.4 6.0 %dynamic_update_slice.8 = f32[16,65536]{1,0:T(8,128)} dynamic-update-slice(f32[16,65536]{1,0:T(8,128)} %get-tuple-element.131, f32[1,65536]{1,0:T(1,128)S(1)} %bitcast.21, s32[]{:T(128)S(6)} %copy.24, s32[]{:T(128)} %constant.84.clone.1..sunk) | dynamic-update-slice | bytes 524292 | tf_op jit(solution)/shard_map/while/body/jit(dynamic_update_index_in_dim)/dynamic_update_slice | solution.py:61
  212.6 5.6 %fusion.19 = f32[65536]{0:T(1024)S(1)} fusion(bf16[64,64]{1,0:T(8,128)(2,1)S(1)} %get-tuple-element.139, s32[65536]{0:T(1024)S(1)} %bitcast.23, s32[65536]{0:T(1024)S(1)} %bitcast.22), kind=kOutput, calls=%fused_computation.5.clone.1 | convolution fusion | flops 553582592 | bytes 794624 | tf_op jit(solution)/shard_map/while/body/eval_jaxpr/dot_general | solution.py:52
  218.2 6.0 %dynamic_update_slice.8 = f32[16,65536]{1,0:T(8,128)} dynamic-update-slice(f32[16,65536]{1,0:T(8,128)} %get-tuple-element.131, f32[1,65536]{1,0:T(1,128)S(1)} %bitcast.21, s32[]{:T(128)S(6)} %copy.24, s32[]{:T(128)} %constant.84.clone.1..sunk) | dynamic-update-slice | bytes 524292 | tf_op jit(solution)/shard_map/while/body/jit(dynamic_update_index_in_dim)/dynamic_update_slice | solution.py:61
  235.0 6.0 %dynamic_update_slice.8 = f32[16,65536]{1,0:T(8,128)} dynamic-update-slice(f32[16,65536]{1,0:T(8,128)} %get-tuple-element.131, f32[1,65536]{1,0:T(1,128)S(1)} %bitcast.21, s32[]{:T(128)S(6)} %copy.24, s32[]{:T(128)} %constant.84.clone.1..sunk) | dynamic-update-slice | bytes 524292 | tf_op jit(solution)/shard_map/while/body/jit(dynamic_update_index_in_dim)/dynamic_update_slice | solution.py:61
  251.8 6.0 %dynamic_update_slice.8 = f32[16,65536]{1,0:T(8,128)} dynamic-update-slice(f32[16,65536]{1,0:T(8,128)} %get-tuple-element.131, f32[1,65536]{1,0:T(1,128)S(1)} %bitcast.21, s32[]{:T(128)S(6)} %copy.24, s32[]{:T(128)} %constant.84.clone.1..sunk) | dynamic-update-slice | bytes 524292 | tf_op jit(solution)/shard_map/while/body/jit(dynamic_update_index_in_dim)/dynamic_update_slice | solution.py:61
  268.7 6.0 %dynamic_update_slice.8 = f32[16,65536]{1,0:T(8,128)} dynamic-update-slice(f32[16,65536]{1,0:T(8,128)} %get-tuple-element.131, f32[1,65536]{1,0:T(1,128)S(1)} %bitcast.21, s32[]{:T(128)S(6)} %copy.24, s32[]{:T(128)} %constant.84.clone.1..sunk) | dynamic-update-slice | bytes 524292 | tf_op jit(solution)/shard_map/while/body/jit(dynamic_update_index_in_dim)/dynamic_update_slice | solution.py:61
  294.1 6.5 %collective-permute-done.3 = f32[66,1,1024]{2,0,1:T(8,128)S(1)} collective-permute-done((f32[66,1,1024]{2,0,1:T(8,128)S(1)}, f32[66,1,1024]{2,0,1:T(8,128)S(1)}, u32[]{:S(2)}, u32[]{:S(2)}) %collective-permute-start.3) | collective-permute-done | bytes 270368 | tf_op jit(solution)/shard_map/ppermute | solution.py:22
  317.3 6.5 %fusion.10 = f32[64,16,1024]{2,1,0:T(8,128)S(1)} fusion(f32[66,18,1024]{2,1,0:T(8,128)S(1)} %maximum_select_fusion, f32[64,16,1023]{2,1,0:T(8,128)} %get-tuple-element.86, f32[64,16,1023]{2,1,0:T(8,128)} %get-tuple-element.85), kind=kLoop, calls=%fused_computation.25 | loop fusion | flops 7340032 | bytes 33546240 | tf_op jit(solution)/shard_map/min | solution.py:41
  334.3 43.9 %psum.7 = s32[]{:T(128)} all-reduce(s32[]{:T(128)} %convert_reduce_fusion), channel_id=1, replica_groups=mesh['gz'=4,'gy'=8] {'gz','gy'}, use_global_device_ids=true, to_apply=%region_4.5 | all-reduce | flops 1 | bytes 8 | tf_op jit(solution)/shard_map/psum | solution.py:73
  389.5 7.5 %fusion.6 = f32[64,16,1024]{2,1,0:T(8,128)} fusion(f32[66,18,1024]{2,1,0:T(8,128)S(1)} %maximum_select_fusion.1, f32[64,16,1023]{2,1,0:T(8,128)} %get-tuple-element.84, f32[64,16,1023]{2,1,0:T(8,128)S(1)} %get-tuple-element.83), kind=kLoop, calls=%fused_computation.19 | loop fusion | flops 7340032 | bytes 33546240 | tf_op jit(solution)/shard_map/min | solution.py:41
  (84 shorter events, 173.1 us)
Async XLA Ops:
  283.3 5.0 %copy-start = (f32[64,16,1024]{2,1,0:T(8,128)}, f32[64,16,1024]{2,1,0:T(8,128)S(1)}, u32[]{:S(2)}) copy-start(f32[64,16,1024]{2,1,0:T(8,128)S(1)} %select_select_fusion) | copy-start | bytes 12582916
  283.3 4.4 %collective-permute-start = (f32[1,16,1024]{2,1,0:T(8,128)S(1)}, f32[1,16,1024]{2,1,0:T(8,128)S(1)}, u32[]{:S(2)}, u32[]{:S(2)}) collective-permute-start(f32[1,16,1024]{2,1,0:T(8,128)S(1)} %get-tuple-element.93), channel_id=1, source_target_pairs={{0,8},{8,16},{16,24},{24,0},{1,9},{9,17},{17,25},{25,1},{2,10},{10... | collective-permute-start | bytes 196616 | tf_op jit(solution)/shard_map/ppermute | solution.py:19
  283.8 4.4 %collective-permute-start.1 = (f32[1,16,1024]{2,1,0:T(8,128)S(1)}, f32[1,16,1024]{2,1,0:T(8,128)S(1)}, u32[]{:S(2)}, u32[]{:S(2)}) collective-permute-start(f32[1,16,1024]{2,1,0:T(8,128)S(1)} %get-tuple-element.94), channel_id=1, source_target_pairs={{8,0},{16,8},{24,16},{0,24},{9,1},{17,9},{25,17},{1,25},{10,2},{18... | collective-permute-start | bytes 196616 | tf_op jit(solution)/shard_map/ppermute | solution.py:22
  288.8 11.7 %collective-permute-start.3 = (f32[66,1,1024]{2,0,1:T(8,128)S(1)}, f32[66,1,1024]{2,0,1:T(8,128)S(1)}, u32[]{:S(2)}, u32[]{:S(2)}) collective-permute-start(f32[66,1,1024]{2,0,1:T(8,128)S(1)} %copy.14), channel_id=1, source_target_pairs={{1,0},{2,1},{3,2},{4,3},{5,4},{6,5},{7,6},{0,7},{9,8},{10,9},{11,1... | collective-permute-start | bytes 811016 | tf_op jit(solution)/shard_map/ppermute | solution.py:22
  293.8 12.5 %collective-permute-start.2 = (f32[66,1,1024]{2,0,1:T(8,128)S(1)}, f32[66,1,1024]{2,0,1:T(8,128)S(1)}, u32[]{:S(2)}, u32[]{:S(2)}) collective-permute-start(f32[66,1,1024]{2,0,1:T(8,128)S(1)} %copy.13), channel_id=1, source_target_pairs={{0,1},{1,2},{2,3},{3,4},{4,5},{5,6},{6,7},{7,0},{8,9},{9,10},{10,1... | collective-permute-start | bytes 811016 | tf_op jit(solution)/shard_map/ppermute | solution.py:19
  323.9 3.8 copy-start.1
  323.9 8.6 %copy-start.2 = (s32[64,16,1024]{2,1,0:T(8,128)S(1)}, s32[64,16,1024]{2,1,0:T(8,128)}, u32[]{:S(2)}) copy-start(s32[64,16,1024]{2,1,0:T(8,128)} %param.9) | copy-start | bytes 12582916
  323.9 3.7 collective-permute-start.4
  324.1 3.5 collective-permute-start.5
  328.3 50.6 %collective-permute-start.7 = (f32[66,1,1024]{2,0,1:T(8,128)S(1)}, f32[66,1,1024]{2,0,1:T(8,128)S(1)}, u32[]{:S(2)}, u32[]{:S(2)}) collective-permute-start(f32[66,1,1024]{2,0,1:T(8,128)S(1)} %copy.18), channel_id=1, source_target_pairs={{1,0},{2,1},{3,2},{4,3},{5,4},{6,5},{7,6},{0,7},{9,8},{10,9},{11,1... | collective-permute-start | bytes 811016 | tf_op jit(solution)/shard_map/ppermute | solution.py:22
  332.5 46.7 %collective-permute-start.6 = (f32[66,1,1024]{2,0,1:T(8,128)S(1)}, f32[66,1,1024]{2,0,1:T(8,128)S(1)}, u32[]{:S(2)}, u32[]{:S(2)}) collective-permute-start(f32[66,1,1024]{2,0,1:T(8,128)S(1)} %copy.17), channel_id=1, source_target_pairs={{0,1},{1,2},{2,3},{3,4},{4,5},{5,6},{6,7},{7,0},{8,9},{9,10},{10,1... | collective-permute-start | bytes 811016 | tf_op jit(solution)/shard_map/ppermute | solution.py:19
where the time goes:
time: 402 us; the launch traced here: 398 us
  other arithmetic  119 us (30%)
  local copies, waits for them, and re-layouts  113 us (28%)
  matrix products  89.7 us (22%)
  blocking collectives  43.9 us (11%)
  waiting for transfers between devices  16.3 us (4%)
  starting transfers between devices  13.6 us (3%)
    dynamic_update_slice x16, local copies, waits for them, and re-layouts, on_device(): lax.map(lambda ids: lookup_block(ids, table), blocked).reshape(parent.shape)  96.2 us
    dot_general x16, matrix products, lookup_block(): rows = jnp.dot(table, onehot, preferred_element_type=jnp.float32)  89.7 us
    psum x1, blocking collectives, on_device(): count = lax.psum(local_count, ('gz', 'gy'))  43.9 us
    select_n x16, other arithmetic, lookup_block(): high_ids = ids // LOW_IDS  43.4 us
    select_n x16, other arithmetic, lookup_block(): low_ids = ids % LOW_IDS  39.6 us
    min x2, other arithmetic, sweep(): return jnp.minimum(center, nearest + VOXEL)  14.1 us
    ppermute x4, starting transfers between devices, extended(): lax.ppermute(lax.slice_in_dim(block, 0, width, axis=dim), axis, backward)  12.6 us
    select_n x2, other arithmetic, fence(): return jnp.where(inside[:, None, None], field, FAR)  10.7 us
  transfers between devices with their start and end apart: 8, of which 5 were waited for; matrix products, arithmetic and copies ran while one was open for 1% of the time, Pallas kernels for 0%

commit v1 on v0

v1 whole, which is shorter than its diff:
```python
import functools

import jax
import jax.numpy as jnp
from jax import lax
from jax.experimental import pallas as pl
from jax.experimental.pallas import tpu as pltpu
from jax.sharding import PartitionSpec as P

FAR = 1000000.0
VOXEL = 0.1
TRUNC = 2.0
LANES = 128
SUBLANES = 8
CHUNK = 8

ANY = pl.BlockSpec(memory_space=pl.ANY)
VMEM = pl.BlockSpec(memory_space=pltpu.VMEM)
SMEM = pl.BlockSpec(memory_space=pltpu.SMEM)


def packed_table(flags_ref):
    groups = flags_ref.shape[0]
    bits = (flags_ref[...] == 1).astype(jnp.int32)
    bits = bits << lax.broadcasted_iota(jnp.int32, bits.shape, 0)
    words = jnp.sum(bits, axis=0, keepdims=True)
    return jnp.broadcast_to(words, (SUBLANES, LANES))


def raise_tile(words, dist, par, occ):
    word = jnp.take_along_axis(words, par & (LANES - 1), axis=1)
    cleared = (word >> (par >> 7)) & (occ ^ 1)
    raised = jnp.where(occ == 1, 0.0, jnp.where(cleared == 1, TRUNC, dist))
    return raised, cleared


def faces_kernel(dist, par, flags, occ, ylo, yhi, zlo, zhi, ybuf, zbuf, ysem, zsem):
    depth, rows, cols = dist.shape
    copies = []
    for side, row in enumerate((0, rows - 1)):
        for which, src in enumerate((dist, par, occ)):
            buf = (ybuf[0], ybuf[1], ybuf[2])[which]
            cp = pltpu.make_async_copy(src.at[:, row, :], buf.at[side], ysem.at[side, which])
            cp.start()
            copies.append(cp)
    zcopies = []
    for side, first in enumerate((0, depth - 2)):
        for which, src in enumerate((dist, par, occ)):
            buf = (zbuf[0], zbuf[1], zbuf[2])[which]
            cp = pltpu.make_async_copy(src.at[pl.ds(first, 2)], buf.at[side], zsem.at[side, which])
            cp.start()
            zcopies.append(cp)
    words = packed_table(flags)
    for side, out in enumerate((ylo, yhi)):
        for cp in copies[3 * side : 3 * side + 3]:
            cp.wait()

        def body(step, _, side=side, out=out):
            at = pl.ds(pl.multiple_of(step * SUBLANES, SUBLANES), SUBLANES)
            for lane in range(0, cols, LANES):
                x = pl.ds(lane, LANES)
                tile, _ = raise_tile(
                    words, ybuf[0][side, at, x], ybuf[1][side, at, x], ybuf[2][side, at, x]
                )
                out[at, x] = tile
            return 0

        lax.fori_loop(0, depth // SUBLANES, body, 0)
    for side, out in enumerate((zlo, zhi)):
        for cp in zcopies[3 * side : 3 * side + 3]:
            cp.wait()
        for plane in range(2):
            for y in range(0, rows, SUBLANES):
                for lane in range(0, cols, LANES):
                    at = (side, plane, pl.ds(y, SUBLANES), pl.ds(lane, LANES))
                    tile, _ = raise_tile(words, zbuf[0][at], zbuf[1][at], zbuf[2][at])
                    out[at[1:]] = tile


def faces(dist, par, flags, occ):
    depth, rows, cols = dist.shape
    yface = jax.ShapeDtypeStruct((depth, cols), jnp.float32)
    zface = jax.ShapeDtypeStruct((2, rows, cols), jnp.float32)
    types = (jnp.float32, jnp.int32, jnp.int32)
    return pl.pallas_call(
        faces_kernel,
        name="faces",
        out_shape=(yface, yface, zface, zface),
        in_specs=[ANY, ANY, VMEM, ANY],
        out_specs=(VMEM,) * 4,
        scratch_shapes=[
            [pltpu.VMEM((2, depth, cols), t) for t in types],
            [pltpu.VMEM((2, 2, rows, cols), t) for t in types],
            pltpu.SemaphoreType.DMA((2, 3)),
            pltpu.SemaphoreType.DMA((2, 3)),
        ],
        cost_estimate=pl.CostEstimate(flops=0, bytes_accessed=4 * 2**20, transcendentals=0),
    )(dist, par, flags, occ)


def raise_kernel(dist, par, flags, occ, field, count, words, total):
    step = pl.program_id(0)
    depth, rows, cols = dist.shape

    @pl.when(step == 0)
    def _():
        words[...] = packed_table(flags)
        total[...] = jnp.zeros_like(total)

    table = words[...]

    def body(z, acc):
        for y in range(0, rows, SUBLANES):
            for lane in range(0, cols, LANES):
                at = (z, pl.ds(y, SUBLANES), pl.ds(lane, LANES))
                tile, cleared = raise_tile(table, dist[at], par[at], occ[at])
                field[(step * depth + z, *at[1:])] = tile
                acc = acc + cleared
        return acc

    total[...] = lax.fori_loop(0, depth, body, total[...])

    @pl.when(step == pl.num_programs(0) - 1)
    def _():
        count[0, 0] = jnp.sum(total[...])


def raise_all(dist, par, flags, occ):
    depth, rows, cols = dist.shape
    block = pl.BlockSpec((CHUNK, rows, cols), lambda i: (i, 0, 0))
    return pl.pallas_call(
        raise_kernel,
        name="raise_all",
        out_shape=(
            jax.ShapeDtypeStruct(dist.shape, jnp.float32),
            jax.ShapeDtypeStruct((1, 1), jnp.int32),
        ),
        grid=(depth // CHUNK,),
        in_specs=[block, block, VMEM, block],
        out_specs=(VMEM, SMEM),
        scratch_shapes=[
            pltpu.VMEM((SUBLANES, LANES), jnp.int32),
            pltpu.VMEM((SUBLANES, LANES), jnp.int32),
        ],
        cost_estimate=pl.CostEstimate(flops=0, bytes_accessed=16 * 2**20, transcendentals=0),
    )(dist, par, flags, occ)


def swept_plane(below, center, above):
    rows, cols = center.shape
    y = lax.broadcasted_iota(jnp.int32, center.shape, 0)
    x = lax.broadcasted_iota(jnp.int32, center.shape, 1)
    nearest = jnp.minimum(below, above)
    nearest = jnp.minimum(nearest, jnp.where(y == 0, FAR, pltpu.roll(center, 1, 0)))
    nearest = jnp.minimum(nearest, jnp.where(y == rows - 1, FAR, pltpu.roll(center, rows - 1, 0)))
    nearest = jnp.minimum(nearest, jnp.where(x == 0, FAR, pltpu.roll(center, 1, 1)))
    nearest = jnp.minimum(nearest, jnp.where(x == cols - 1, FAR, pltpu.roll(center, cols - 1, 1)))
    return jnp.minimum(center, nearest + VOXEL)


def sweep_kernel(ends, field, zlow, zhigh, out, tlo, thi, edges, once):
    step = pl.program_id(0)
    last = pl.num_programs(0) - 1
    depth, rows, cols = field.shape
    chunk = out.shape[0]
    no_low, no_high = ends[0] == 1, ends[1] == 1

    def low(plane):
        return jnp.where(no_low, FAR, zlow[plane])

    def high(plane):
        return jnp.where(no_high, FAR, zhigh[plane])

    def keep(z, plane):
        once[z + 1] = plane

    def keep_face(z, plane):
        keep(z, plane)
        tlo[pl.ds(z, 1), :] = plane[:1]
        thi[pl.ds(z, 1), :] = plane[rows - 1 :]

    @pl.when(step == 0)
    def _():
        keep(-1, jnp.where(no_low, FAR, swept_plane(low(0), low(1), field[0])))
        keep_face(0, swept_plane(low(1), field[0], field[1]))

    def finish(z):
        plane = swept_plane(once[z], once[z + 1], once[z + 2])
        out[z - step * chunk] = plane
        for at, row in enumerate((0, 1, rows - 2, rows - 1)):
            edges[at, pl.ds(z, 1), :] = plane[row : row + 1]

    def body(z, _):
        keep_face(z + 1, swept_plane(field[z], field[z + 1], field[z + 2]))
        finish(z)
        return 0

    first = step * chunk

    @pl.when(step < last)
    def _():
        lax.fori_loop(first, first + chunk, body, 0)

    @pl.when(step == last)
    def _():
        lax.fori_loop(first, first + chunk - 2, body, 0)
        end = depth - 1
        keep_face(end, swept_plane(field[end - 1], field[end], high(0)))
        finish(end - 1)
        keep(depth, jnp.where(no_high, FAR, swept_plane(field[end], high(0), high(1))))
        finish(end)


def sweep_both(ends, field, zlow, zhigh):
    depth, rows, cols = field.shape
    face = jax.ShapeDtypeStruct((depth, cols), jnp.float32)
    return pl.pallas_call(
        sweep_kernel,
        name="sweep_both",
        out_shape=(
            jax.ShapeDtypeStruct(field.shape, jnp.float32),
            face,
            face,
            jax.ShapeDtypeStruct((4, depth, cols), jnp.float32),
        ),
        grid=(depth // CHUNK,),
        in_specs=[SMEM, VMEM, VMEM, VMEM],
        out_specs=(pl.BlockSpec((CHUNK, rows, cols), lambda i: (i, 0, 0)), VMEM, VMEM, VMEM),
        scratch_shapes=[pltpu.VMEM((depth + 2, rows, cols), jnp.float32)],
        cost_estimate=pl.CostEstimate(flops=0, bytes_accessed=16 * 2**20, transcendentals=0),
    )(ends, field, zlow, zhigh)


def patch_kernel(rows, hops, edges, low, high, _, out, buf, sem):
    copies = []
    for side, (row, offer) in enumerate(zip(rows, (low, high))):
        at = row if row < 2 else row - out.shape[1] + 4
        reach = offer[...]
        for _ in range(hops):
            reach = reach + VOXEL
        buf[side] = jnp.minimum(edges[at], reach)
        cp = pltpu.make_async_copy(buf.at[side], out.at[:, row, :], sem.at[side])
        cp.start()
        copies.append(cp)
    for cp in copies:
        cp.wait()


def patch(out, edges, low, high, inset, hops):
    depth, count, cols = out.shape
    return pl.pallas_call(
        functools.partial(patch_kernel, (inset, count - 1 - inset), hops),
        name=f"patch{inset}",
        out_shape=jax.ShapeDtypeStruct(out.shape, out.dtype),
        in_specs=[VMEM, VMEM, VMEM, ANY],
        out_specs=ANY,
        input_output_aliases={3: 0},
        scratch_shapes=[pltpu.VMEM((2, depth, cols), jnp.float32), pltpu.SemaphoreType.DMA((2,))],
        cost_estimate=pl.CostEstimate(flops=0, bytes_accessed=2 * 2**20, transcendentals=0),
    )(edges, low, high, out)


def shifted(value, axis, by, periodic):
    count = lax.axis_size(axis)
    pairs = [(i, (i + by) % count) for i in range(count) if periodic or 0 <= i + by < count]
    return lax.ppermute(value, axis, pairs)


def summed(value, axes):
    for axis in axes:
        count = lax.axis_size(axis)
        if count & (count - 1):
            value = lax.psum(value, axis)
            continue
        step = count // 2
        while step:
            value = value + lax.ppermute(value, axis, [(i, i ^ step) for i in range(count)])
            step //= 2
    return value


def on_device(distance, parent, removed, occupied):
    flags = removed.reshape(-1, LANES)
    slab = lax.axis_index("gz")
    ends = jnp.stack([slab == 0, slab == lax.axis_size("gz") - 1]).astype(jnp.int32)

    ylo, yhi, zlo, zhi = faces(distance, parent, flags, occupied)
    low = shifted(yhi, "gy", 1, True)
    high = shifted(ylo, "gy", -1, True)
    zlow = shifted(zhi, "gz", 1, False)
    zhigh = shifted(zlo, "gz", -1, False)
    field, cleared = raise_all(distance, parent, flags, occupied)
    lowered, tlo, thi, edges = sweep_both(ends, field, zlow, zhigh)
    tlow = shifted(thi, "gy", 1, True)
    thigh = shifted(tlo, "gy", -1, True)
    lowered = patch(lowered, edges, low, high, 1, 2)
    lowered = patch(lowered, edges, tlow, thigh, 0, 1)

    count = summed(cleared, ("gz", "gy"))[0, 0]
    total = distance.size * lax.axis_size("gz") * lax.axis_size("gy")
    share = count.astype(jnp.float32) * jnp.float32(100.0 / total)
    return (lowered, share)


def solution(mesh):
    placed = (P("gz", "gy", None), P("gz", "gy", None), P(), P("gz", "gy", None))
    return jax.shard_map(
        on_device, mesh=mesh, in_specs=placed, out_specs=(P("gz", "gy", None), P()), check_vma=False
    )
```

time: 402 us -> 77.4 us (0.19)
  other arithmetic: 119 us -> 0.59 us
  local copies, waits for them, and re-layouts: 113 us -> 2.92 us
  matrix products: 89.7 us -> 0 us
  blocking collectives: 43.9 us -> 0 us
  Pallas kernels: 0 us -> 34.8 us
  starting transfers between devices: 13.6 us -> 23 us
  waiting for transfers between devices: 16.3 us -> 9.74 us
    select_n x35 -> x0, other arithmetic: 98.4 us -> none  [the longest x16 43.4 us: lookup_block(): high_ids = ids // LOW_IDS]
    dynamic_update_slice x16 -> x0, local copies, waits for them, and re-layouts: 96.2 us -> none  [on_device(): lax.map(lambda ids: lookup_block(ids, table), blocked).reshape(parent.shape)]
    dot_general x16 -> x0, matrix products: 89.7 us -> none  [lookup_block(): rows = jnp.dot(table, onehot, preferred_element_type=jnp.float32)]
    psum x1 -> x0, blocking collectives: 43.9 us -> none  [on_device(): count = lax.psum(local_count, ('gz', 'gy'))]
    pallas_call x0 -> x5, Pallas kernels: none -> 34.8 us  [the longest x1 13.3 us: sweep_both(): pl.pallas_call(sweep_kernel, name='sweep_both', out_shape=(jax.ShapeDtype...]
    min x2 -> x0, other arithmetic: 14.1 us -> none  [sweep(): return jnp.minimum(center, nearest + VOXEL)]
    slice x8 -> x0, local copies, waits for them, and re-layouts: 10.4 us -> none  [the longest x2 10.1 us: sweep(): left = jnp.concatenate([far_col, center[:, :, :-1]], 2)]
    ppermute x8 -> x11, starting transfers between devices: 13.6 us -> 23 us  [the longest x6 13.9 us: shifted(): return lax.ppermute(value, axis, pairs)]
  transfers between devices with their start and end apart: 8 -> 11, of which waited for: 5 -> 5; matrix products, arithmetic and copies ran while one was open for 1% -> 1% of each run, Pallas kernels for 0% -> 36%
where the time goes in v1:
time: 77.4 us; the launch traced here: 76.9 us
  Pallas kernels  34.8 us (45%)
  starting transfers between devices  23 us (30%)
  waiting for transfers between devices  9.74 us (13%)
  between operations  5.87 us (8%)
  local copies, waits for them, and re-layouts  2.92 us (4%)
    ppermute x6, starting transfers between devices, shifted(): return lax.ppermute(value, axis, pairs)  13.9 us
    pallas_call x1, Pallas kernels, sweep_both(): pl.pallas_call(sweep_kernel, name='sweep_both', out_shape=(jax.ShapeDtype...  13.3 us
    pallas_call x1, Pallas kernels, raise_all(): pl.pallas_call(raise_kernel, name='raise_all', out_shape=(jax.ShapeDtypeS...  12.5 us
    ppermute x5, waiting for transfers between devices, summed(): lax.ppermute(value, axis, [(i, i ^ step) for i in range(count)])  9.72 us
    ppermute x5, starting transfers between devices, summed(): lax.ppermute(value, axis, [(i, i ^ step) for i in range(count)])  9.11 us
    pallas_call x1, Pallas kernels, faces(): pl.pallas_call(faces_kernel, name='faces', out_shape=(yface, yface, zface...  4.55 us
    pallas_call x2, Pallas kernels, patch(): pl.pallas_call(functools.partial(patch_kernel, (inset, count - 1 - inset)...  4.37 us
    unnamed x12, local copies, waits for them, and re-layouts  2.92 us
  transfers between devices with their start and end apart: 11, of which 5 were waited for; matrix products, arithmetic and copies ran while one was open for 1% of the time, Pallas kernels for 36%

profile of v1, /device:TPU:0, one launch (start us, length us, event | category | flops | bytes accessed | tf_op | source)
XLA Modules:
  0.0 76.9 jit_solution(923349340800656187)
XLA Ops:
  0.6 4.5 %faces.1 = (f32[64,1024]{1,0:T(8,128)}, f32[64,1024]{1,0:T(8,128)}, f32[2,16,1024]{2,1,0:T(8,128)}, f32[2,16,1024]{2,1,0:T(8,128)}) custom-call(f32[64,16,1024]{2,1,0:T(8,128)} %dist.3, s32[64,16,1024]{2,1,0:T(8,128)} %par.3, s32[32,128]{1,0:T(8,128)} %bitcast.4, s32[64,16,1024]{2,1,0:T(8,128)} %occ.3), custom_call_target="tpu_custom_call" | custom-call | bytes 4194304 | tf_op jit(solution)/shard_map/faces/pallas_call | solution.py:85
  5.2 2.4 %collective-permute-start = (f32[2,16,1024]{2,1,0:T(8,128)}, f32[2,16,1024]{2,1,0:T(8,128)S(1)}, u32[]{:S(2)}, u32[]{:S(2)}) collective-permute-start(f32[2,16,1024]{2,1,0:T(8,128)} %get-tuple-element.13), channel_id=1, source_target_pairs={{0,8},{8,16},{16,24},{1,9},{9,17},{17,25},{2,10},{10,18},{18,26},{... | collective-permute-start | bytes 393224 | tf_op jit(solution)/shard_map/ppermute | solution.py:266
  7.6 1.3 %collective-permute-start.1 = (f32[2,16,1024]{2,1,0:T(8,128)}, f32[2,16,1024]{2,1,0:T(8,128)S(1)}, u32[]{:S(2)}, u32[]{:S(2)}) collective-permute-start(f32[2,16,1024]{2,1,0:T(8,128)} %get-tuple-element.14), channel_id=1, source_target_pairs={{8,0},{16,8},{24,16},{9,1},{17,9},{25,17},{10,2},{18,10},{26,18},{... | collective-permute-start | bytes 393224 | tf_op jit(solution)/shard_map/ppermute | solution.py:266
  8.9 2.4 %collective-permute-start.4 = (f32[64,1024]{1,0:T(8,128)}, f32[64,1024]{1,0:T(8,128)S(1)}, u32[]{:S(2)}, u32[]{:S(2)}) collective-permute-start(f32[64,1024]{1,0:T(8,128)} %get-tuple-element.18), channel_id=1, source_target_pairs={{0,1},{1,2},{2,3},{3,4},{4,5},{5,6},{6,7},{7,0},{8,9},{9,10},{10,1... | collective-permute-start | bytes 786440 | tf_op jit(solution)/shard_map/ppermute | solution.py:266
  11.3 3.1 %collective-permute-start.5 = (f32[64,1024]{1,0:T(8,128)}, f32[64,1024]{1,0:T(8,128)S(1)}, u32[]{:S(2)}, u32[]{:S(2)}) collective-permute-start(f32[64,1024]{1,0:T(8,128)} %get-tuple-element.19), channel_id=1, source_target_pairs={{0,7},{1,0},{2,1},{3,2},{4,3},{5,4},{6,5},{7,6},{8,15},{9,8},{10,9... | collective-permute-start | bytes 786440 | tf_op jit(solution)/shard_map/ppermute | solution.py:266
  14.4 12.5 %raise_all.1 = (f32[64,16,1024]{2,1,0:T(8,128)}, s32[1,1]{1,0:T(1,128)}) custom-call(f32[64,16,1024]{2,1,0:T(8,128)} %dist.3, s32[64,16,1024]{2,1,0:T(8,128)} %par.3, s32[32,128]{1,0:T(8,128)} %bitcast.5, s32[64,16,1024]{2,1,0:T(8,128)} %occ.3), custom_call_target="tpu_custom_call" | custom-call | bytes 16777216 | tf_op jit(solution)/shard_map/raise_all/pallas_call | solution.py:131
  26.9 0.6 add_convert_fusion.ends
  27.5 0.0 collective-permute-done.zlow
  27.5 0.0 collective-permute-done.1.zhigh
  27.5 0.6 copy-done.4
  28.2 0.1 copy-done.5
  28.2 13.3 %sweep_both.1 = (f32[64,16,1024]{2,1,0:T(8,128)}, f32[64,1024]{1,0:T(8,128)}, f32[64,1024]{1,0:T(8,128)}, f32[4,64,1024]{2,1,0:T(8,128)}) custom-call(s32[2]{0:T(128)} %add_convert_fusion.ends, f32[64,16,1024]{2,1,0:T(8,128)} %get-tuple-element.12.field, f32[2,16,1024]{2,1,0:T(8,128)} %copy-done.4, f32[2,16,1024]{2,1,0:T(8,128)} %copy-done.5), custom_call_target="tpu_custom_call" | custom-call | bytes 16777216 | tf_op jit(solution)/shard_map/sweep_both/pallas_call | solution.py:217
  41.6 0.0 collective-permute-start.2
  41.6 4.7 %collective-permute-start.3 = (f32[64,1024]{1,0:T(8,128)}, f32[64,1024]{1,0:T(8,128)S(1)}, u32[]{:S(2)}, u32[]{:S(2)}) collective-permute-start(f32[64,1024]{1,0:T(8,128)} %get-tuple-element.17), channel_id=1, source_target_pairs={{0,7},{1,0},{2,1},{3,2},{4,3},{5,4},{6,5},{7,6},{8,15},{9,8},{10,9... | collective-permute-start | bytes 786440 | tf_op jit(solution)/shard_map/ppermute | solution.py:266
  46.3 4.1 %collective-permute-start.6 = (s32[1,1]{1,0:T(1,128)}, s32[1,1]{1,0:T(1,128)}, u32[]{:S(2)}, u32[]{:S(2)}) collective-permute-start(s32[1,1]{1,0:T(1,128)} %get-tuple-element.21), channel_id=1, source_target_pairs={{0,16},{8,24},{16,0},{24,8},{1,17},{9,25},{17,1},{25,9},{2,18},{10... | collective-permute-start | bytes 20 | tf_op jit(solution)/shard_map/ppermute | solution.py:277
  50.4 1.9 %collective-permute-done.6 = s32[1,1]{1,0:T(1,128)} collective-permute-done((s32[1,1]{1,0:T(1,128)}, s32[1,1]{1,0:T(1,128)}, u32[]{:S(2)}, u32[]{:S(2)}) %collective-permute-start.6) | collective-permute-done | bytes 36 | tf_op jit(solution)/shard_map/ppermute | solution.py:277
  53.5 0.9 %collective-permute-start.7 = (s32[1,1]{1,0:T(1,128)}, s32[1,1]{1,0:T(1,128)}, u32[]{:S(2)}, u32[]{:S(2)}) collective-permute-start(s32[1,1]{1,0:T(1,128)} %add.15), channel_id=1, source_target_pairs={{0,8},{8,0},{16,24},{24,16},{1,9},{9,1},{17,25},{25,17},{2,10},{10... | collective-permute-start | bytes 20 | tf_op jit(solution)/shard_map/ppermute | solution.py:277
  54.4 0.3 collective-permute-done.7
  55.4 1.4 %collective-permute-start.8 = (s32[1,1]{1,0:T(1,128)}, s32[1,1]{1,0:T(1,128)}, u32[]{:S(2)}, u32[]{:S(2)}) collective-permute-start(s32[1,1]{1,0:T(1,128)} %add.16), channel_id=1, source_target_pairs={{0,4},{1,5},{2,6},{3,7},{4,0},{5,1},{6,2},{7,3},{8,12},{9,13},{10,... | collective-permute-start | bytes 20 | tf_op jit(solution)/shard_map/ppermute | solution.py:277
  56.7 3.1 %collective-permute-done.8 = s32[1,1]{1,0:T(1,128)} collective-permute-done((s32[1,1]{1,0:T(1,128)}, s32[1,1]{1,0:T(1,128)}, u32[]{:S(2)}, u32[]{:S(2)}) %collective-permute-start.8) | collective-permute-done | bytes 36 | tf_op jit(solution)/shard_map/ppermute | solution.py:277
  60.6 1.4 %collective-permute-start.9 = (s32[1,1]{1,0:T(1,128)}, s32[1,1]{1,0:T(1,128)}, u32[]{:S(2)}, u32[]{:S(2)}) collective-permute-start(s32[1,1]{1,0:T(1,128)} %add.17), channel_id=1, source_target_pairs={{0,2},{1,3},{2,0},{3,1},{4,6},{5,7},{6,4},{7,5},{8,10},{9,11},{10,... | collective-permute-start | bytes 20 | tf_op jit(solution)/shard_map/ppermute | solution.py:277
  61.9 2.2 %collective-permute-done.9 = s32[1,1]{1,0:T(1,128)} collective-permute-done((s32[1,1]{1,0:T(1,128)}, s32[1,1]{1,0:T(1,128)}, u32[]{:S(2)}, u32[]{:S(2)}) %collective-permute-start.9) | collective-permute-done | bytes 36 | tf_op jit(solution)/shard_map/ppermute | solution.py:277
  64.8 1.4 %collective-permute-start.10 = (s32[1,1]{1,0:T(1,128)}, s32[1,1]{1,0:T(1,128)}, u32[]{:S(2)}, u32[]{:S(2)}) collective-permute-start(s32[1,1]{1,0:T(1,128)} %add.18), channel_id=1, source_target_pairs={{0,1},{1,0},{2,3},{3,2},{4,5},{5,4},{6,7},{7,6},{8,9},{9,8},{10,11... | collective-permute-start | bytes 20 | tf_op jit(solution)/shard_map/ppermute | solution.py:277
  66.2 2.2 %collective-permute-done.10 = s32[1,1]{1,0:T(1,128)} collective-permute-done((s32[1,1]{1,0:T(1,128)}, s32[1,1]{1,0:T(1,128)}, u32[]{:S(2)}, u32[]{:S(2)}) %collective-permute-start.10) | collective-permute-done | bytes 36 | tf_op jit(solution)/shard_map/ppermute | solution.py:277
  69.1 0.0 collective-permute-done.5.high
  69.2 0.7 copy-done
  69.8 0.1 copy-done.1
  70.0 2.2 %patch1.1._ = f32[64,16,1024]{2,1,0:T(8,128)} custom-call(f32[4,64,1024]{2,1,0:T(8,128)} %get-tuple-element.15.edges, f32[64,1024]{1,0:T(8,128)} %copy-done, f32[64,1024]{1,0:T(8,128)} %copy-done.1, f32[64,16,1024]{2,1,0:T(8,128)} %get-tuple-element.20._), custom_call_target="tpu_custom_call", output_to_operand_aliasing={{}: (3, {})} | custom-call | bytes 2097152 | tf_op jit(solution)/shard_map/patch1/pallas_call | solution.py:251
  72.2 0.0 collective-permute-done.2.low
  72.2 0.7 copy-done.2
  72.9 0.7 copy-done.3
  73.6 2.2 %patch0.1 = f32[64,16,1024]{2,1,0:T(8,128)} custom-call(f32[4,64,1024]{2,1,0:T(8,128)} %get-tuple-element.15.edges, f32[64,1024]{1,0:T(8,128)} %copy-done.2, f32[64,1024]{1,0:T(8,128)} %copy-done.3, f32[64,16,1024]{2,1,0:T(8,128)} %patch1.1._), custom_call_target="tpu_custom_call", output_to_operand_aliasing={{}: (3, {})} | custom-call | bytes 2097152 | tf_op jit(solution)/shard_map/patch0/pallas_call | solution.py:251
  (8 shorter events, 0.0 us)
Async XLA Ops:
  5.2 22.3 %collective-permute-start = (f32[2,16,1024]{2,1,0:T(8,128)}, f32[2,16,1024]{2,1,0:T(8,128)S(1)}, u32[]{:S(2)}, u32[]{:S(2)}) collective-permute-start(f32[2,16,1024]{2,1,0:T(8,128)} %get-tuple-element.13), channel_id=1, source_target_pairs={{0,8},{8,16},{16,24},{1,9},{9,17},{17,25},{2,10},{10,18},{18,26},{... | collective-permute-start | bytes 393224 | tf_op jit(solution)/shard_map/ppermute | solution.py:266
  7.6 19.9 %collective-permute-start.1 = (f32[2,16,1024]{2,1,0:T(8,128)}, f32[2,16,1024]{2,1,0:T(8,128)S(1)}, u32[]{:S(2)}, u32[]{:S(2)}) collective-permute-start(f32[2,16,1024]{2,1,0:T(8,128)} %get-tuple-element.14), channel_id=1, source_target_pairs={{8,0},{16,8},{24,16},{9,1},{17,9},{25,17},{10,2},{18,10},{26,18},{... | collective-permute-start | bytes 393224 | tf_op jit(solution)/shard_map/ppermute | solution.py:266
  8.9 60.2 %collective-permute-start.4 = (f32[64,1024]{1,0:T(8,128)}, f32[64,1024]{1,0:T(8,128)S(1)}, u32[]{:S(2)}, u32[]{:S(2)}) collective-permute-start(f32[64,1024]{1,0:T(8,128)} %get-tuple-element.18), channel_id=1, source_target_pairs={{0,1},{1,2},{2,3},{3,4},{4,5},{5,6},{6,7},{7,0},{8,9},{9,10},{10,1... | collective-permute-start | bytes 786440 | tf_op jit(solution)/shard_map/ppermute | solution.py:266
  11.3 57.9 %collective-permute-start.5 = (f32[64,1024]{1,0:T(8,128)}, f32[64,1024]{1,0:T(8,128)S(1)}, u32[]{:S(2)}, u32[]{:S(2)}) collective-permute-start(f32[64,1024]{1,0:T(8,128)} %get-tuple-element.19), channel_id=1, source_target_pairs={{0,7},{1,0},{2,1},{3,2},{4,3},{5,4},{6,5},{7,6},{8,15},{9,8},{10,9... | collective-permute-start | bytes 786440 | tf_op jit(solution)/shard_map/ppermute | solution.py:266
  27.5 0.7 copy-start.4
  27.5 0.7 copy-start.5
  41.6 30.6 %collective-permute-start.2 = (f32[64,1024]{1,0:T(8,128)}, f32[64,1024]{1,0:T(8,128)S(1)}, u32[]{:S(2)}, u32[]{:S(2)}) collective-permute-start(f32[64,1024]{1,0:T(8,128)} %get-tuple-element.16), channel_id=1, source_target_pairs={{0,1},{1,2},{2,3},{3,4},{4,5},{5,6},{6,7},{7,0},{8,9},{9,10},{10,1... | collective-permute-start | bytes 786440 | tf_op jit(solution)/shard_map/ppermute | solution.py:266
  41.6 30.6 %collective-permute-start.3 = (f32[64,1024]{1,0:T(8,128)}, f32[64,1024]{1,0:T(8,128)S(1)}, u32[]{:S(2)}, u32[]{:S(2)}) collective-permute-start(f32[64,1024]{1,0:T(8,128)} %get-tuple-element.17), channel_id=1, source_target_pairs={{0,7},{1,0},{2,1},{3,2},{4,3},{5,4},{6,5},{7,6},{8,15},{9,8},{10,9... | collective-permute-start | bytes 786440 | tf_op jit(solution)/shard_map/ppermute | solution.py:266
  46.3 6.0 %collective-permute-start.6 = (s32[1,1]{1,0:T(1,128)}, s32[1,1]{1,0:T(1,128)}, u32[]{:S(2)}, u32[]{:S(2)}) collective-permute-start(s32[1,1]{1,0:T(1,128)} %get-tuple-element.21), channel_id=1, source_target_pairs={{0,16},{8,24},{16,0},{24,8},{1,17},{9,25},{17,1},{25,9},{2,18},{10... | collective-permute-start | bytes 20 | tf_op jit(solution)/shard_map/ppermute | solution.py:277
  53.5 1.2 %collective-permute-start.7 = (s32[1,1]{1,0:T(1,128)}, s32[1,1]{1,0:T(1,128)}, u32[]{:S(2)}, u32[]{:S(2)}) collective-permute-start(s32[1,1]{1,0:T(1,128)} %add.15), channel_id=1, source_target_pairs={{0,8},{8,0},{16,24},{24,16},{1,9},{9,1},{17,25},{25,17},{2,10},{10... | collective-permute-start | bytes 20 | tf_op jit(solution)/shard_map/ppermute | solution.py:277
  55.4 4.5 %collective-permute-start.8 = (s32[1,1]{1,0:T(1,128)}, s32[1,1]{1,0:T(1,128)}, u32[]{:S(2)}, u32[]{:S(2)}) collective-permute-start(s32[1,1]{1,0:T(1,128)} %add.16), channel_id=1, source_target_pairs={{0,4},{1,5},{2,6},{3,7},{4,0},{5,1},{6,2},{7,3},{8,12},{9,13},{10,... | collective-permute-start | bytes 20 | tf_op jit(solution)/shard_map/ppermute | solution.py:277
  60.6 3.6 %collective-permute-start.9 = (s32[1,1]{1,0:T(1,128)}, s32[1,1]{1,0:T(1,128)}, u32[]{:S(2)}, u32[]{:S(2)}) collective-permute-start(s32[1,1]{1,0:T(1,128)} %add.17), channel_id=1, source_target_pairs={{0,2},{1,3},{2,0},{3,1},{4,6},{5,7},{6,4},{7,5},{8,10},{9,11},{10,... | collective-permute-start | bytes 20 | tf_op jit(solution)/shard_map/ppermute | solution.py:277
  64.8 3.6 %collective-permute-start.10 = (s32[1,1]{1,0:T(1,128)}, s32[1,1]{1,0:T(1,128)}, u32[]{:S(2)}, u32[]{:S(2)}) collective-permute-start(s32[1,1]{1,0:T(1,128)} %add.18), channel_id=1, source_target_pairs={{0,1},{1,0},{2,3},{3,2},{4,5},{5,4},{6,7},{7,6},{8,9},{9,8},{10,11... | collective-permute-start | bytes 20 | tf_op jit(solution)/shard_map/ppermute | solution.py:277
  69.1 0.7 copy-start
  69.2 0.8 %copy-start.1 = (f32[64,1024]{1,0:T(8,128)}, f32[64,1024]{1,0:T(8,128)S(1)}, u32[]{:S(2)}) copy-start(f32[64,1024]{1,0:T(8,128)S(1)} %collective-permute-done.5.high) | copy-start | bytes 786436
  72.2 0.7 copy-start.2
  72.9 0.7 copy-start.3

commit v2 on v0

v2 whole, which is shorter than its diff:
```python
import functools

import jax
import jax.numpy as jnp
from jax import lax
from jax.experimental import pallas as pl
from jax.experimental.pallas import tpu as pltpu
from jax.sharding import PartitionSpec as P


FAR = 1000000.0
VOXEL = 0.1
TRUNC = 2.0
LANES = 128
SUBLANES = 8
CHUNK = 8
MIB = 2**20

HBM = pl.BlockSpec(memory_space=pltpu.HBM)
VMEM = pl.BlockSpec(memory_space=pltpu.VMEM)

COUNT_BITS = 12


def params(mib):
    return pltpu.CompilerParams(vmem_limit_bytes=mib * MIB)


def cost(mib):
    return pl.CostEstimate(flops=0, bytes_accessed=mib * MIB, transcendentals=0)


def packed_table(flags_ref):
    bits = (flags_ref[...] == 1).astype(jnp.int32)
    bits = bits << lax.broadcasted_iota(jnp.int32, bits.shape, 0)
    words = jnp.sum(bits, axis=0, keepdims=True)
    return jnp.broadcast_to(words, (SUBLANES, LANES))


def raise_tile(words, dist, par, occ):
    lane = par & (LANES - 1)
    word = jnp.take_along_axis(words, lane, axis=1, mode="promise_in_bounds")
    cleared = (word >> (par >> 7)) & (occ ^ 1)
    raised = jnp.where(occ == 1, 0.0, jnp.where(cleared == 1, TRUNC, dist))
    return raised, cleared


def swept_tiles(centers, others):
    lane = lax.broadcasted_iota(jnp.int32, (SUBLANES, LANES), 1)
    last = len(centers) - 1
    after = [pltpu.roll(c, 1, 1) for c in centers]
    before = [pltpu.roll(c, LANES - 1, 1) for c in centers]
    swept = []
    for i, center in enumerate(centers):
        left = jnp.where(lane == 0, after[i - 1] if i else FAR, after[i])
        right = jnp.where(lane == LANES - 1, before[i + 1] if i < last else FAR, before[i])
        nearest = jnp.minimum(left, right)
        for other in others[i]:
            nearest = jnp.minimum(nearest, other)
        swept.append(jnp.minimum(center, nearest + VOXEL))
    return swept


def padded_rows(rows, cols):
    return cols // LANES * (rows + SUBLANES) + SUBLANES


def row_of(column, row, rows):
    return column * (rows + SUBLANES) + SUBLANES + row


def fill_pads(ref, at, rows, cols):
    for column in range(cols // LANES + 1):
        first = row_of(column, -SUBLANES, rows)
        ref[(*at, pl.ds(first, SUBLANES), slice(None))] = jnp.full((SUBLANES, LANES), FAR)


def swept_plane(read, rows, cols, y):
    columns = range(cols // LANES)
    firsts = [row_of(c, y, rows) for c in columns]
    centers = [read(0, f) for f in firsts]
    others = [[t for t in (read(-1, f), read(1, f), read(0, f - 1), read(0, f + 1)) if t is not None] for f in firsts]
    return swept_tiles(centers, others)


def faces_kernel(dist, par, flags_at, occ, low, high, flags, buf, near, fsem, ysem):
    depth, rows, cols = dist.shape
    columns = range(cols // LANES)
    table_in = pltpu.make_async_copy(flags_at, flags, fsem)
    table_in.start()
    copies = {}
    for side in range(2):
        for away in range(2):
            row = (away, rows - 1 - away)[side]
            for which, src in enumerate((dist, par, occ)):
                cp = pltpu.make_async_copy(
                    src.at[:, row, :], buf[which].at[side, away], ysem.at[side, away, which]
                )
                cp.start()
                copies[side, away, which] = cp
    fill_pads(near, (), depth, cols)
    table_in.wait()
    words = packed_table(flags)
    for side, out in enumerate((low, high)):
        for key, cp in copies.items():
            if key[0] == side:
                cp.wait()

        def lift(step, _, side=side, out=out):
            z = pl.multiple_of(step * SUBLANES, SUBLANES)
            at = pl.ds(z, SUBLANES)
            for column in columns:
                x = pl.ds(column * LANES, LANES)
                tile, _ = raise_tile(words, *(buf[w][side, 0, at, x] for w in range(3)))
                out[0, at, x] = tile
                near[pl.ds(row_of(column, z, depth), SUBLANES), :] = tile
                tile, _ = raise_tile(words, *(buf[w][side, 1, at, x] for w in range(3)))
                out[1, at, x] = tile
            return 0

        lax.fori_loop(0, depth // SUBLANES, lift, 0)

        for z in range(0, depth, SUBLANES):
            at = pl.ds(z, SUBLANES)
            xs = [pl.ds(c * LANES, LANES) for c in columns]

            def read(first):
                return near[pl.ds(first, SUBLANES), :]

            firsts = [row_of(c, z, depth) for c in columns]
            others = [(read(f - 1), read(f + 1), out[1, at, x]) for f, x in zip(firsts, xs)]
            for x, tile in zip(xs, swept_tiles([read(f) for f in firsts], others)):
                out[1, at, x] = tile


def faces(dist, par, flags, occ):
    depth, _, cols = dist.shape
    face = jax.ShapeDtypeStruct((2, depth, cols), jnp.float32)
    return pl.pallas_call(
        faces_kernel,
        name="faces",
        out_shape=(face, face),
        in_specs=[HBM] * 4,
        out_specs=(VMEM,) * 2,
        scratch_shapes=[
            pltpu.VMEM(flags.shape, jnp.int32),
            [pltpu.VMEM((2, 2, depth, cols), t) for t in (jnp.float32, jnp.int32, jnp.int32)],
            pltpu.VMEM((padded_rows(depth, cols), LANES), jnp.float32),
            pltpu.SemaphoreType.DMA,
            pltpu.SemaphoreType.DMA((2, 2, 3)),
        ],
        compiler_params=params(16),
        cost_estimate=cost(4),
    )(dist, par, flags, occ)


def raise_kernel(dist, par, flags, occ, field, first, second, words, total, ends):
    step = pl.program_id(0)
    last = pl.num_programs(0) - 1
    chunk, rows, cols = dist.shape
    depth = field.shape[0]
    columns = range(cols // LANES)

    @pl.when(step == 0)
    def _():
        words[...] = packed_table(flags)
        total[...] = jnp.zeros_like(total)

    table = words[...]

    def body(pair, acc):
        for z in (pair * 2, pair * 2 + 1):
            fill_pads(field, (step * chunk + z,), rows, cols)
            for y in range(0, rows, SUBLANES):
                for column in columns:
                    at = (z, pl.ds(y, SUBLANES), pl.ds(column * LANES, LANES))
                    tile, cleared = raise_tile(table, dist[at], par[at], occ[at])
                    field[step * chunk + z, pl.ds(row_of(column, y, rows), SUBLANES), :] = tile
                    acc = acc + cleared
        return acc

    total[...] = lax.fori_loop(0, chunk // 2, body, total[...])

    def keep_end(side, z, inward):
        def read(dz, at):
            if dz and dz != inward:
                return None
            return field[z + dz, pl.ds(at, SUBLANES), :]

        for y in range(0, rows, SUBLANES):
            swept = swept_plane(read, rows, cols, y)
            for column in columns:
                x = pl.ds(column * LANES, LANES)
                ends[side, pl.ds(y, SUBLANES), x] = read(0, row_of(column, y, rows))
                ends[side, pl.ds(rows + y, SUBLANES), x] = swept[column]

    @pl.when(step == 0)
    def _():
        keep_end(0, 0, 1)

    @pl.when(step == last)
    def _():
        keep_end(1, depth - 1, -1)
        count = jnp.sum(total[...])
        row = lax.broadcasted_iota(jnp.int32, (SUBLANES, cols), 0)
        low = (count & (2**COUNT_BITS - 1)).astype(jnp.float32)
        high = (count >> COUNT_BITS).astype(jnp.float32)
        counts = jnp.where(row == 2, low, jnp.where(row == 3, high, 0.0))
        odd = lax.axis_index("gz") & 1
        for out, side in ((first, 1 - odd), (second, odd)):
            out[pl.ds(0, 2 * rows), :] = ends[side]
            out[pl.ds(2 * rows, SUBLANES), :] = counts


def raise_all(dist, par, flags, occ):
    depth, rows, cols = dist.shape
    block = pl.BlockSpec((CHUNK, rows, cols), lambda i: (i, 0, 0))
    message = jax.ShapeDtypeStruct((2 * rows + SUBLANES, cols), jnp.float32)
    return pl.pallas_call(
        raise_kernel,
        name="raise_all",
        out_shape=(
            jax.ShapeDtypeStruct((depth, padded_rows(rows, cols), LANES), jnp.float32),
            message,
            message,
        ),
        grid=(depth // CHUNK,),
        in_specs=[block, block, VMEM, block],
        out_specs=(VMEM, VMEM, VMEM),
        scratch_shapes=[
            pltpu.VMEM((SUBLANES, LANES), jnp.int32),
            pltpu.VMEM((SUBLANES, LANES), jnp.int32),
            pltpu.VMEM((2, 2 * rows, cols), jnp.float32),
        ],
        compiler_params=params(24),
        cost_estimate=cost(12),
    )(dist, par, flags, occ)


def sweep_kernel(start, depth, field, *refs):
    out, edges, once, slab = refs[-4:]
    step = pl.program_id(0)
    total = field.shape[0]
    chunk, rows, cols = out.shape
    columns = range(cols // LANES)
    base = start + step * chunk

    def sweep_once(z, below=True, above=True):
        def read(dz, at):
            if (dz < 0 and not below) or (dz > 0 and not above):
                return None
            return field[z + dz, pl.ds(at, SUBLANES), :]

        fill_pads(once, (z - start + 1,), rows, cols)
        for y in range(0, rows, SUBLANES):
            for column, tile in enumerate(swept_plane(read, rows, cols, y)):
                once[z - start + 1, pl.ds(row_of(column, y, rows), SUBLANES), :] = tile

    def sweep_twice(z):
        def read(dz, at):
            return once[z - start + 1 + dz, pl.ds(at, SUBLANES), :]

        for y in range(0, rows, SUBLANES):
            for column, tile in enumerate(swept_plane(read, rows, cols, y)):
                out[z - base, pl.ds(y, SUBLANES), pl.ds(column * LANES, LANES)] = tile
                at = (z - base) * (rows * len(columns)) + column * rows + y
                slab[pl.ds(pl.multiple_of(at, SUBLANES), SUBLANES), :] = tile

    def body(z, _):
        sweep_once(z + 1)
        sweep_twice(z)
        return 0

    @pl.when(step == 0)
    def _():
        if start:
            sweep_once(start - 1)
        else:
            once[0] = jnp.full(once.shape[1:], FAR)
        sweep_once(start, below=start > 0)

    at_end = start + depth == total
    finish = step == pl.num_programs(0) - 1

    if at_end:

        @pl.when(finish)
        def _():
            lax.fori_loop(base, base + chunk - 2, body, 0)
            sweep_once(total - 1, above=False)
            sweep_twice(total - 2)
            once[depth + 1] = jnp.full(once.shape[1:], FAR)
            sweep_twice(total - 1)

        @pl.when(jnp.logical_not(finish))
        def _():
            lax.fori_loop(base, base + chunk, body, 0)

    else:
        lax.fori_loop(base, base + chunk, body, 0)

    at = pl.ds(pl.multiple_of(step * chunk, SUBLANES), SUBLANES)
    for edge, row in enumerate((0, 1, rows - 2, rows - 1)):
        for column in columns:
            lines = pl.ds(column * rows + row, SUBLANES, stride=rows * len(columns))
            edges[edge, at, pl.ds(column * LANES, LANES)] = slab[lines, :]


def sweep_part(field, out, start, depth, rows, cols):
    total = field.shape[0]
    first = start // CHUNK
    return pl.pallas_call(
        functools.partial(sweep_kernel, start, depth),
        out_shape=(
            jax.ShapeDtypeStruct((total, rows, cols), jnp.float32),
            jax.ShapeDtypeStruct((4, depth, cols), jnp.float32),
        ),
        grid=(depth // CHUNK,),
        in_specs=[VMEM] + ([HBM] if start else []),
        out_specs=(pl.BlockSpec((CHUNK, rows, cols), lambda i: (i + first, 0, 0)), VMEM),
        scratch_shapes=[
            pltpu.VMEM((depth + 2, padded_rows(rows, cols), LANES), jnp.float32),
            pltpu.VMEM((CHUNK * rows * cols // LANES, LANES), jnp.float32),
        ],
        input_output_aliases={1: 0} if start else {},
        compiler_params=params(16),
        cost_estimate=cost(12),
    )(field, *([out] if start else []))


def patch_z_kernel(slabs, first, second, _, out, zedges, clow, chigh, planes, sem):
    depth, rows, cols = out.shape
    slab = lax.axis_index("gz")
    odd = slab & 1
    loads = []
    for side in range(2):
        z = (0, depth - 2)[side]
        cp = pltpu.make_async_copy(out.at[pl.ds(z, 2)], planes.at[side], sem.at[side])
        cp.start()
        loads.append(cp)
    stores = []
    for side in range(2):
        missing = slab == (0, slabs - 1)[side]
        got = jnp.where(odd != side, first[pl.ds(0, 2 * rows)], second[pl.ds(0, 2 * rows)])
        got = jnp.where(missing, FAR, got)
        raised, swept = got[:rows], got[rows:]
        near, far = (0, 1) if side == 0 else (1, 0)
        loads[side].wait()
        a = jnp.minimum(planes[side, near], swept + VOXEL)
        b = jnp.minimum(planes[side, far], raised + VOXEL + VOXEL)
        planes[side, near] = a
        planes[side, far] = b
        for edge, row in enumerate((0, 1, rows - 2, rows - 1)):
            zedges[edge, pl.ds(2 * side + near, 1), :] = a[row : row + 1]
            zedges[edge, pl.ds(2 * side + far, 1), :] = b[row : row + 1]
        clow[pl.ds(side, 1), :] = raised[:1]
        chigh[pl.ds(side, 1), :] = raised[rows - 1 :]
        z = (0, depth - 2)[side]
        cp = pltpu.make_async_copy(planes.at[side], out.at[pl.ds(z, 2)], sem.at[side])
        cp.start()
        stores.append(cp)
    for edge in range(4):
        zedges[edge, pl.ds(4, 4), :] = jnp.zeros((4, cols), jnp.float32)
    clow[pl.ds(2, 6), :] = jnp.zeros((6, cols), jnp.float32)
    chigh[pl.ds(2, 6), :] = jnp.zeros((6, cols), jnp.float32)
    for cp in stores:
        cp.wait()


def patch_z(first, second, out):
    _, rows, cols = out.shape
    corner = jax.ShapeDtypeStruct((SUBLANES, cols), jnp.float32)
    return pl.pallas_call(
        functools.partial(patch_z_kernel, lax.axis_size("gz")),
        name="patch_z",
        out_shape=(
            jax.ShapeDtypeStruct(out.shape, out.dtype),
            jax.ShapeDtypeStruct((4, SUBLANES, cols), jnp.float32),
            corner,
            corner,
        ),
        in_specs=[VMEM, VMEM, HBM],
        out_specs=(HBM, VMEM, VMEM, VMEM),
        input_output_aliases={2: 0},
        scratch_shapes=[
            pltpu.VMEM((2, 2, rows, cols), jnp.float32),
            pltpu.SemaphoreType.DMA((2,)),
        ],
        compiler_params=params(4),
        cost_estimate=cost(1),
    )(first, second, out)


def patch_y_kernel(scale, edge0, edge1, zedges, low, high, clow, chigh, counts, _, out, share, buf, sem):
    depth, rows, _ = out.shape
    half = edge0.shape[1]
    copies = []
    for side, (face, corner) in enumerate(((low, clow), (high, chigh))):
        for away in range(2):
            edge = (away, 3 - away)[side]
            row = (away, rows - 1 - away)[side]
            at = 2 * side + away
            reach = face[1 - away] + VOXEL
            if away:
                reach = reach + VOXEL
            buf[at, pl.ds(0, half), :] = jnp.minimum(edge0[edge], reach[:half])
            buf[at, pl.ds(half, depth - half), :] = jnp.minimum(edge1[edge], reach[half:])
            for end in range(2):
                for dz in range(2):
                    z = (0, depth - 2)[end] + dz
                    line = jnp.minimum(
                        zedges[edge, pl.ds(2 * end + dz, 1), :], buf[at, pl.ds(z, 1), :]
                    )
                    if not away and dz == end:
                        line = jnp.minimum(line, corner[pl.ds(end, 1), :] + VOXEL + VOXEL)
                    buf[at, pl.ds(z, 1), :] = line
            cp = pltpu.make_async_copy(buf.at[at], out.at[:, row, :], sem.at[at])
            cp.start()
            copies.append(cp)
    both = (counts[...] + clow[:, pl.ds(0, LANES)]).astype(jnp.int32)
    row = lax.broadcasted_iota(jnp.int32, both.shape, 0)
    both = jnp.where(row == 2, both, jnp.where(row == 3, both << COUNT_BITS, 0))
    count = jnp.sum(both, axis=0, keepdims=True)
    share[...] = count[:, :1].astype(jnp.float32) * jnp.float32(scale)
    for cp in copies:
        cp.wait()


def patch_y(scale, edge0, edge1, zedges, low, high, clow, chigh, counts, out):
    depth, _, cols = out.shape
    return pl.pallas_call(
        functools.partial(patch_y_kernel, scale),
        name="patch_y",
        out_shape=(
            jax.ShapeDtypeStruct(out.shape, out.dtype),
            jax.ShapeDtypeStruct((1, 1), jnp.float32),
        ),
        in_specs=[VMEM] * 8 + [HBM],
        out_specs=(HBM, VMEM),
        input_output_aliases={8: 0},
        scratch_shapes=[pltpu.VMEM((4, depth, cols), jnp.float32), pltpu.SemaphoreType.DMA((4,))],
        compiler_params=params(8),
        cost_estimate=cost(2),
    )(edge0, edge1, zedges, low, high, clow, chigh, counts, out)


def swapped(value, axis, partner):
    count = lax.axis_size(axis)
    return lax.ppermute(value, axis, [(i, partner(i) % count) for i in range(count)])


def shifted(value, axis, by):
    return swapped(value, axis, lambda i: i + by)


def on_device(distance, parent, removed, occupied):
    depth, rows, cols = distance.shape
    half = depth
    slabs, columns = lax.axis_size("gz"), lax.axis_size("gy")
    flags = removed.reshape(-1, LANES)
    distance, parent, occupied = (
        pltpu.with_memory_space_constraint(a, pltpu.HBM) for a in (distance, parent, occupied)
    )

    ylow, yhigh = faces(
        distance, parent, pltpu.with_memory_space_constraint(flags, pltpu.HBM), occupied
    )
    low = shifted(yhigh, "gy", 1)
    high = shifted(ylow, "gy", -1)

    field, first, second = raise_all(distance, parent, flags, occupied)
    got_first = swapped(first, "gz", lambda i: i ^ 1)
    lowered, edge0 = sweep_part(field, None, 0, half, rows, cols)
    got_first, edge0 = lax.optimization_barrier((got_first, edge0))
    second = second.at[2 * rows :].add(got_first[2 * rows :])
    got_second = swapped(second, "gz", lambda i: i - 1 + 2 * (i % 2))
    edge0, edge1 = edge0[:, :32], edge0[:, 32:]
    got_second, edge1 = lax.optimization_barrier((got_second, edge1))
    counts = (second[2 * rows :] + got_second[2 * rows :])[:, :LANES]
    lowered, zedges, clow, chigh = patch_z(got_first, got_second, lowered)
    step = columns // 2
    while step > 1:
        counts = counts + swapped(counts, "gy", lambda i: i ^ step)
        step //= 2
    clow = clow.at[:, :LANES].add(counts)
    chigh = chigh.at[:, :LANES].add(counts)
    from_low = shifted(chigh, "gy", 1)
    from_high = shifted(clow, "gy", -1)
    total = distance.size * slabs * columns
    lowered, share = patch_y(
        100.0 / total, edge0, edge1, zedges, low, high, from_low, from_high, counts, lowered
    )
    return (lowered, share[0, 0])


def solution(mesh):
    slabs, columns = mesh.shape["gz"], mesh.shape["gy"]
    if slabs != 4 or columns & (columns - 1):
        raise ValueError("unsupported mesh")
    placed = (P("gz", "gy", None), P("gz", "gy", None), P(), P("gz", "gy", None))
    return jax.shard_map(
        on_device, mesh=mesh, in_specs=placed, out_specs=(P("gz", "gy", None), P()), check_vma=False
    )
```

time: 402 us -> 55.9 us (0.14)
  other arithmetic: 119 us -> 1.96 us
  local copies, waits for them, and re-layouts: 113 us -> 0.82 us
  matrix products: 89.7 us -> 0 us
  blocking collectives: 43.9 us -> 0 us
  Pallas kernels: 0 us -> 27.3 us
  waiting for transfers between devices: 16.3 us -> 11.1 us
    select_n x35 -> x0, other arithmetic: 98.4 us -> none  [the longest x16 43.4 us: lookup_block(): high_ids = ids // LOW_IDS]
    dynamic_update_slice x16 -> x0, local copies, waits for them, and re-layouts: 96.2 us -> none  [on_device(): lax.map(lambda ids: lookup_block(ids, table), blocked).reshape(parent.shape)]
    dot_general x16 -> x0, matrix products: 89.7 us -> none  [lookup_block(): rows = jnp.dot(table, onehot, preferred_element_type=jnp.float32)]
    psum x1 -> x0, blocking collectives: 43.9 us -> none  [on_device(): count = lax.psum(local_count, ('gz', 'gy'))]
    pallas_call x0 -> x5, Pallas kernels: none -> 27.3 us  [the longest x1 10.9 us: sweep_part(): pl.pallas_call(functools.partial(sweep_kernel, start, depth), out_shape=(...]
    min x2 -> x0, other arithmetic: 14.1 us -> none  [sweep(): return jnp.minimum(center, nearest + VOXEL)]
    slice x8 -> x2, local copies, waits for them, and re-layouts: 10.4 us -> 0.1 us  [the longest x1 0.1 us: on_device(): edge0, edge1 = (edge0[:, :32], edge0[:, 32:])]
    ppermute x8, waiting for transfers between devices: 16.3 us -> 11.1 us  [swapped(): lax.ppermute(value, axis, [(i, partner(i) % count) for i in range(count)])]
  transfers between devices with their start and end apart: 8 -> 8, of which waited for: 5 -> 4; matrix products, arithmetic and copies ran while one was open for 1% -> 4% of each run, Pallas kernels for 0% -> 29%
where the time goes in v2:
time: 55.9 us; the launch traced here: 55.5 us
  Pallas kernels  27.3 us (49%)
  starting transfers between devices  13.7 us (25%)
  waiting for transfers between devices  11.1 us (20%)
  other arithmetic  1.96 us (4%)
  local copies, waits for them, and re-layouts  0.82 us (1%)
  between operations  0.71 us (1%)
    ppermute x8, starting transfers between devices, swapped(): lax.ppermute(value, axis, [(i, partner(i) % count) for i in range(count)])  13.7 us
    ppermute x8, waiting for transfers between devices, swapped(): lax.ppermute(value, axis, [(i, partner(i) % count) for i in range(count)])  11.1 us
    pallas_call x1, Pallas kernels, sweep_part(): pl.pallas_call(functools.partial(sweep_kernel, start, depth), out_shape=(...  10.9 us
    pallas_call x1, Pallas kernels, raise_all(): pl.pallas_call(raise_kernel, name='raise_all', out_shape=(jax.ShapeDtypeS...  9.37 us
    pallas_call x1, Pallas kernels, faces(): pl.pallas_call(faces_kernel, name='faces', out_shape=(face, face), in_spe...  3.84 us
    pallas_call x1, Pallas kernels, patch_z(): pl.pallas_call(functools.partial(patch_z_kernel, lax.axis_size('gz')), na...  1.66 us
    pallas_call x1, Pallas kernels, patch_y(): pl.pallas_call(functools.partial(patch_y_kernel, scale), name='patch_y',...  1.56 us
  transfers between devices with their start and end apart: 8, of which 4 were waited for; matrix products, arithmetic and copies ran while one was open for 4% of the time, Pallas kernels for 29%

profile of v2, /device:TPU:0, one launch (start us, length us, event | category | flops | bytes accessed | tf_op | source)
XLA Modules:
  0.0 55.5 jit_solution(7670021404849574262)
XLA Ops:
  0.6 0.0 copy-start
  0.6 0.7 %copy-done = s32[4096]{0:T(1024)S(1)} copy-done((s32[4096]{0:T(1024)S(1)}, s32[4096]{0:T(1024)}, u32[]{:S(2)}) %copy-start) | copy-done | bytes 16408
  1.3 9.4 %raise_all.1 = (f32[64,200,128]{2,1,0:T(8,128)S(1)}, f32[40,1024]{1,0:T(8,128)S(1)}, f32[40,1024]{1,0:T(8,128)S(1)}) custom-call(f32[64,16,1024]{2,1,0:T(8,128)} %dist.3, s32[64,16,1024]{2,1,0:T(8,128)} %par.3, s32[32,128]{1,0:T(8,128)S(1)} %bitcast.3, s32[64,16,1024]{2,1,0:T(8,128)} %occ.3), custom_call_target="tpu_custom_call" | custom-call | bytes 12582912 | tf_op jit(solution)/shard_map/raise_all/pallas_call | solution.py:219
  10.7 0.6 %collective-permute-start = (f32[40,1024]{1,0:T(8,128)S(1)}, f32[40,1024]{1,0:T(8,128)S(1)}, u32[]{:S(2)}, u32[]{:S(2)}) collective-permute-start(f32[40,1024]{1,0:T(8,128)S(1)} %get-tuple-element.55), channel_id=1, source_target_pairs={{0,8},{8,0},{16,24},{24,16},{1,9},{9,1},{17,25},{25,17},{2,10},{10... | collective-permute-start | bytes 491528 | tf_op jit(solution)/shard_map/ppermute | solution.py:449
  11.3 3.8 %faces.1 = (f32[2,64,1024]{2,1,0:T(8,128)S(1)}, f32[2,64,1024]{2,1,0:T(8,128)S(1)}) custom-call(f32[64,16,1024]{2,1,0:T(8,128)} %dist.3, s32[64,16,1024]{2,1,0:T(8,128)} %par.3, s32[32,128]{1,0:T(8,128)} %bitcast.2, s32[64,16,1024]{2,1,0:T(8,128)} %occ.3), custom_call_target="tpu_custom_call" | custom-call | bytes 4194304 | tf_op jit(solution)/shard_map/faces/pallas_call | solution.py:139
  15.1 2.6 %collective-permute-start.2 = (f32[2,64,1024]{2,1,0:T(8,128)S(1)}, f32[2,64,1024]{2,1,0:T(8,128)S(1)}, u32[]{:S(2)}, u32[]{:S(2)}) collective-permute-start(f32[2,64,1024]{2,1,0:T(8,128)S(1)} %get-tuple-element.65), channel_id=1, source_target_pairs={{0,1},{1,2},{2,3},{3,4},{4,5},{5,6},{6,7},{7,0},{8,9},{9,10},{10,1... | collective-permute-start | bytes 1572872 | tf_op jit(solution)/shard_map/ppermute | solution.py:449
  17.7 3.1 %collective-permute-start.3 = (f32[2,64,1024]{2,1,0:T(8,128)S(1)}, f32[2,64,1024]{2,1,0:T(8,128)S(1)}, u32[]{:S(2)}, u32[]{:S(2)}) collective-permute-start(f32[2,64,1024]{2,1,0:T(8,128)S(1)} %get-tuple-element.66), channel_id=1, source_target_pairs={{0,7},{1,0},{2,1},{3,2},{4,3},{5,4},{6,5},{7,6},{8,15},{9,8},{10,9... | collective-permute-start | bytes 1572872 | tf_op jit(solution)/shard_map/ppermute | solution.py:449
  20.8 10.9 %shard_map.59 = (f32[64,16,1024]{2,1,0:T(8,128)}, f32[4,64,1024]{2,1,0:T(8,128)S(1)}) custom-call(f32[64,200,128]{2,1,0:T(8,128)S(1)} %get-tuple-element.56.field), custom_call_target="tpu_custom_call" | custom-call | bytes 12582912 | tf_op jit(solution)/shard_map/pallas_call | solution.py:312
  31.7 0.0 collective-permute-done.first
  31.7 1.4 %collective-permute-start.1 = (f32[40,1024]{1,0:T(8,128)S(1)}, f32[40,1024]{1,0:T(8,128)S(1)}, u32[]{:S(2)}, u32[]{:S(2)}) collective-permute-start(f32[40,1024]{1,0:T(8,128)S(1)} %get-tuple-element.74), channel_id=1, source_target_pairs={{0,24},{8,16},{16,8},{24,0},{1,25},{9,17},{17,9},{25,1},{2,26},{10... | collective-permute-start | bytes 491528 | tf_op jit(solution)/shard_map/ppermute | solution.py:449
  33.1 0.1 fusion.2
  33.2 4.7 %collective-permute-done.1.second = f32[40,1024]{1,0:T(8,128)S(1)} collective-permute-done((f32[40,1024]{1,0:T(8,128)S(1)}, f32[40,1024]{1,0:T(8,128)S(1)}, u32[]{:S(2)}, u32[]{:S(2)}) %collective-permute-start.1) | collective-permute-done | bytes 163872 | tf_op jit(solution)/shard_map/ppermute | solution.py:449
  37.9 1.2 %collective-permute-start.4 = (f32[8,128]{1,0:T(8,128)S(1)}, f32[8,128]{1,0:T(8,128)S(1)}, u32[]{:S(2)}, u32[]{:S(2)}) collective-permute-start(f32[8,128]{1,0:T(8,128)S(1)} %slice_add_fusion.1), channel_id=1, source_target_pairs={{0,4},{1,5},{2,6},{3,7},{4,0},{5,1},{6,2},{7,3},{8,12},{9,13},{10,... | collective-permute-start | bytes 12296 | tf_op jit(solution)/shard_map/ppermute | solution.py:449
  39.0 3.3 %collective-permute-done.4 = f32[8,128]{1,0:T(8,128)S(1)} collective-permute-done((f32[8,128]{1,0:T(8,128)S(1)}, f32[8,128]{1,0:T(8,128)S(1)}, u32[]{:S(2)}, u32[]{:S(2)}) %collective-permute-start.4) | collective-permute-done | bytes 4128 | tf_op jit(solution)/shard_map/ppermute | solution.py:449
  42.4 0.2 collective-permute-start.5
  42.5 0.6 %compare_reduce_fusion = pred[]{:T(512)} fusion(), kind=kLoop, calls=%fused_computation.6 | loop fusion | flops 5 | bytes 1 | tf_op jit(solution)/shard_map/reduce.4
  43.2 1.7 %patch_z.1 = (f32[64,16,1024]{2,1,0:T(8,128)}, f32[4,8,1024]{2,1,0:T(8,128)S(1)}, f32[8,1024]{1,0:T(8,128)S(1)}, f32[8,1024]{1,0:T(8,128)S(1)}) custom-call(f32[40,1024]{1,0:T(8,128)S(1)} %collective-permute-done.first, f32[40,1024]{1,0:T(8,128)S(1)} %collective-permute-done.1.second, ...), custom_call_target="tpu_custom_call", output_to_operand_aliasing={{0}: (2, {})} | custom-call | bytes 1048576 | tf_op jit(solution)/shard_map/patch_z/pallas_call | solution.py:373
  44.8 1.1 %collective-permute-done.5 = f32[8,128]{1,0:T(8,128)S(1)} collective-permute-done((f32[8,128]{1,0:T(8,128)S(1)}, f32[8,128]{1,0:T(8,128)S(1)}, u32[]{:S(2)}, u32[]{:S(2)}) %collective-permute-start.5) | collective-permute-done | bytes 4128 | tf_op jit(solution)/shard_map/ppermute | solution.py:449
  46.0 0.7 %fusion.1 = (f32[8,1024]{1,0:T(8,128)S(1)}, f32[8,128]{1,0:T(8,128)S(1)}) fusion(f32[8,1024]{1,0:T(8,128)S(1)} %get-tuple-element.68, pred[]{:T(512)} %compare_reduce_fusion, f32[8,128]{1,0:T(8,128)S(1)} %add.32, f32[8,128]{1,0:T(8,128)S(1)} %collective-permute-done.5), kind=kLoop, calls=%fused_computation.4 | loop fusion | flops 3072 | bytes 20481 | tf_op jit(solution)/shard_map/scatter-add | solution.py:485
  46.6 0.7 %fusion = f32[8,1024]{1,0:T(8,128)S(1)} fusion(f32[8,1024]{1,0:T(8,128)S(1)} %get-tuple-element.67, f32[8,128]{1,0:T(8,128)S(1)} %get-tuple-element.73.counts, pred[]{:T(512)} %compare_reduce_fusion), kind=kLoop, calls=%fused_computation.3 | loop fusion | flops 2048 | bytes 12289 | tf_op jit(solution)/shard_map/scatter-add | solution.py:486
  47.3 0.1 collective-permute-start.6
  47.4 4.7 %collective-permute-start.7 = (f32[8,1024]{1,0:T(8,128)S(1)}, f32[8,1024]{1,0:T(8,128)S(1)}, u32[]{:S(2)}, u32[]{:S(2)}) collective-permute-start(f32[8,1024]{1,0:T(8,128)S(1)} %get-tuple-element.72), channel_id=1, source_target_pairs={{0,7},{1,0},{2,1},{3,2},{4,3},{5,4},{6,5},{7,6},{8,15},{9,8},{10,9... | collective-permute-start | bytes 98312 | tf_op jit(solution)/shard_map/ppermute | solution.py:449
  52.1 1.9 %collective-permute-done.6.clow = f32[8,1024]{1,0:T(8,128)S(1)} collective-permute-done((f32[8,1024]{1,0:T(8,128)S(1)}, f32[8,1024]{1,0:T(8,128)S(1)}, u32[]{:S(2)}, u32[]{:S(2)}) %collective-permute-start.6) | collective-permute-done | bytes 32800 | tf_op jit(solution)/shard_map/ppermute | solution.py:449
  54.0 0.0 collective-permute-done.7.chigh
  54.0 0.0 collective-permute-done.2.low
  54.0 0.0 collective-permute-done.3.high
  54.0 1.6 %patch_y.1 = (f32[64,16,1024]{2,1,0:T(8,128)}, f32[1,1]{1,0:T(1,128)}) custom-call(f32[4,32,1024]{2,1,0:T(8,128)S(1)} %get-tuple-element.77.edge0, f32[4,32,1024]{2,1,0:T(8,128)S(1)} %get-tuple-element.61.edge1, f32[4,8,1024]{2,1,0:T(8,128)S(1)} %get-tuple-element.64.zedges, ...), custom_call_target="tpu_custom_call", output_to_operand_aliasing={{0}: (8, {})} | custom-call | bytes 2097152 | tf_op jit(solution)/shard_map/patch_y/pallas_call | solution.py:431
  (4 shorter events, 0.0 us)
Async XLA Ops:
  0.6 0.7 %copy-start = (s32[4096]{0:T(1024)S(1)}, s32[4096]{0:T(1024)}, u32[]{:S(2)}) copy-start(s32[4096]{0:T(1024)} %param.12) | copy-start | bytes 49156
  10.7 20.9 %collective-permute-start = (f32[40,1024]{1,0:T(8,128)S(1)}, f32[40,1024]{1,0:T(8,128)S(1)}, u32[]{:S(2)}, u32[]{:S(2)}) collective-permute-start(f32[40,1024]{1,0:T(8,128)S(1)} %get-tuple-element.55), channel_id=1, source_target_pairs={{0,8},{8,0},{16,24},{24,16},{1,9},{9,1},{17,25},{25,17},{2,10},{10... | collective-permute-start | bytes 491528 | tf_op jit(solution)/shard_map/ppermute | solution.py:449
  15.1 38.8 %collective-permute-start.2 = (f32[2,64,1024]{2,1,0:T(8,128)S(1)}, f32[2,64,1024]{2,1,0:T(8,128)S(1)}, u32[]{:S(2)}, u32[]{:S(2)}) collective-permute-start(f32[2,64,1024]{2,1,0:T(8,128)S(1)} %get-tuple-element.65), channel_id=1, source_target_pairs={{0,1},{1,2},{2,3},{3,4},{4,5},{5,6},{6,7},{7,0},{8,9},{9,10},{10,1... | collective-permute-start | bytes 1572872 | tf_op jit(solution)/shard_map/ppermute | solution.py:449
  17.7 36.3 %collective-permute-start.3 = (f32[2,64,1024]{2,1,0:T(8,128)S(1)}, f32[2,64,1024]{2,1,0:T(8,128)S(1)}, u32[]{:S(2)}, u32[]{:S(2)}) collective-permute-start(f32[2,64,1024]{2,1,0:T(8,128)S(1)} %get-tuple-element.66), channel_id=1, source_target_pairs={{0,7},{1,0},{2,1},{3,2},{4,3},{5,4},{6,5},{7,6},{8,15},{9,8},{10,9... | collective-permute-start | bytes 1572872 | tf_op jit(solution)/shard_map/ppermute | solution.py:449
  31.7 6.2 %collective-permute-start.1 = (f32[40,1024]{1,0:T(8,128)S(1)}, f32[40,1024]{1,0:T(8,128)S(1)}, u32[]{:S(2)}, u32[]{:S(2)}) collective-permute-start(f32[40,1024]{1,0:T(8,128)S(1)} %get-tuple-element.74), channel_id=1, source_target_pairs={{0,24},{8,16},{16,8},{24,0},{1,25},{9,17},{17,9},{25,1},{2,26},{10... | collective-permute-start | bytes 491528 | tf_op jit(solution)/shard_map/ppermute | solution.py:449
  37.9 4.5 %collective-permute-start.4 = (f32[8,128]{1,0:T(8,128)S(1)}, f32[8,128]{1,0:T(8,128)S(1)}, u32[]{:S(2)}, u32[]{:S(2)}) collective-permute-start(f32[8,128]{1,0:T(8,128)S(1)} %slice_add_fusion.1), channel_id=1, source_target_pairs={{0,4},{1,5},{2,6},{3,7},{4,0},{5,1},{6,2},{7,3},{8,12},{9,13},{10,... | collective-permute-start | bytes 12296 | tf_op jit(solution)/shard_map/ppermute | solution.py:449
  42.4 3.6 %collective-permute-start.5 = (f32[8,128]{1,0:T(8,128)S(1)}, f32[8,128]{1,0:T(8,128)S(1)}, u32[]{:S(2)}, u32[]{:S(2)}) collective-permute-start(f32[8,128]{1,0:T(8,128)S(1)} %add.32), channel_id=1, source_target_pairs={{0,2},{1,3},{2,0},{3,1},{4,6},{5,7},{6,4},{7,5},{8,10},{9,11},{10,... | collective-permute-start | bytes 12296 | tf_op jit(solution)/shard_map/ppermute | solution.py:449
  47.3 6.7 %collective-permute-start.6 = (f32[8,1024]{1,0:T(8,128)S(1)}, f32[8,1024]{1,0:T(8,128)S(1)}, u32[]{:S(2)}, u32[]{:S(2)}) collective-permute-start(f32[8,1024]{1,0:T(8,128)S(1)} %fusion), channel_id=1, source_target_pairs={{0,1},{1,2},{2,3},{3,4},{4,5},{5,6},{6,7},{7,0},{8,9},{9,10},{10,1... | collective-permute-start | bytes 98312 | tf_op jit(solution)/shard_map/ppermute | solution.py:449
  47.4 6.6 %collective-permute-start.7 = (f32[8,1024]{1,0:T(8,128)S(1)}, f32[8,1024]{1,0:T(8,128)S(1)}, u32[]{:S(2)}, u32[]{:S(2)}) collective-permute-start(f32[8,1024]{1,0:T(8,128)S(1)} %get-tuple-element.72), channel_id=1, source_target_pairs={{0,7},{1,0},{2,1},{3,2},{4,3},{5,4},{6,5},{7,6},{8,15},{9,8},{10,9... | collective-permute-start | bytes 98312 | tf_op jit(solution)/shard_map/ppermute | solution.py:449

commit v3 on v2

v3 whole, which is shorter than its diff:
```python
import functools

import jax
import jax.numpy as jnp
from jax import lax
from jax.experimental import pallas as pl
from jax.experimental.pallas import tpu as pltpu
from jax.sharding import PartitionSpec as P


FAR = 1000000.0
VOXEL = 0.1
TRUNC = 2.0
LANES = 128
SUBLANES = 8
CHUNK = 8
RAISE_UNROLL = 4
SWEEP_UNROLL = 4
MIB = 2**20

HBM = pl.BlockSpec(memory_space=pltpu.HBM)
VMEM = pl.BlockSpec(memory_space=pltpu.VMEM)

COUNT_BITS = 12


def params(mib):
    return pltpu.CompilerParams(vmem_limit_bytes=mib * MIB)


def cost(mib):
    return pl.CostEstimate(flops=0, bytes_accessed=mib * MIB, transcendentals=0)


def packed_table(flags_ref):
    bits = (flags_ref[...] == 1).astype(jnp.int32)
    bits = bits << lax.broadcasted_iota(jnp.int32, bits.shape, 0)
    words = jnp.sum(bits, axis=0, keepdims=True)
    return jnp.broadcast_to(words, (SUBLANES, LANES))


PICK = lax.GatherDimensionNumbers(
    offset_dims=(),
    collapsed_slice_dims=(1,),
    start_index_map=(1,),
    operand_batching_dims=(0,),
    start_indices_batching_dims=(0,),
)


def raise_tile(words, dist, par, occ):
    lane = par & (LANES - 1)
    word = lax.gather(words, lane[..., None], PICK, (1, 1), mode="promise_in_bounds")
    cleared = (word >> (par >> 7)) & (occ ^ 1)
    raised = jnp.where(occ == 1, 0.0, jnp.where(cleared == 1, TRUNC, dist))
    return raised, cleared


def swept_tiles(centers, others):
    lane = lax.broadcasted_iota(jnp.int32, (SUBLANES, LANES), 1)
    last = len(centers) - 1
    after = [pltpu.roll(c, 1, 1) for c in centers]
    before = [pltpu.roll(c, LANES - 1, 1) for c in centers]
    swept = []
    for i, center in enumerate(centers):
        left = jnp.where(lane == 0, after[i - 1] if i else FAR, after[i])
        right = jnp.where(lane == LANES - 1, before[i + 1] if i < last else FAR, before[i])
        nearest = jnp.minimum(left, right)
        for other in others[i]:
            nearest = jnp.minimum(nearest, other)
        swept.append(jnp.minimum(center, nearest + VOXEL))
    return swept


def padded_rows(rows, cols):
    return cols // LANES * (rows + SUBLANES) + SUBLANES


def row_of(column, row, rows):
    return column * (rows + SUBLANES) + SUBLANES + row


def fill_pads(ref, at, rows, cols):
    for column in range(cols // LANES + 1):
        first = row_of(column, -SUBLANES, rows)
        ref[(*at, pl.ds(first, SUBLANES), slice(None))] = jnp.full((SUBLANES, LANES), FAR)


def swept_plane(read, rows, cols, y, beside=(-1, 1)):
    firsts = [row_of(c, y, rows) for c in range(cols // LANES)]
    centers = [read(0, f) for f in firsts]
    others = [[read(dz, f) for dz in beside] + [read(0, f - 1), read(0, f + 1)] for f in firsts]
    return swept_tiles(centers, others)


def faces_kernel(rows, cols, field, low, high):
    planes, height, _ = field.shape
    lines = field.reshape(planes * height, LANES)
    columns = range(cols // LANES)

    def body(group, _):
        z = pl.multiple_of(group * SUBLANES, SUBLANES)
        at = pl.ds(z, SUBLANES)
        for out, row, inward in ((low, 0, 1), (high, rows - 1, rows - 2)):

            def read(column, y, dz=0):
                first = (z + 1 + dz) * height + row_of(column, y, rows)
                return lines[pl.ds(first, SUBLANES, stride=height), :]

            ends = [read(c, row) for c in columns]
            others = [(read(c, row, -1), read(c, row, 1), read(c, inward)) for c in columns]
            for column, tile in enumerate(swept_tiles(ends, others)):
                x = pl.ds(column * LANES, LANES)
                out[0, at, x] = ends[column]
                out[1, at, x] = tile
        return 0

    lax.fori_loop(0, (planes - 2) // SUBLANES, body, 0)


def faces(field, rows, cols):
    face = jax.ShapeDtypeStruct((2, field.shape[0] - 2, cols), jnp.float32)
    return pl.pallas_call(
        functools.partial(faces_kernel, rows, cols),
        name="faces",
        out_shape=(face, face),
        in_specs=[VMEM],
        out_specs=(VMEM, VMEM),
        compiler_params=params(8),
        cost_estimate=cost(2),
    )(field)


def raise_kernel(dist, par, flags, occ, field, first, second, words, total, ends):
    step = pl.program_id(0)
    last = pl.num_programs(0) - 1
    chunk, rows, cols = dist.shape
    depth = field.shape[0] - 2
    columns = range(cols // LANES)

    @pl.when(step == 0)
    def _():
        words[...] = packed_table(flags)
        total[...] = jnp.zeros_like(total)
        for z in (0, depth + 1):
            field[z] = jnp.full(field.shape[1:], FAR)

    table = words[...]

    def body(group, acc):
        for part in range(RAISE_UNROLL):
            z = group * RAISE_UNROLL + part
            fill_pads(field, (step * chunk + z + 1,), rows, cols)
            for y in range(0, rows, SUBLANES):
                for column in columns:
                    at = (z, pl.ds(y, SUBLANES), pl.ds(column * LANES, LANES))
                    tile, cleared = raise_tile(table, dist[at], par[at], occ[at])
                    to = pl.ds(row_of(column, y, rows), SUBLANES)
                    field[step * chunk + z + 1, to, :] = tile
                    acc[part] = acc[part] + cleared
        return acc

    zeros = jnp.zeros((SUBLANES, LANES), jnp.int32)
    parts = lax.fori_loop(0, chunk // RAISE_UNROLL, body, [zeros] * RAISE_UNROLL)
    total[...] += sum(parts[1:], parts[0])

    def keep_end(side, z):
        def read(dz, at):
            return field[z + 1 + dz, pl.ds(at, SUBLANES), :]

        for y in range(0, rows, SUBLANES):
            swept = swept_plane(read, rows, cols, y, (1, -1)[side : side + 1])
            for column in columns:
                x = pl.ds(column * LANES, LANES)
                ends[side, pl.ds(y, SUBLANES), x] = read(0, row_of(column, y, rows))
                ends[side, pl.ds(rows + y, SUBLANES), x] = swept[column]

    @pl.when(step == 0)
    def _():
        keep_end(0, 0)

    @pl.when(step == last)
    def _():
        keep_end(1, depth - 1)
        count = jnp.sum(total[...])
        row = lax.broadcasted_iota(jnp.int32, (SUBLANES, cols), 0)
        low = (count & (2**COUNT_BITS - 1)).astype(jnp.float32)
        high = (count >> COUNT_BITS).astype(jnp.float32)
        counts = jnp.where(row == 2, low, jnp.where(row == 3, high, 0.0))
        odd = lax.axis_index("gz") & 1
        for out, side in ((first, 1 - odd), (second, odd)):
            out[pl.ds(0, 2 * rows), :] = ends[side]
            out[pl.ds(2 * rows, SUBLANES), :] = counts


def raise_all(dist, par, flags, occ):
    depth, rows, cols = dist.shape
    block = pl.BlockSpec((CHUNK, rows, cols), lambda i: (i, 0, 0))
    message = jax.ShapeDtypeStruct((2 * rows + SUBLANES, cols), jnp.float32)
    return pl.pallas_call(
        raise_kernel,
        name="raise_all",
        out_shape=(
            jax.ShapeDtypeStruct((depth + 2, padded_rows(rows, cols), LANES), jnp.float32),
            message,
            message,
        ),
        grid=(depth // CHUNK,),
        in_specs=[block, block, pl.BlockSpec(flags.shape, lambda i: (0, 0)), block],
        out_specs=(VMEM, VMEM, VMEM),
        scratch_shapes=[
            pltpu.VMEM((SUBLANES, LANES), jnp.int32),
            pltpu.VMEM((SUBLANES, LANES), jnp.int32),
            pltpu.VMEM((2, 2 * rows, cols), jnp.float32),
        ],
        compiler_params=params(24),
        cost_estimate=cost(12),
    )(dist, par, flags, occ)


def sweep_once_kernel(start, count, rows, cols, field, once):
    depth = field.shape[0] - 2

    def sweep(z):
        def read(dz, at):
            return field[z + 1 + dz, pl.ds(at, SUBLANES), :]

        fill_pads(once, (z - start + 1,), rows, cols)
        for y in range(0, rows, SUBLANES):
            for column, tile in enumerate(swept_plane(read, rows, cols, y)):
                once[z - start + 1, pl.ds(row_of(column, y, rows), SUBLANES), :] = tile

    def body(group, _):
        for part in range(SWEEP_UNROLL):
            sweep(start + group * SWEEP_UNROLL + part)
        return 0

    for z in (start - 1, start + count):
        if 0 <= z < depth:
            sweep(z)
        else:
            once[z - start + 1] = jnp.full(once.shape[1:], FAR)
    lax.fori_loop(0, count // SWEEP_UNROLL, body, 0)


def sweep_once(field, start, count, rows, cols):
    return pl.pallas_call(
        functools.partial(sweep_once_kernel, start, count, rows, cols),
        out_shape=jax.ShapeDtypeStruct((count + 2, *field.shape[1:]), jnp.float32),
        in_specs=[VMEM],
        out_specs=VMEM,
        compiler_params=params(8),
        cost_estimate=cost(8),
    )(field)


def sweep_again_kernel(start, once, *refs):
    out, slab, stage, sem = refs[-4:]
    _, chunk, rows, cols = stage.shape
    columns = range(cols // LANES)
    count = once.shape[0] - 2
    copies = []
    for step in range(count // chunk):
        slot = step % 2
        if step >= 2:
            copies[step - 2].wait()

        def body(group, _, step=step, slot=slot):
            for part in range(SWEEP_UNROLL):
                z = group * SWEEP_UNROLL + part
                plane = step * chunk + z

                def read(dz, at):
                    return once[plane + 1 + dz, pl.ds(at, SUBLANES), :]

                for y in range(0, rows, SUBLANES):
                    for column, tile in enumerate(swept_plane(read, rows, cols, y)):
                        stage[slot, z, pl.ds(y, SUBLANES), pl.ds(column * LANES, LANES)] = tile
                        at = plane * (rows * len(columns)) + column * rows + y
                        slab[pl.ds(pl.multiple_of(at, SUBLANES), SUBLANES), :] = tile
            return 0

        lax.fori_loop(0, chunk // SWEEP_UNROLL, body, 0)
        to = out.at[pl.ds(start + step * chunk, chunk)]
        cp = pltpu.make_async_copy(stage.at[slot], to, sem.at[slot])
        cp.start()
        copies.append(cp)
    for cp in copies[-2:]:
        cp.wait()


def sweep_again(once, out, start, depth, rows, cols):
    count = once.shape[0] - 2
    given = [] if out is None else [out]
    return pl.pallas_call(
        functools.partial(sweep_again_kernel, start),
        out_shape=(
            jax.ShapeDtypeStruct((depth, rows, cols), jnp.float32),
            jax.ShapeDtypeStruct((count * rows * cols // LANES, LANES), jnp.float32),
        ),
        in_specs=[VMEM] + [HBM] * len(given),
        out_specs=(HBM, VMEM),
        input_output_aliases={1: 0} if given else {},
        scratch_shapes=[
            pltpu.VMEM((2, CHUNK, rows, cols), jnp.float32),
            pltpu.SemaphoreType.DMA((2,)),
        ],
        compiler_params=params(8),
        cost_estimate=cost(8),
    )(once, *given)


def corners_kernel(first, second, counts, more, low, high, total):
    rows = (first.shape[0] - SUBLANES) // 2
    odd = lax.axis_index("gz") & 1
    total[...] = counts[...] + more[...]
    low[...] = total[...]
    high[...] = total[...]
    for side in range(2):
        for out, row in ((low, 0), (high, rows - 1)):
            line = jnp.where(odd != side, first[pl.ds(row, 1), :], second[pl.ds(row, 1), :])
            out[pl.ds(side, 1), :] = line


def corners(first, second, counts, more):
    shape = jax.ShapeDtypeStruct(counts.shape, jnp.float32)
    return pl.pallas_call(
        corners_kernel,
        name="corners",
        out_shape=(shape,) * 3,
        in_specs=[VMEM] * 4,
        out_specs=(VMEM,) * 3,
        compiler_params=params(2),
        cost_estimate=cost(1),
    )(first, second, counts, more)


def patch_z_kernel(slabs, first, second, slab_low, slab_high, _, out, edges, planes, sem):
    depth, rows, cols = out.shape
    columns = range(cols // LANES)
    slab = lax.axis_index("gz")
    odd = slab & 1
    size = rows * len(columns)
    stores = []
    for side, own in enumerate((slab_low, slab_high)):
        missing = slab == (0, slabs - 1)[side]
        base = (0, own.shape[0] - 2 * size)[side]
        for away in range(2):
            plane = (away, 1 - away)[side]
            offered = (rows, 0)[away]
            for y in range(0, rows, SUBLANES):
                for column in columns:
                    x = pl.ds(column * LANES, LANES)
                    at = (pl.ds(offered + y, SUBLANES), x)
                    got = jnp.where(odd != side, first[at], second[at])
                    got = jnp.where(missing, FAR, got) + VOXEL
                    if away:
                        got = got + VOXEL
                    tile = own[pl.ds(base + plane * size + column * rows + y, SUBLANES), :]
                    planes[side, plane, pl.ds(y, SUBLANES), x] = jnp.minimum(tile, got)
        to = out.at[pl.ds((0, depth - 2)[side], 2)]
        cp = pltpu.make_async_copy(planes.at[side], to, sem.at[side])
        cp.start()
        stores.append(cp)
    for edge, row in enumerate((0, 1, rows - 2, rows - 1)):
        z = 0
        for own in (slab_low, slab_high):
            for base in range(0, own.shape[0], SUBLANES * size):
                for column in columns:
                    tile = own[pl.ds(base + column * rows + row, SUBLANES, stride=size), :]
                    edges[edge, pl.ds(z, SUBLANES), pl.ds(column * LANES, LANES)] = tile
                z += SUBLANES
        for side in range(2):
            for plane in range(2):
                at = pl.ds((0, depth - 2)[side] + plane, 1)
                edges[edge, at, :] = planes[side, plane, pl.ds(row, 1), :]
    for cp in stores:
        cp.wait()


def patch_z(first, second, slab_low, slab_high, out):
    depth, rows, cols = out.shape
    return pl.pallas_call(
        functools.partial(patch_z_kernel, lax.axis_size("gz")),
        name="patch_z",
        out_shape=(
            jax.ShapeDtypeStruct(out.shape, out.dtype),
            jax.ShapeDtypeStruct((4, depth, cols), jnp.float32),
        ),
        in_specs=[VMEM] * 4 + [HBM],
        out_specs=(HBM, VMEM),
        input_output_aliases={4: 0},
        scratch_shapes=[
            pltpu.VMEM((2, 2, rows, cols), jnp.float32),
            pltpu.SemaphoreType.DMA((2,)),
        ],
        compiler_params=params(4),
        cost_estimate=cost(1),
    )(first, second, slab_low, slab_high, out)


def patch_y_kernel(scale, slabs, edges, low, high, clow, chigh, counts, _, out, share, buf, sem):
    depth, rows, _ = out.shape
    slab = lax.axis_index("gz")
    copies = []
    for side, (face, corner) in enumerate(((low, clow), (high, chigh))):
        for away in range(2):
            edge = (away, 3 - away)[side]
            row = (away, rows - 1 - away)[side]
            at = 2 * side + away
            reach = face[1 - away] + VOXEL
            if away:
                reach = reach + VOXEL
            buf[at] = jnp.minimum(edges[edge], reach)
            if not away:
                for end, z in enumerate((0, depth - 1)):
                    missing = slab == (0, slabs - 1)[end]
                    offer = jnp.where(missing, FAR, corner[pl.ds(end, 1), :])
                    line = jnp.minimum(buf[at, pl.ds(z, 1), :], offer + VOXEL + VOXEL)
                    buf[at, pl.ds(z, 1), :] = line
            cp = pltpu.make_async_copy(buf.at[at], out.at[:, row, :], sem.at[at])
            cp.start()
            copies.append(cp)
    x = pl.ds(0, LANES)
    both = (counts[:, x] + clow[:, x]).astype(jnp.int32)
    row = lax.broadcasted_iota(jnp.int32, both.shape, 0)
    both = jnp.where(row == 2, both, jnp.where(row == 3, both << COUNT_BITS, 0))
    count = jnp.sum(both, axis=0, keepdims=True)
    share[...] = count[:, :1].astype(jnp.float32) * jnp.float32(scale)
    for cp in copies:
        cp.wait()


def patch_y(scale, edges, low, high, clow, chigh, counts, out):
    depth, _, cols = out.shape
    return pl.pallas_call(
        functools.partial(patch_y_kernel, scale, lax.axis_size("gz")),
        name="patch_y",
        out_shape=(
            jax.ShapeDtypeStruct(out.shape, out.dtype),
            jax.ShapeDtypeStruct((1, 1), jnp.float32),
        ),
        in_specs=[VMEM] * 6 + [HBM],
        out_specs=(HBM, VMEM),
        input_output_aliases={6: 0},
        scratch_shapes=[pltpu.VMEM((4, depth, cols), jnp.float32), pltpu.SemaphoreType.DMA((4,))],
        compiler_params=params(8),
        cost_estimate=cost(2),
    )(edges, low, high, clow, chigh, counts, out)


def swapped(value, axis, partner):
    count = lax.axis_size(axis)
    return lax.ppermute(value, axis, [(i, partner(i) % count) for i in range(count)])


def shifted(value, axis, by):
    return swapped(value, axis, lambda i: i + by)


def on_device(distance, parent, removed, occupied):
    depth, rows, cols = distance.shape
    half = depth // 2
    slabs, columns = lax.axis_size("gz"), lax.axis_size("gy")
    tied = lax.optimization_barrier
    distance, parent, flags, occupied = (
        pltpu.with_memory_space_constraint(a, pltpu.HBM)
        for a in (distance, parent, removed.reshape(-1, LANES), occupied)
    )

    field, first, second = raise_all(distance, parent, flags, occupied)
    got_first = swapped(first, "gz", lambda i: i ^ 1)
    ylow, yhigh = faces(field, rows, cols)
    low = shifted(yhigh, "gy", 1)
    high = shifted(ylow, "gy", -1)
    once0 = sweep_once(field, 0, half, rows, cols)
    got_first, once0 = tied((got_first, once0))
    second = second.at[2 * rows :].add(got_first[2 * rows :])
    got_second = swapped(second, "gz", lambda i: i - 1 + 2 * (i % 2))
    once1 = sweep_once(field, half, half, rows, cols)
    got_second, once1 = tied((got_second, once1))
    counts = second[2 * rows :] + got_second[2 * rows :]
    more = jnp.zeros_like(counts)

    lowered, half0 = sweep_again(once0, None, 0, depth, rows, cols)
    lowered, half1 = sweep_again(once1, lowered, half, depth, rows, cols)
    step = columns // 2
    turn = 0
    while step > 1:
        if turn:
            counts = counts + more
        more = swapped(counts, "gy", lambda i: i ^ step)
        if turn == 0:
            more, half0 = tied((more, half0))
        elif turn == 1:
            more, half1 = tied((more, half1))
        step //= 2
        turn += 1
    clow, chigh, counts = corners(got_first, got_second, counts, more)
    from_low = shifted(chigh, "gy", 1)
    from_high = shifted(clow, "gy", -1)
    lowered, edges = patch_z(got_first, got_second, half0, half1, lowered)
    total = distance.size * slabs * columns
    lowered, share = patch_y(100.0 / total, edges, low, high, from_low, from_high, counts, lowered)
    return (lowered, share[0, 0])


def solution(mesh):
    slabs, columns = mesh.shape["gz"], mesh.shape["gy"]
    if slabs != 4 or columns < 8 or columns & (columns - 1):
        raise ValueError("unsupported mesh")
    placed = (P("gz", "gy", None), P("gz", "gy", None), P(), P("gz", "gy", None))
    return jax.shard_map(
        on_device, mesh=mesh, in_specs=placed, out_specs=(P("gz", "gy", None), P()), check_vma=False
    )
```

time: 55.9 us -> 43.1 us (0.77)
  Pallas kernels: 27.3 us -> 21.2 us
  waiting for transfers between devices: 11.1 us -> 6.01 us
  other arithmetic: 1.96 us -> 0.02 us
  starting transfers between devices: 13.7 us -> 14.8 us
  local copies, waits for them, and re-layouts: 0.82 us -> 0.01 us
    ppermute x8, waiting for transfers between devices: 11.1 us -> 6.01 us  [swapped(): lax.ppermute(value, axis, [(i, partner(i) % count) for i in range(count)])]
    pallas_call x3 -> x7, Pallas kernels: 16.3 us -> 11.8 us  [the longest x2 5.76 us: sweep_again(): pl.pallas_call(functools.partial(sweep_again_kernel, start), out_shape=(j...]
    scatter-add x2 -> x0, other arithmetic: 1.3 us -> none  [the longest x1 0.65 us: on_device(): chigh = chigh.at[:, :LANES].add(counts)]
    ppermute x8, starting transfers between devices: 13.7 us -> 14.8 us  [swapped(): lax.ppermute(value, axis, [(i, partner(i) % count) for i in range(count)])]
    pallas_call x1, Pallas kernels: 1.66 us -> 0.75 us  [patch_z(): pl.pallas_call(functools.partial(patch_z_kernel, lax.axis_size('gz')), na...]
    pallas_call x1, Pallas kernels: 9.37 us -> 8.67 us  [raise_all(): pl.pallas_call(raise_kernel, name='raise_all', out_shape=(jax.ShapeDtypeS...]
    unnamed x2 -> x1, local copies, waits for them, and re-layouts: 0.71 us -> 0.01 us
    another operation x1 -> x0, other arithmetic: 0.64 us -> none
  transfers between devices with their start and end apart: 8 -> 8, of which waited for: 4 -> 3; matrix products, arithmetic and copies ran while one was open for 4% -> 0% of each run, Pallas kernels for 29% -> 26%
where the time goes in v3:
time: 43.1 us; the launch traced here: 42.8 us
  Pallas kernels  21.2 us (49%)
  starting transfers between devices  14.8 us (34%)
  waiting for transfers between devices  6.01 us (14%)
  between operations  0.74 us (2%)
    ppermute x8, starting transfers between devices, swapped(): lax.ppermute(value, axis, [(i, partner(i) % count) for i in range(count)])  14.8 us
    pallas_call x1, Pallas kernels, raise_all(): pl.pallas_call(raise_kernel, name='raise_all', out_shape=(jax.ShapeDtypeS...  8.67 us
    ppermute x8, waiting for transfers between devices, swapped(): lax.ppermute(value, axis, [(i, partner(i) % count) for i in range(count)])  6.01 us
    pallas_call x2, Pallas kernels, sweep_again(): pl.pallas_call(functools.partial(sweep_again_kernel, start), out_shape=(j...  5.76 us
    pallas_call x2, Pallas kernels, sweep_once(): pl.pallas_call(functools.partial(sweep_once_kernel, start, count, rows, c...  3.58 us
    pallas_call x1, Pallas kernels, patch_y(): pl.pallas_call(functools.partial(patch_y_kernel, scale, lax.axis_size('gz...  1.56 us
    pallas_call x1, Pallas kernels, faces(): pl.pallas_call(functools.partial(faces_kernel, rows, cols), name='faces',...  0.89 us
  transfers between devices with their start and end apart: 8, of which 3 were waited for; matrix products, arithmetic and copies ran while one was open for 0% of the time, Pallas kernels for 26%

profile of v3, /device:TPU:0, one launch (start us, length us, event | category | flops | bytes accessed | tf_op | source)
XLA Modules:
  0.0 42.8 jit_solution(3228729056054701614)
XLA Ops:
  0.6 8.7 %raise_all.1 = (f32[66,200,128]{2,1,0:T(8,128)S(1)}, f32[40,1024]{1,0:T(8,128)S(1)}, f32[40,1024]{1,0:T(8,128)S(1)}) custom-call(f32[64,16,1024]{2,1,0:T(8,128)} %dist.1, s32[64,16,1024]{2,1,0:T(8,128)} %par.1, s32[32,128]{1,0:T(8,128)} %bitcast.2, s32[64,16,1024]{2,1,0:T(8,128)} %occ.1), custom_call_target="tpu_custom_call" | custom-call | bytes 12582912 | tf_op jit(solution)/shard_map/raise_all/pallas_call | solution.py:200
  9.3 0.6 %collective-permute-start = (f32[40,1024]{1,0:T(8,128)S(1)}, f32[40,1024]{1,0:T(8,128)S(1)}, u32[]{:S(2)}, u32[]{:S(2)}) collective-permute-start(f32[40,1024]{1,0:T(8,128)S(1)} %get-tuple-element.38), channel_id=1, source_target_pairs={{0,8},{8,0},{16,24},{24,16},{1,9},{9,1},{17,25},{25,17},{2,10},{10... | collective-permute-start | bytes 491528 | tf_op jit(solution)/shard_map/ppermute | solution.py:454
  9.9 0.9 %faces.1 = (f32[2,64,1024]{2,1,0:T(8,128)S(1)}, f32[2,64,1024]{2,1,0:T(8,128)S(1)}) custom-call(f32[66,200,128]{2,1,0:T(8,128)S(1)} %get-tuple-element.39.field), custom_call_target="tpu_custom_call" | custom-call | bytes 2097152 | tf_op jit(solution)/shard_map/faces/pallas_call | solution.py:123
  10.8 2.6 %collective-permute-start.4 = (f32[2,64,1024]{2,1,0:T(8,128)S(1)}, f32[2,64,1024]{2,1,0:T(8,128)S(1)}, u32[]{:S(2)}, u32[]{:S(2)}) collective-permute-start(f32[2,64,1024]{2,1,0:T(8,128)S(1)} %get-tuple-element.53), channel_id=1, source_target_pairs={{0,1},{1,2},{2,3},{3,4},{4,5},{5,6},{6,7},{7,0},{8,9},{9,10},{10,1... | collective-permute-start | bytes 1572872 | tf_op jit(solution)/shard_map/ppermute | solution.py:454
  13.3 3.1 %collective-permute-start.5 = (f32[2,64,1024]{2,1,0:T(8,128)S(1)}, f32[2,64,1024]{2,1,0:T(8,128)S(1)}, u32[]{:S(2)}, u32[]{:S(2)}) collective-permute-start(f32[2,64,1024]{2,1,0:T(8,128)S(1)} %get-tuple-element.54), channel_id=1, source_target_pairs={{0,7},{1,0},{2,1},{3,2},{4,3},{5,4},{6,5},{7,6},{8,15},{9,8},{10,9... | collective-permute-start | bytes 1572872 | tf_op jit(solution)/shard_map/ppermute | solution.py:454
  16.4 1.8 %shard_map.59.once = f32[34,200,128]{2,1,0:T(8,128)S(1)} custom-call(f32[66,200,128]{2,1,0:T(8,128)S(1)} %get-tuple-element.39.field), custom_call_target="tpu_custom_call" | custom-call | bytes 8388608 | tf_op jit(solution)/shard_map/pallas_call | solution.py:247
  18.3 0.0 collective-permute-done.first
  18.3 1.4 %collective-permute-start.1 = (f32[40,1024]{1,0:T(8,128)S(1)}, f32[40,1024]{1,0:T(8,128)S(1)}, u32[]{:S(2)}, u32[]{:S(2)}) collective-permute-start(f32[40,1024]{1,0:T(8,128)S(1)} %fusion), channel_id=1, source_target_pairs={{0,24},{8,16},{16,8},{24,0},{1,25},{9,17},{17,9},{25,1},{2,26},{10... | collective-permute-start | bytes 491528 | tf_op jit(solution)/shard_map/ppermute | solution.py:454
  19.7 1.8 %shard_map.60.once = f32[34,200,128]{2,1,0:T(8,128)S(1)} custom-call(f32[66,200,128]{2,1,0:T(8,128)S(1)} %get-tuple-element.39.field), custom_call_target="tpu_custom_call" | custom-call | bytes 8388608 | tf_op jit(solution)/shard_map/pallas_call | solution.py:247
  21.5 3.0 %collective-permute-done.1.second = f32[40,1024]{1,0:T(8,128)S(1)} collective-permute-done((f32[40,1024]{1,0:T(8,128)S(1)}, f32[40,1024]{1,0:T(8,128)S(1)}, u32[]{:S(2)}, u32[]{:S(2)}) %collective-permute-start.1) | collective-permute-done | bytes 163872 | tf_op jit(solution)/shard_map/ppermute | solution.py:454
  24.5 1.2 %collective-permute-start.2 = (f32[8,1024]{1,0:T(8,128)S(1)}, f32[8,1024]{1,0:T(8,128)S(1)}, u32[]{:S(2)}, u32[]{:S(2)}) collective-permute-start(f32[8,1024]{1,0:T(8,128)S(1)} %slice_add_fusion), channel_id=1, source_target_pairs={{0,4},{1,5},{2,6},{3,7},{4,0},{5,1},{6,2},{7,3},{8,12},{9,13},{10,... | collective-permute-start | bytes 98312 | tf_op jit(solution)/shard_map/ppermute | solution.py:454
  25.7 2.9 %shard_map.61 = (f32[64,16,1024]{2,1,0:T(8,128)}, f32[4096,128]{1,0:T(8,128)S(1)}) custom-call(f32[34,200,128]{2,1,0:T(8,128)S(1)} %shard_map.59.once), custom_call_target="tpu_custom_call" | custom-call | bytes 8388608 | tf_op jit(solution)/shard_map/pallas_call | solution.py:295
  28.6 1.9 %collective-permute-done.2 = f32[8,1024]{1,0:T(8,128)S(1)} collective-permute-done((f32[8,1024]{1,0:T(8,128)S(1)}, f32[8,1024]{1,0:T(8,128)S(1)}, u32[]{:S(2)}, u32[]{:S(2)}) %collective-permute-start.2) | collective-permute-done | bytes 32800 | tf_op jit(solution)/shard_map/ppermute | solution.py:454
  30.4 1.2 %collective-permute-start.3 = (f32[8,1024]{1,0:T(8,128)S(1)}, f32[8,1024]{1,0:T(8,128)S(1)}, u32[]{:S(2)}, u32[]{:S(2)}) collective-permute-start(f32[8,1024]{1,0:T(8,128)S(1)} %add.15.counts), channel_id=1, source_target_pairs={{0,2},{1,3},{2,0},{3,1},{4,6},{5,7},{6,4},{7,5},{8,10},{9,11},{10,... | collective-permute-start | bytes 98312 | tf_op jit(solution)/shard_map/ppermute | solution.py:454
  31.7 2.9 %shard_map.62 = (f32[64,16,1024]{2,1,0:T(8,128)}, f32[4096,128]{1,0:T(8,128)S(1)}) custom-call(f32[34,200,128]{2,1,0:T(8,128)S(1)} %shard_map.60.once, f32[64,16,1024]{2,1,0:T(8,128)} %get-tuple-element.48.refs_0_), custom_call_target="tpu_custom_call", output_to_operand_aliasing={{0}: (1, {})} | custom-call | bytes 8388608 | tf_op jit(solution)/shard_map/pallas_call | solution.py:295
  34.6 0.0 collective-permute-done.3.more
  34.6 0.3 collective-permute-start.6
  34.9 4.5 %collective-permute-start.7 = (f32[8,1024]{1,0:T(8,128)S(1)}, f32[8,1024]{1,0:T(8,128)S(1)}, u32[]{:S(2)}, u32[]{:S(2)}) collective-permute-start(f32[8,1024]{1,0:T(8,128)S(1)} %get-tuple-element.57), channel_id=1, source_target_pairs={{0,7},{1,0},{2,1},{3,2},{4,3},{5,4},{6,5},{7,6},{8,15},{9,8},{10,9... | collective-permute-start | bytes 98312 | tf_op jit(solution)/shard_map/ppermute | solution.py:454
  39.4 0.7 %patch_z.1 = (f32[64,16,1024]{2,1,0:T(8,128)}, f32[4,64,1024]{2,1,0:T(8,128)S(1)}) custom-call(f32[40,1024]{1,0:T(8,128)S(1)} %collective-permute-done.first, f32[40,1024]{1,0:T(8,128)S(1)} %collective-permute-done.1.second, f32[4096,128]{1,0:T(8,128)S(1)} %get-tuple-element.45.slab_low, ...), custom_call_target="tpu_custom_call", output_to_operand_aliasing={{0}: (4, {})} | custom-call | bytes 1048576 | tf_op jit(solution)/shard_map/patch_z/pallas_call | solution.py:383
  40.1 1.1 %collective-permute-done.6.clow = f32[8,1024]{1,0:T(8,128)S(1)} collective-permute-done((f32[8,1024]{1,0:T(8,128)S(1)}, f32[8,1024]{1,0:T(8,128)S(1)}, u32[]{:S(2)}, u32[]{:S(2)}) %collective-permute-start.6) | collective-permute-done | bytes 32800 | tf_op jit(solution)/shard_map/ppermute | solution.py:454
  41.3 0.0 collective-permute-done.7.chigh
  41.3 0.0 collective-permute-done.4.low
  41.3 0.0 collective-permute-done.5.high
  41.3 1.6 %patch_y.1 = (f32[64,16,1024]{2,1,0:T(8,128)}, f32[1,1]{1,0:T(1,128)}) custom-call(f32[4,64,1024]{2,1,0:T(8,128)S(1)} %get-tuple-element.52.edges, f32[2,64,1024]{2,1,0:T(8,128)S(1)} %collective-permute-done.4.low, f32[2,64,1024]{2,1,0:T(8,128)S(1)} %collective-permute-done.5.high, ...), custom_call_target="tpu_custom_call", output_to_operand_aliasing={{0}: (6, {})} | custom-call | bytes 2097152 | tf_op jit(solution)/shard_map/patch_y/pallas_call | solution.py:436
  (5 shorter events, 0.1 us)
Async XLA Ops:
  9.3 9.0 %collective-permute-start = (f32[40,1024]{1,0:T(8,128)S(1)}, f32[40,1024]{1,0:T(8,128)S(1)}, u32[]{:S(2)}, u32[]{:S(2)}) collective-permute-start(f32[40,1024]{1,0:T(8,128)S(1)} %get-tuple-element.38), channel_id=1, source_target_pairs={{0,8},{8,0},{16,24},{24,16},{1,9},{9,1},{17,25},{25,17},{2,10},{10... | collective-permute-start | bytes 491528 | tf_op jit(solution)/shard_map/ppermute | solution.py:454
  10.8 30.5 %collective-permute-start.4 = (f32[2,64,1024]{2,1,0:T(8,128)S(1)}, f32[2,64,1024]{2,1,0:T(8,128)S(1)}, u32[]{:S(2)}, u32[]{:S(2)}) collective-permute-start(f32[2,64,1024]{2,1,0:T(8,128)S(1)} %get-tuple-element.53), channel_id=1, source_target_pairs={{0,1},{1,2},{2,3},{3,4},{4,5},{5,6},{6,7},{7,0},{8,9},{9,10},{10,1... | collective-permute-start | bytes 1572872 | tf_op jit(solution)/shard_map/ppermute | solution.py:454
  13.3 27.9 %collective-permute-start.5 = (f32[2,64,1024]{2,1,0:T(8,128)S(1)}, f32[2,64,1024]{2,1,0:T(8,128)S(1)}, u32[]{:S(2)}, u32[]{:S(2)}) collective-permute-start(f32[2,64,1024]{2,1,0:T(8,128)S(1)} %get-tuple-element.54), channel_id=1, source_target_pairs={{0,7},{1,0},{2,1},{3,2},{4,3},{5,4},{6,5},{7,6},{8,15},{9,8},{10,9... | collective-permute-start | bytes 1572872 | tf_op jit(solution)/shard_map/ppermute | solution.py:454
  18.3 6.2 %collective-permute-start.1 = (f32[40,1024]{1,0:T(8,128)S(1)}, f32[40,1024]{1,0:T(8,128)S(1)}, u32[]{:S(2)}, u32[]{:S(2)}) collective-permute-start(f32[40,1024]{1,0:T(8,128)S(1)} %fusion), channel_id=1, source_target_pairs={{0,24},{8,16},{16,8},{24,0},{1,25},{9,17},{17,9},{25,1},{2,26},{10... | collective-permute-start | bytes 491528 | tf_op jit(solution)/shard_map/ppermute | solution.py:454
  24.5 6.0 %collective-permute-start.2 = (f32[8,1024]{1,0:T(8,128)S(1)}, f32[8,1024]{1,0:T(8,128)S(1)}, u32[]{:S(2)}, u32[]{:S(2)}) collective-permute-start(f32[8,1024]{1,0:T(8,128)S(1)} %slice_add_fusion), channel_id=1, source_target_pairs={{0,4},{1,5},{2,6},{3,7},{4,0},{5,1},{6,2},{7,3},{8,12},{9,13},{10,... | collective-permute-start | bytes 98312 | tf_op jit(solution)/shard_map/ppermute | solution.py:454
  30.4 4.1 %collective-permute-start.3 = (f32[8,1024]{1,0:T(8,128)S(1)}, f32[8,1024]{1,0:T(8,128)S(1)}, u32[]{:S(2)}, u32[]{:S(2)}) collective-permute-start(f32[8,1024]{1,0:T(8,128)S(1)} %add.15.counts), channel_id=1, source_target_pairs={{0,2},{1,3},{2,0},{3,1},{4,6},{5,7},{6,4},{7,5},{8,10},{9,11},{10,... | collective-permute-start | bytes 98312 | tf_op jit(solution)/shard_map/ppermute | solution.py:454
  34.6 6.7 %collective-permute-start.6 = (f32[8,1024]{1,0:T(8,128)S(1)}, f32[8,1024]{1,0:T(8,128)S(1)}, u32[]{:S(2)}, u32[]{:S(2)}) collective-permute-start(f32[8,1024]{1,0:T(8,128)S(1)} %get-tuple-element.56), channel_id=1, source_target_pairs={{0,1},{1,2},{2,3},{3,4},{4,5},{5,6},{6,7},{7,0},{8,9},{9,10},{10,1... | collective-permute-start | bytes 98312 | tf_op jit(solution)/shard_map/ppermute | solution.py:454
  34.9 6.4 %collective-permute-start.7 = (f32[8,1024]{1,0:T(8,128)S(1)}, f32[8,1024]{1,0:T(8,128)S(1)}, u32[]{:S(2)}, u32[]{:S(2)}) collective-permute-start(f32[8,1024]{1,0:T(8,128)S(1)} %get-tuple-element.57), channel_id=1, source_target_pairs={{0,7},{1,0},{2,1},{3,2},{4,3},{5,4},{6,5},{7,6},{8,15},{9,8},{10,9... | collective-permute-start | bytes 98312 | tf_op jit(solution)/shard_map/ppermute | solution.py:454

commit v4 on v3

--- a/solution.py
+++ b/solution.py
@@ -16,6 +16,7 @@
 CHUNK = 8
 RAISE_UNROLL = 4
 SWEEP_UNROLL = 4
+STORES = 4
 MIB = 2**20
 
 HBM = pl.BlockSpec(memory_space=pltpu.HBM)
@@ -131,38 +132,50 @@
     )(field)
 
 
-def raise_kernel(dist, par, flags, occ, field, first, second, words, total, ends):
-    step = pl.program_id(0)
-    last = pl.num_programs(0) - 1
-    chunk, rows, cols = dist.shape
-    depth = field.shape[0] - 2
+def raise_kernel(dist, par, flags_at, occ, field, first, second, flags, buf, ends, fsem, sem):
+    depth, rows, cols = dist.shape
     columns = range(cols // LANES)
-
-    @pl.when(step == 0)
-    def _():
-        words[...] = packed_table(flags)
-        total[...] = jnp.zeros_like(total)
-        for z in (0, depth + 1):
-            field[z] = jnp.full(field.shape[1:], FAR)
-
-    table = words[...]
-
-    def body(group, acc):
-        for part in range(RAISE_UNROLL):
-            z = group * RAISE_UNROLL + part
-            fill_pads(field, (step * chunk + z + 1,), rows, cols)
-            for y in range(0, rows, SUBLANES):
-                for column in columns:
-                    at = (z, pl.ds(y, SUBLANES), pl.ds(column * LANES, LANES))
-                    tile, cleared = raise_tile(table, dist[at], par[at], occ[at])
-                    to = pl.ds(row_of(column, y, rows), SUBLANES)
-                    field[step * chunk + z + 1, to, :] = tile
-                    acc[part] = acc[part] + cleared
-        return acc
+    chunks = depth // CHUNK
+
+    def reads(chunk):
+        at = pl.ds(chunk * CHUNK, CHUNK)
+        return [
+            pltpu.make_async_copy(src.at[at], dst.at[at], sem.at[which, chunk])
+            for which, (src, dst) in enumerate(zip((dist, par, occ), buf))
+        ]
+
+    table_in = pltpu.make_async_copy(flags_at, flags, fsem)
+    table_in.start()
+    for chunk in range(chunks):
+        for cp in reads(chunk):
+            cp.start()
+    for z in (0, depth + 1):
+        field[z] = jnp.full(field.shape[1:], FAR)
+    table_in.wait()
+    table = packed_table(flags)
+
+    def body(chunk, acc):
+        for cp in reads(chunk):
+            cp.wait()
+
+        def planes(group, acc):
+            for part in range(RAISE_UNROLL):
+                z = chunk * CHUNK + group * RAISE_UNROLL + part
+                fill_pads(field, (z + 1,), rows, cols)
+                for y in range(0, rows, SUBLANES):
+                    for column in columns:
+                        at = (z, pl.ds(y, SUBLANES), pl.ds(column * LANES, LANES))
+                        tile, cleared = raise_tile(table, *(b[at] for b in buf))
+                        to = pl.ds(row_of(column, y, rows), SUBLANES)
+                        field[z + 1, to, :] = tile
+                        acc[part] = acc[part] + cleared
+            return acc
+
+        return lax.fori_loop(0, CHUNK // RAISE_UNROLL, planes, acc)
 
     zeros = jnp.zeros((SUBLANES, LANES), jnp.int32)
-    parts = lax.fori_loop(0, chunk // RAISE_UNROLL, body, [zeros] * RAISE_UNROLL)
-    total[...] += sum(parts[1:], parts[0])
+    parts = lax.fori_loop(0, chunks, body, [zeros] * RAISE_UNROLL)
+    total = sum(parts[1:], parts[0])
 
     def keep_end(side, z):
         def read(dz, at):
@@ -175,27 +188,21 @@
                 ends[side, pl.ds(y, SUBLANES), x] = read(0, row_of(column, y, rows))
                 ends[side, pl.ds(rows + y, SUBLANES), x] = swept[column]
 
-    @pl.when(step == 0)
-    def _():
-        keep_end(0, 0)
-
-    @pl.when(step == last)
-    def _():
-        keep_end(1, depth - 1)
-        count = jnp.sum(total[...])
-        row = lax.broadcasted_iota(jnp.int32, (SUBLANES, cols), 0)
-        low = (count & (2**COUNT_BITS - 1)).astype(jnp.float32)
-        high = (count >> COUNT_BITS).astype(jnp.float32)
-        counts = jnp.where(row == 2, low, jnp.where(row == 3, high, 0.0))
-        odd = lax.axis_index("gz") & 1
-        for out, side in ((first, 1 - odd), (second, odd)):
-            out[pl.ds(0, 2 * rows), :] = ends[side]
-            out[pl.ds(2 * rows, SUBLANES), :] = counts
+    keep_end(0, 0)
+    keep_end(1, depth - 1)
+    count = jnp.sum(total)
+    row = lax.broadcasted_iota(jnp.int32, (SUBLANES, cols), 0)
+    low = (count & (2**COUNT_BITS - 1)).astype(jnp.float32)
+    high = (count >> COUNT_BITS).astype(jnp.float32)
+    counts = jnp.where(row == 2, low, jnp.where(row == 3, high, 0.0))
+    odd = lax.axis_index("gz") & 1
+    for out, side in ((first, odd), (second, 1 - odd)):
+        out[pl.ds(0, 2 * rows), :] = ends[side]
+        out[pl.ds(2 * rows, SUBLANES), :] = counts
 
 
 def raise_all(dist, par, flags, occ):
     depth, rows, cols = dist.shape
-    block = pl.BlockSpec((CHUNK, rows, cols), lambda i: (i, 0, 0))
     message = jax.ShapeDtypeStruct((2 * rows + SUBLANES, cols), jnp.float32)
     return pl.pallas_call(
         raise_kernel,
@@ -205,15 +212,16 @@
             message,
             message,
         ),
-        grid=(depth // CHUNK,),
-        in_specs=[block, block, pl.BlockSpec(flags.shape, lambda i: (0, 0)), block],
-        out_specs=(VMEM, VMEM, VMEM),
+        in_specs=[HBM] * 4,
+        out_specs=(VMEM,) * 3,
         scratch_shapes=[
-            pltpu.VMEM((SUBLANES, LANES), jnp.int32),
-            pltpu.VMEM((SUBLANES, LANES), jnp.int32),
+            pltpu.VMEM(flags.shape, jnp.int32),
+            [pltpu.VMEM(a.shape, a.dtype) for a in (dist, par, occ)],
             pltpu.VMEM((2, 2 * rows, cols), jnp.float32),
+            pltpu.SemaphoreType.DMA,
+            pltpu.SemaphoreType.DMA((3, depth // CHUNK)),
         ],
-        compiler_params=params(24),
+        compiler_params=params(20),
         cost_estimate=cost(12),
     )(dist, par, flags, occ)
 
@@ -256,14 +264,15 @@
 
 def sweep_again_kernel(start, once, *refs):
     out, slab, stage, sem = refs[-4:]
-    _, chunk, rows, cols = stage.shape
+    chunk, rows, cols = stage.shape[1:]
     columns = range(cols // LANES)
     count = once.shape[0] - 2
+    slots = stage.shape[0]
     copies = []
     for step in range(count // chunk):
-        slot = step % 2
-        if step >= 2:
-            copies[step - 2].wait()
+        slot = step % slots
+        if step >= slots:
+            copies[step - slots].wait()
 
         def body(group, _, step=step, slot=slot):
             for part in range(SWEEP_UNROLL):
@@ -285,7 +294,7 @@
         cp = pltpu.make_async_copy(stage.at[slot], to, sem.at[slot])
         cp.start()
         copies.append(cp)
-    for cp in copies[-2:]:
+    for cp in copies[-slots:]:
         cp.wait()
 
 
@@ -302,8 +311,8 @@
         out_specs=(HBM, VMEM),
         input_output_aliases={1: 0} if given else {},
         scratch_shapes=[
-            pltpu.VMEM((2, CHUNK, rows, cols), jnp.float32),
-            pltpu.SemaphoreType.DMA((2,)),
+            pltpu.VMEM((STORES, CHUNK, rows, cols), jnp.float32),
+            pltpu.SemaphoreType.DMA((STORES,)),
         ],
         compiler_params=params(8),
         cost_estimate=cost(8),
@@ -318,7 +327,7 @@
     high[...] = total[...]
     for side in range(2):
         for out, row in ((low, 0), (high, rows - 1)):
-            line = jnp.where(odd != side, first[pl.ds(row, 1), :], second[pl.ds(row, 1), :])
+            line = jnp.where(odd == side, first[pl.ds(row, 1), :], second[pl.ds(row, 1), :])
             out[pl.ds(side, 1), :] = line
 
 
@@ -352,7 +361,7 @@
                 for column in columns:
                     x = pl.ds(column * LANES, LANES)
                     at = (pl.ds(offered + y, SUBLANES), x)
-                    got = jnp.where(odd != side, first[at], second[at])
+                    got = jnp.where(odd == side, first[at], second[at])
                     got = jnp.where(missing, FAR, got) + VOXEL
                     if away:
                         got = got + VOXEL
@@ -469,14 +478,14 @@
     )
 
     field, first, second = raise_all(distance, parent, flags, occupied)
-    got_first = swapped(first, "gz", lambda i: i ^ 1)
+    got_first = swapped(first, "gz", lambda i: i - 1 + 2 * (i % 2))
     ylow, yhigh = faces(field, rows, cols)
     low = shifted(yhigh, "gy", 1)
     high = shifted(ylow, "gy", -1)
     once0 = sweep_once(field, 0, half, rows, cols)
     got_first, once0 = tied((got_first, once0))
     second = second.at[2 * rows :].add(got_first[2 * rows :])
-    got_second = swapped(second, "gz", lambda i: i - 1 + 2 * (i % 2))
+    got_second = swapped(second, "gz", lambda i: i ^ 1)
     once1 = sweep_once(field, half, half, rows, cols)
     got_second, once1 = tied((got_second, once1))
     counts = second[2 * rows :] + got_second[2 * rows :]

time: 43.1 us -> 43.8 us (1.016)
  waiting for transfers between devices: 6.01 us -> 7.95 us
  Pallas kernels: 21.2 us -> 20.5 us
    ppermute x8, waiting for transfers between devices: 6.01 us -> 7.95 us  [swapped(): lax.ppermute(value, axis, [(i, partner(i) % count) for i in range(count)])]
    pallas_call x2, Pallas kernels: 5.76 us -> 5.07 us  [sweep_again(): pl.pallas_call(functools.partial(sweep_again_kernel, start), out_shape=(j...]
    ppermute x8, starting transfers between devices: 14.8 us -> 14.4 us  [swapped(): lax.ppermute(value, axis, [(i, partner(i) % count) for i in range(count)])]
  transfers between devices with their start and end apart: 8 -> 8, of which waited for: 3 -> 3; matrix products, arithmetic and copies ran while one was open for 0% -> 0% of each run, Pallas kernels for 26% -> 24%
where the time goes in v4:
time: 43.8 us; the launch traced here: 43.6 us
  Pallas kernels  20.5 us (47%)
  starting transfers between devices  14.4 us (33%)
  waiting for transfers between devices  7.95 us (18%)
  between operations  0.74 us (2%)
    ppermute x8, starting transfers between devices, swapped(): lax.ppermute(value, axis, [(i, partner(i) % count) for i in range(count)])  14.4 us
    pallas_call x1, Pallas kernels, raise_all(): pl.pallas_call(raise_kernel, name='raise_all', out_shape=(jax.ShapeDtypeS...  8.65 us
    ppermute x8, waiting for transfers between devices, swapped(): lax.ppermute(value, axis, [(i, partner(i) % count) for i in range(count)])  7.95 us
    pallas_call x2, Pallas kernels, sweep_again(): pl.pallas_call(functools.partial(sweep_again_kernel, start), out_shape=(j...  5.07 us
    pallas_call x2, Pallas kernels, sweep_once(): pl.pallas_call(functools.partial(sweep_once_kernel, start, count, rows, c...  3.58 us
    pallas_call x1, Pallas kernels, patch_y(): pl.pallas_call(functools.partial(patch_y_kernel, scale, lax.axis_size('gz...  1.56 us
    pallas_call x1, Pallas kernels, faces(): pl.pallas_call(functools.partial(faces_kernel, rows, cols), name='faces',...  0.89 us
  transfers between devices with their start and end apart: 8, of which 3 were waited for; matrix products, arithmetic and copies ran while one was open for 0% of the time, Pallas kernels for 24%

profile of v4, /device:TPU:0, one launch (start us, length us, event | category | flops | bytes accessed | tf_op | source)
XLA Modules:
  0.0 43.6 jit_solution(7449399769849430368)
XLA Ops:
  0.6 8.6 %raise_all.1 = (f32[66,200,128]{2,1,0:T(8,128)S(1)}, f32[40,1024]{1,0:T(8,128)S(1)}, f32[40,1024]{1,0:T(8,128)S(1)}) custom-call(f32[64,16,1024]{2,1,0:T(8,128)} %dist.1, s32[64,16,1024]{2,1,0:T(8,128)} %par.1, s32[32,128]{1,0:T(8,128)} %bitcast.2, s32[64,16,1024]{2,1,0:T(8,128)} %occ.1), custom_call_target="tpu_custom_call" | custom-call | bytes 12582912 | tf_op jit(solution)/shard_map/raise_all/pallas_call | solution.py:207
  9.3 2.5 %collective-permute-start = (f32[40,1024]{1,0:T(8,128)S(1)}, f32[40,1024]{1,0:T(8,128)S(1)}, u32[]{:S(2)}, u32[]{:S(2)}) collective-permute-start(f32[40,1024]{1,0:T(8,128)S(1)} %get-tuple-element.38), channel_id=1, source_target_pairs={{0,24},{8,16},{16,8},{24,0},{1,25},{9,17},{17,9},{25,1},{2,26},{10... | collective-permute-start | bytes 491528 | tf_op jit(solution)/shard_map/ppermute | solution.py:463
  11.8 0.9 %faces.1 = (f32[2,64,1024]{2,1,0:T(8,128)S(1)}, f32[2,64,1024]{2,1,0:T(8,128)S(1)}) custom-call(f32[66,200,128]{2,1,0:T(8,128)S(1)} %get-tuple-element.39.field), custom_call_target="tpu_custom_call" | custom-call | bytes 2097152 | tf_op jit(solution)/shard_map/faces/pallas_call | solution.py:124
  12.7 1.6 %collective-permute-start.4 = (f32[2,64,1024]{2,1,0:T(8,128)S(1)}, f32[2,64,1024]{2,1,0:T(8,128)S(1)}, u32[]{:S(2)}, u32[]{:S(2)}) collective-permute-start(f32[2,64,1024]{2,1,0:T(8,128)S(1)} %get-tuple-element.53), channel_id=1, source_target_pairs={{0,1},{1,2},{2,3},{3,4},{4,5},{5,6},{6,7},{7,0},{8,9},{9,10},{10,1... | collective-permute-start | bytes 1572872 | tf_op jit(solution)/shard_map/ppermute | solution.py:463
  14.2 3.2 %collective-permute-start.5 = (f32[2,64,1024]{2,1,0:T(8,128)S(1)}, f32[2,64,1024]{2,1,0:T(8,128)S(1)}, u32[]{:S(2)}, u32[]{:S(2)}) collective-permute-start(f32[2,64,1024]{2,1,0:T(8,128)S(1)} %get-tuple-element.54), channel_id=1, source_target_pairs={{0,7},{1,0},{2,1},{3,2},{4,3},{5,4},{6,5},{7,6},{8,15},{9,8},{10,9... | collective-permute-start | bytes 1572872 | tf_op jit(solution)/shard_map/ppermute | solution.py:463
  17.4 1.8 %shard_map.59.once = f32[34,200,128]{2,1,0:T(8,128)S(1)} custom-call(f32[66,200,128]{2,1,0:T(8,128)S(1)} %get-tuple-element.39.field), custom_call_target="tpu_custom_call" | custom-call | bytes 8388608 | tf_op jit(solution)/shard_map/pallas_call | solution.py:255
  19.3 0.0 collective-permute-done.first
  19.3 0.4 collective-permute-start.1
  19.6 1.8 %shard_map.60.once = f32[34,200,128]{2,1,0:T(8,128)S(1)} custom-call(f32[66,200,128]{2,1,0:T(8,128)S(1)} %get-tuple-element.39.field), custom_call_target="tpu_custom_call" | custom-call | bytes 8388608 | tf_op jit(solution)/shard_map/pallas_call | solution.py:255
  21.4 0.0 collective-permute-done.1.second
  21.5 0.7 %collective-permute-start.2 = (f32[8,1024]{1,0:T(8,128)S(1)}, f32[8,1024]{1,0:T(8,128)S(1)}, u32[]{:S(2)}, u32[]{:S(2)}) collective-permute-start(f32[8,1024]{1,0:T(8,128)S(1)} %slice_add_fusion), channel_id=1, source_target_pairs={{0,4},{1,5},{2,6},{3,7},{4,0},{5,1},{6,2},{7,3},{8,12},{9,13},{10,... | collective-permute-start | bytes 98312 | tf_op jit(solution)/shard_map/ppermute | solution.py:463
  22.1 2.5 %shard_map.61 = (f32[64,16,1024]{2,1,0:T(8,128)}, f32[4096,128]{1,0:T(8,128)S(1)}) custom-call(f32[34,200,128]{2,1,0:T(8,128)S(1)} %shard_map.59.once), custom_call_target="tpu_custom_call" | custom-call | bytes 8388608 | tf_op jit(solution)/shard_map/pallas_call | solution.py:304
  24.7 6.8 %collective-permute-done.2 = f32[8,1024]{1,0:T(8,128)S(1)} collective-permute-done((f32[8,1024]{1,0:T(8,128)S(1)}, f32[8,1024]{1,0:T(8,128)S(1)}, u32[]{:S(2)}, u32[]{:S(2)}) %collective-permute-start.2) | collective-permute-done | bytes 32800 | tf_op jit(solution)/shard_map/ppermute | solution.py:463
  31.4 1.3 %collective-permute-start.3 = (f32[8,1024]{1,0:T(8,128)S(1)}, f32[8,1024]{1,0:T(8,128)S(1)}, u32[]{:S(2)}, u32[]{:S(2)}) collective-permute-start(f32[8,1024]{1,0:T(8,128)S(1)} %add.15.counts), channel_id=1, source_target_pairs={{0,2},{1,3},{2,0},{3,1},{4,6},{5,7},{6,4},{7,5},{8,10},{9,11},{10,... | collective-permute-start | bytes 98312 | tf_op jit(solution)/shard_map/ppermute | solution.py:463
  32.7 2.5 %shard_map.62 = (f32[64,16,1024]{2,1,0:T(8,128)}, f32[4096,128]{1,0:T(8,128)S(1)}) custom-call(f32[34,200,128]{2,1,0:T(8,128)S(1)} %shard_map.60.once, f32[64,16,1024]{2,1,0:T(8,128)} %get-tuple-element.48.refs_0_), custom_call_target="tpu_custom_call", output_to_operand_aliasing={{0}: (1, {})} | custom-call | bytes 8388608 | tf_op jit(solution)/shard_map/pallas_call | solution.py:304
  35.3 0.1 collective-permute-done.3.more
  35.4 0.6 %collective-permute-start.6 = (f32[8,1024]{1,0:T(8,128)S(1)}, f32[8,1024]{1,0:T(8,128)S(1)}, u32[]{:S(2)}, u32[]{:S(2)}) collective-permute-start(f32[8,1024]{1,0:T(8,128)S(1)} %get-tuple-element.56), channel_id=1, source_target_pairs={{0,1},{1,2},{2,3},{3,4},{4,5},{5,6},{6,7},{7,0},{8,9},{9,10},{10,1... | collective-permute-start | bytes 98312 | tf_op jit(solution)/shard_map/ppermute | solution.py:463
  36.0 4.2 %collective-permute-start.7 = (f32[8,1024]{1,0:T(8,128)S(1)}, f32[8,1024]{1,0:T(8,128)S(1)}, u32[]{:S(2)}, u32[]{:S(2)}) collective-permute-start(f32[8,1024]{1,0:T(8,128)S(1)} %get-tuple-element.57), channel_id=1, source_target_pairs={{0,7},{1,0},{2,1},{3,2},{4,3},{5,4},{6,5},{7,6},{8,15},{9,8},{10,9... | collective-permute-start | bytes 98312 | tf_op jit(solution)/shard_map/ppermute | solution.py:463
  40.1 0.8 %patch_z.1 = (f32[64,16,1024]{2,1,0:T(8,128)}, f32[4,64,1024]{2,1,0:T(8,128)S(1)}) custom-call(f32[40,1024]{1,0:T(8,128)S(1)} %collective-permute-done.first, f32[40,1024]{1,0:T(8,128)S(1)} %collective-permute-done.1.second, f32[4096,128]{1,0:T(8,128)S(1)} %get-tuple-element.45.slab_low, ...), custom_call_target="tpu_custom_call", output_to_operand_aliasing={{0}: (4, {})} | custom-call | bytes 1048576 | tf_op jit(solution)/shard_map/patch_z/pallas_call | solution.py:392
  40.9 1.1 %collective-permute-done.6.clow = f32[8,1024]{1,0:T(8,128)S(1)} collective-permute-done((f32[8,1024]{1,0:T(8,128)S(1)}, f32[8,1024]{1,0:T(8,128)S(1)}, u32[]{:S(2)}, u32[]{:S(2)}) %collective-permute-start.6) | collective-permute-done | bytes 32800 | tf_op jit(solution)/shard_map/ppermute | solution.py:463
  42.0 0.0 collective-permute-done.7.chigh
  42.0 0.0 collective-permute-done.4.low
  42.0 0.0 collective-permute-done.5.high
  42.0 1.6 %patch_y.1 = (f32[64,16,1024]{2,1,0:T(8,128)}, f32[1,1]{1,0:T(1,128)}) custom-call(f32[4,64,1024]{2,1,0:T(8,128)S(1)} %get-tuple-element.52.edges, f32[2,64,1024]{2,1,0:T(8,128)S(1)} %collective-permute-done.4.low, f32[2,64,1024]{2,1,0:T(8,128)S(1)} %collective-permute-done.5.high, ...), custom_call_target="tpu_custom_call", output_to_operand_aliasing={{0}: (6, {})} | custom-call | bytes 2097152 | tf_op jit(solution)/shard_map/patch_y/pallas_call | solution.py:445
  (5 shorter events, 0.0 us)
Async XLA Ops:
  9.3 10.0 %collective-permute-start = (f32[40,1024]{1,0:T(8,128)S(1)}, f32[40,1024]{1,0:T(8,128)S(1)}, u32[]{:S(2)}, u32[]{:S(2)}) collective-permute-start(f32[40,1024]{1,0:T(8,128)S(1)} %get-tuple-element.38), channel_id=1, source_target_pairs={{0,24},{8,16},{16,8},{24,0},{1,25},{9,17},{17,9},{25,1},{2,26},{10... | collective-permute-start | bytes 491528 | tf_op jit(solution)/shard_map/ppermute | solution.py:463
  12.7 29.4 %collective-permute-start.4 = (f32[2,64,1024]{2,1,0:T(8,128)S(1)}, f32[2,64,1024]{2,1,0:T(8,128)S(1)}, u32[]{:S(2)}, u32[]{:S(2)}) collective-permute-start(f32[2,64,1024]{2,1,0:T(8,128)S(1)} %get-tuple-element.53), channel_id=1, source_target_pairs={{0,1},{1,2},{2,3},{3,4},{4,5},{5,6},{6,7},{7,0},{8,9},{9,10},{10,1... | collective-permute-start | bytes 1572872 | tf_op jit(solution)/shard_map/ppermute | solution.py:463
  14.2 27.8 %collective-permute-start.5 = (f32[2,64,1024]{2,1,0:T(8,128)S(1)}, f32[2,64,1024]{2,1,0:T(8,128)S(1)}, u32[]{:S(2)}, u32[]{:S(2)}) collective-permute-start(f32[2,64,1024]{2,1,0:T(8,128)S(1)} %get-tuple-element.54), channel_id=1, source_target_pairs={{0,7},{1,0},{2,1},{3,2},{4,3},{5,4},{6,5},{7,6},{8,15},{9,8},{10,9... | collective-permute-start | bytes 1572872 | tf_op jit(solution)/shard_map/ppermute | solution.py:463
  19.3 2.2 %collective-permute-start.1 = (f32[40,1024]{1,0:T(8,128)S(1)}, f32[40,1024]{1,0:T(8,128)S(1)}, u32[]{:S(2)}, u32[]{:S(2)}) collective-permute-start(f32[40,1024]{1,0:T(8,128)S(1)} %fusion), channel_id=1, source_target_pairs={{0,8},{8,0},{16,24},{24,16},{1,9},{9,1},{17,25},{25,17},{2,10},{10... | collective-permute-start | bytes 491528 | tf_op jit(solution)/shard_map/ppermute | solution.py:463
  21.5 10.0 %collective-permute-start.2 = (f32[8,1024]{1,0:T(8,128)S(1)}, f32[8,1024]{1,0:T(8,128)S(1)}, u32[]{:S(2)}, u32[]{:S(2)}) collective-permute-start(f32[8,1024]{1,0:T(8,128)S(1)} %slice_add_fusion), channel_id=1, source_target_pairs={{0,4},{1,5},{2,6},{3,7},{4,0},{5,1},{6,2},{7,3},{8,12},{9,13},{10,... | collective-permute-start | bytes 98312 | tf_op jit(solution)/shard_map/ppermute | solution.py:463
  31.4 3.9 %collective-permute-start.3 = (f32[8,1024]{1,0:T(8,128)S(1)}, f32[8,1024]{1,0:T(8,128)S(1)}, u32[]{:S(2)}, u32[]{:S(2)}) collective-permute-start(f32[8,1024]{1,0:T(8,128)S(1)} %add.15.counts), channel_id=1, source_target_pairs={{0,2},{1,3},{2,0},{3,1},{4,6},{5,7},{6,4},{7,5},{8,10},{9,11},{10,... | collective-permute-start | bytes 98312 | tf_op jit(solution)/shard_map/ppermute | solution.py:463
  35.4 6.7 %collective-permute-start.6 = (f32[8,1024]{1,0:T(8,128)S(1)}, f32[8,1024]{1,0:T(8,128)S(1)}, u32[]{:S(2)}, u32[]{:S(2)}) collective-permute-start(f32[8,1024]{1,0:T(8,128)S(1)} %get-tuple-element.56), channel_id=1, source_target_pairs={{0,1},{1,2},{2,3},{3,4},{4,5},{5,6},{6,7},{7,0},{8,9},{9,10},{10,1... | collective-permute-start | bytes 98312 | tf_op jit(solution)/shard_map/ppermute | solution.py:463
  36.0 6.0 %collective-permute-start.7 = (f32[8,1024]{1,0:T(8,128)S(1)}, f32[8,1024]{1,0:T(8,128)S(1)}, u32[]{:S(2)}, u32[]{:S(2)}) collective-permute-start(f32[8,1024]{1,0:T(8,128)S(1)} %get-tuple-element.57), channel_id=1, source_target_pairs={{0,7},{1,0},{2,1},{3,2},{4,3},{5,4},{6,5},{7,6},{8,15},{9,8},{10,9... | collective-permute-start | bytes 98312 | tf_op jit(solution)/shard_map/ppermute | solution.py:463

commit v5 on v4

--- a/solution.py
+++ b/solution.py
@@ -14,7 +14,9 @@
 LANES = 128
 SUBLANES = 8
 CHUNK = 8
-RAISE_UNROLL = 4
+READ = 8
+AHEAD = 3
+RAISE_UNROLL = 8
 SWEEP_UNROLL = 4
 STORES = 4
 MIB = 2**20
@@ -94,7 +96,7 @@
     return swept_tiles(centers, others)
 
 
-def faces_kernel(rows, cols, field, low, high):
+def faces_kernel(start, rows, cols, field, low, high):
     planes, height, _ = field.shape
     lines = field.reshape(planes * height, LANES)
     columns = range(cols // LANES)
@@ -105,7 +107,7 @@
         for out, row, inward in ((low, 0, 1), (high, rows - 1, rows - 2)):
 
             def read(column, y, dz=0):
-                first = (z + 1 + dz) * height + row_of(column, y, rows)
+                first = (start + z + 1 + dz) * height + row_of(column, y, rows)
                 return lines[pl.ds(first, SUBLANES, stride=height), :]
 
             ends = [read(c, row) for c in columns]
@@ -116,14 +118,13 @@
                 out[1, at, x] = tile
         return 0
 
-    lax.fori_loop(0, (planes - 2) // SUBLANES, body, 0)
-
-
-def faces(field, rows, cols):
-    face = jax.ShapeDtypeStruct((2, field.shape[0] - 2, cols), jnp.float32)
-    return pl.pallas_call(
-        functools.partial(faces_kernel, rows, cols),
-        name="faces",
+    lax.fori_loop(0, low.shape[1] // SUBLANES, body, 0)
+
+
+def faces(field, start, count, rows, cols):
+    face = jax.ShapeDtypeStruct((2, count, cols), jnp.float32)
+    return pl.pallas_call(
+        functools.partial(faces_kernel, start, rows, cols),
         out_shape=(face, face),
         in_specs=[VMEM],
         out_specs=(VMEM, VMEM),
@@ -132,98 +133,145 @@
     )(field)
 
 
-def raise_kernel(dist, par, flags_at, occ, field, first, second, flags, buf, ends, fsem, sem):
-    depth, rows, cols = dist.shape
+def raise_planes(start, count, dist, par, flags_at, occ, field, flags, buf, fsem, sem):
+    _, rows, cols = dist.shape
     columns = range(cols // LANES)
-    chunks = depth // CHUNK
+    chunks = count // READ
 
     def reads(chunk):
-        at = pl.ds(chunk * CHUNK, CHUNK)
+        source, target = pl.ds(start + chunk * READ, READ), pl.ds(chunk * READ, READ)
         return [
-            pltpu.make_async_copy(src.at[at], dst.at[at], sem.at[which, chunk])
+            pltpu.make_async_copy(src.at[source], dst.at[target], sem.at[which, chunk])
             for which, (src, dst) in enumerate(zip((dist, par, occ), buf))
         ]
 
     table_in = pltpu.make_async_copy(flags_at, flags, fsem)
     table_in.start()
-    for chunk in range(chunks):
+    for chunk in range(min(AHEAD, chunks)):
         for cp in reads(chunk):
             cp.start()
-    for z in (0, depth + 1):
-        field[z] = jnp.full(field.shape[1:], FAR)
+    for z in (0, field.shape[0] - 1):
+        if start < z <= start + count + 1 or z == start == 0:
+            field[z] = jnp.full(field.shape[1:], FAR)
     table_in.wait()
     table = packed_table(flags)
 
     def body(chunk, acc):
+        @pl.when(chunk + AHEAD < chunks)
+        def _():
+            for cp in reads(chunk + AHEAD):
+                cp.start()
+
         for cp in reads(chunk):
             cp.wait()
 
         def planes(group, acc):
             for part in range(RAISE_UNROLL):
-                z = chunk * CHUNK + group * RAISE_UNROLL + part
-                fill_pads(field, (z + 1,), rows, cols)
+                z = chunk * READ + group * RAISE_UNROLL + part
+                fill_pads(field, (start + z + 1,), rows, cols)
                 for y in range(0, rows, SUBLANES):
                     for column in columns:
                         at = (z, pl.ds(y, SUBLANES), pl.ds(column * LANES, LANES))
                         tile, cleared = raise_tile(table, *(b[at] for b in buf))
                         to = pl.ds(row_of(column, y, rows), SUBLANES)
-                        field[z + 1, to, :] = tile
+                        field[start + z + 1, to, :] = tile
                         acc[part] = acc[part] + cleared
             return acc
 
-        return lax.fori_loop(0, CHUNK // RAISE_UNROLL, planes, acc)
+        return lax.fori_loop(0, READ // RAISE_UNROLL, planes, acc)
 
     zeros = jnp.zeros((SUBLANES, LANES), jnp.int32)
     parts = lax.fori_loop(0, chunks, body, [zeros] * RAISE_UNROLL)
-    total = sum(parts[1:], parts[0])
-
-    def keep_end(side, z):
-        def read(dz, at):
-            return field[z + 1 + dz, pl.ds(at, SUBLANES), :]
-
-        for y in range(0, rows, SUBLANES):
-            swept = swept_plane(read, rows, cols, y, (1, -1)[side : side + 1])
-            for column in columns:
-                x = pl.ds(column * LANES, LANES)
-                ends[side, pl.ds(y, SUBLANES), x] = read(0, row_of(column, y, rows))
-                ends[side, pl.ds(rows + y, SUBLANES), x] = swept[column]
-
-    keep_end(0, 0)
-    keep_end(1, depth - 1)
-    count = jnp.sum(total)
+    return sum(parts[1:], parts[0])
+
+
+def keep_end(field, z, inward, rows, cols, out):
+    def read(dz, at):
+        return field[z + 1 + dz, pl.ds(at, SUBLANES), :]
+
+    for y in range(0, rows, SUBLANES):
+        swept = swept_plane(read, rows, cols, y, (inward,))
+        for column in range(cols // LANES):
+            x = pl.ds(column * LANES, LANES)
+            out[pl.ds(y, SUBLANES), x] = read(0, row_of(column, y, rows))
+            out[pl.ds(rows + y, SUBLANES), x] = swept[column]
+
+
+def raise_start_kernel(count, dist, par, flags_at, occ, field, end, total, flags, buf, fsem, sem):
+    _, rows, cols = dist.shape
+    total[...] = raise_planes(0, count, dist, par, flags_at, occ, field, flags, buf, fsem, sem)
+    keep_end(field, 0, 1, rows, cols, end)
+
+
+def raise_rest_kernel(
+    start, dist, par, flags_at, occ, low, before, _, field, first, second, counts, flags, buf, high, fsem, sem
+):
+    depth, rows, cols = dist.shape
+    total = raise_planes(
+        start, depth - start, dist, par, flags_at, occ, field, flags, buf, fsem, sem
+    )
+    count = jnp.sum(total + before[...])
     row = lax.broadcasted_iota(jnp.int32, (SUBLANES, cols), 0)
-    low = (count & (2**COUNT_BITS - 1)).astype(jnp.float32)
-    high = (count >> COUNT_BITS).astype(jnp.float32)
-    counts = jnp.where(row == 2, low, jnp.where(row == 3, high, 0.0))
-    odd = lax.axis_index("gz") & 1
-    for out, side in ((first, odd), (second, 1 - odd)):
-        out[pl.ds(0, 2 * rows), :] = ends[side]
-        out[pl.ds(2 * rows, SUBLANES), :] = counts
-
-
-def raise_all(dist, par, flags, occ):
+    small = (count & (2**COUNT_BITS - 1)).astype(jnp.float32)
+    large = (count >> COUNT_BITS).astype(jnp.float32)
+    counts[...] = jnp.where(row == 2, small, jnp.where(row == 3, large, 0.0))
+    keep_end(field, depth - 1, -1, rows, cols, high)
+    odd = (lax.axis_index("gz") & 1) == 1
+    for y in range(0, 2 * rows, SUBLANES):
+        at = pl.ds(y, SUBLANES)
+        first[at, :] = jnp.where(odd, high[at, :], low[at, :])
+        second[at, :] = jnp.where(odd, low[at, :], high[at, :])
+    first[pl.ds(2 * rows, SUBLANES), :] = counts[...]
+    second[pl.ds(2 * rows, SUBLANES), :] = counts[...]
+
+
+def raise_scratch(count, dist, par, flags, occ):
+    return [
+        pltpu.VMEM(flags.shape, jnp.int32),
+        [pltpu.VMEM((count, *a.shape[1:]), a.dtype) for a in (dist, par, occ)],
+        pltpu.SemaphoreType.DMA,
+        pltpu.SemaphoreType.DMA((3, count // READ)),
+    ]
+
+
+def raise_start(dist, par, flags, occ, count):
     depth, rows, cols = dist.shape
-    message = jax.ShapeDtypeStruct((2 * rows + SUBLANES, cols), jnp.float32)
-    return pl.pallas_call(
-        raise_kernel,
-        name="raise_all",
+    return pl.pallas_call(
+        functools.partial(raise_start_kernel, count),
+        name="raise_start",
         out_shape=(
             jax.ShapeDtypeStruct((depth + 2, padded_rows(rows, cols), LANES), jnp.float32),
-            message,
-            message,
+            jax.ShapeDtypeStruct((2 * rows, cols), jnp.float32),
+            jax.ShapeDtypeStruct((SUBLANES, LANES), jnp.int32),
         ),
         in_specs=[HBM] * 4,
         out_specs=(VMEM,) * 3,
-        scratch_shapes=[
-            pltpu.VMEM(flags.shape, jnp.int32),
-            [pltpu.VMEM(a.shape, a.dtype) for a in (dist, par, occ)],
-            pltpu.VMEM((2, 2 * rows, cols), jnp.float32),
-            pltpu.SemaphoreType.DMA,
-            pltpu.SemaphoreType.DMA((3, depth // CHUNK)),
-        ],
+        scratch_shapes=raise_scratch(count, dist, par, flags, occ),
         compiler_params=params(20),
-        cost_estimate=cost(12),
+        cost_estimate=cost(8),
     )(dist, par, flags, occ)
+
+
+def raise_rest(dist, par, flags, occ, low, before, field, start):
+    depth, rows, cols = dist.shape
+    message = jax.ShapeDtypeStruct((2 * rows + SUBLANES, cols), jnp.float32)
+    scratch = raise_scratch(depth - start, dist, par, flags, occ)
+    return pl.pallas_call(
+        functools.partial(raise_rest_kernel, start),
+        name="raise_rest",
+        out_shape=(
+            jax.ShapeDtypeStruct(field.shape, jnp.float32),
+            message,
+            message,
+            jax.ShapeDtypeStruct((SUBLANES, cols), jnp.float32),
+        ),
+        in_specs=[HBM] * 4 + [VMEM] * 3,
+        out_specs=(VMEM,) * 4,
+        input_output_aliases={6: 0},
+        scratch_shapes=scratch[:2] + [pltpu.VMEM((2 * rows, cols), jnp.float32)] + scratch[2:],
+        compiler_params=params(20),
+        cost_estimate=cost(8),
+    )(dist, par, flags, occ, low, before, field)
 
 
 def sweep_once_kernel(start, count, rows, cols, field, once):
@@ -408,19 +456,23 @@
     )(first, second, slab_low, slab_high, out)
 
 
-def patch_y_kernel(scale, slabs, edges, low, high, clow, chigh, counts, _, out, share, buf, sem):
+def patch_y_kernel(scale, slabs, edges, low0, low1, high0, high1, clow, chigh, counts, _, out, share, buf, sem):
     depth, rows, _ = out.shape
     slab = lax.axis_index("gz")
     copies = []
-    for side, (face, corner) in enumerate(((low, clow), (high, chigh))):
+    for side, (parts, corner) in enumerate((((low0, low1), clow), ((high0, high1), chigh))):
         for away in range(2):
             edge = (away, 3 - away)[side]
             row = (away, rows - 1 - away)[side]
             at = 2 * side + away
-            reach = face[1 - away] + VOXEL
-            if away:
-                reach = reach + VOXEL
-            buf[at] = jnp.minimum(edges[edge], reach)
+            z = 0
+            for face in parts:
+                planes = pl.ds(z, face.shape[1])
+                reach = face[1 - away] + VOXEL
+                if away:
+                    reach = reach + VOXEL
+                buf[at, planes, :] = jnp.minimum(edges[edge, planes, :], reach)
+                z += face.shape[1]
             if not away:
                 for end, z in enumerate((0, depth - 1)):
                     missing = slab == (0, slabs - 1)[end]
@@ -440,7 +492,7 @@
         cp.wait()
 
 
-def patch_y(scale, edges, low, high, clow, chigh, counts, out):
+def patch_y(scale, edges, lows, highs, clow, chigh, counts, out):
     depth, _, cols = out.shape
     return pl.pallas_call(
         functools.partial(patch_y_kernel, scale, lax.axis_size("gz")),
@@ -449,13 +501,13 @@
             jax.ShapeDtypeStruct(out.shape, out.dtype),
             jax.ShapeDtypeStruct((1, 1), jnp.float32),
         ),
-        in_specs=[VMEM] * 6 + [HBM],
+        in_specs=[VMEM] * 8 + [HBM],
         out_specs=(HBM, VMEM),
-        input_output_aliases={6: 0},
+        input_output_aliases={8: 0},
         scratch_shapes=[pltpu.VMEM((4, depth, cols), jnp.float32), pltpu.SemaphoreType.DMA((4,))],
         compiler_params=params(8),
         cost_estimate=cost(2),
-    )(edges, low, high, clow, chigh, counts, out)
+    )(edges, *lows, *highs, clow, chigh, counts, out)
 
 
 def swapped(value, axis, partner):
@@ -476,41 +528,50 @@
         pltpu.with_memory_space_constraint(a, pltpu.HBM)
         for a in (distance, parent, removed.reshape(-1, LANES), occupied)
     )
-
-    field, first, second = raise_all(distance, parent, flags, occupied)
+    lows, highs = [], []
+
+    def send(field, start, count):
+        ylow, yhigh = faces(field, start, count, rows, cols)
+        lows.append(shifted(yhigh, "gy", 1))
+        highs.append(shifted(ylow, "gy", -1))
+
+    early = half + READ
+    field, end, total = raise_start(distance, parent, flags, occupied, early)
+    send(field, 0, half)
+    field, first, second, counts = raise_rest(
+        distance, parent, flags, occupied, end, total, field, early
+    )
+
+    bit = 2
+    while bit < columns:
+        masks = [m for m in (bit, 2 * bit, 3 * bit) if m < columns]
+        got = []
+        for mask in masks:
+            got.append(swapped(counts, "gy", lambda i: i ^ mask))
+        counts = sum(got, counts)
+        bit *= 4
+    send(field, half, depth - half)
+    once0 = sweep_once(field, 0, half, rows, cols)
+    counts, once0 = tied((counts, once0))
+
+    first = first.at[2 * rows :].set(counts)
     got_first = swapped(first, "gz", lambda i: i - 1 + 2 * (i % 2))
-    ylow, yhigh = faces(field, rows, cols)
-    low = shifted(yhigh, "gy", 1)
-    high = shifted(ylow, "gy", -1)
-    once0 = sweep_once(field, 0, half, rows, cols)
-    got_first, once0 = tied((got_first, once0))
-    second = second.at[2 * rows :].add(got_first[2 * rows :])
+    once1 = sweep_once(field, half, half, rows, cols)
+    lowered, half0 = sweep_again(once0, None, 0, depth, rows, cols)
+    got_first, half0 = tied((got_first, half0))
+    counts = counts + got_first[2 * rows :]
+    second = second.at[2 * rows :].set(counts)
     got_second = swapped(second, "gz", lambda i: i ^ 1)
-    once1 = sweep_once(field, half, half, rows, cols)
-    got_second, once1 = tied((got_second, once1))
-    counts = second[2 * rows :] + got_second[2 * rows :]
-    more = jnp.zeros_like(counts)
-
-    lowered, half0 = sweep_again(once0, None, 0, depth, rows, cols)
     lowered, half1 = sweep_again(once1, lowered, half, depth, rows, cols)
-    step = columns // 2
-    turn = 0
-    while step > 1:
-        if turn:
-            counts = counts + more
-        more = swapped(counts, "gy", lambda i: i ^ step)
-        if turn == 0:
-            more, half0 = tied((more, half0))
-        elif turn == 1:
-            more, half1 = tied((more, half1))
-        step //= 2
-        turn += 1
-    clow, chigh, counts = corners(got_first, got_second, counts, more)
+    got_second, half1 = tied((got_second, half1))
+    clow, chigh, counts = corners(got_first, got_second, counts, got_second[2 * rows :])
     from_low = shifted(chigh, "gy", 1)
     from_high = shifted(clow, "gy", -1)
     lowered, edges = patch_z(got_first, got_second, half0, half1, lowered)
     total = distance.size * slabs * columns
-    lowered, share = patch_y(100.0 / total, edges, low, high, from_low, from_high, counts, lowered)
+    lowered, share = patch_y(
+        100.0 / total, edges, lows, highs, from_low, from_high, counts, lowered
+    )
     return (lowered, share[0, 0])
 
 

time: 43.8 us -> 49.7 us (1.13)
  starting transfers between devices: 14.4 us -> 19.2 us
  waiting for transfers between devices: 7.95 us -> 9.49 us
  Pallas kernels: 20.5 us -> 20 us
    ppermute x8 -> x11, starting transfers between devices: 14.4 us -> 19.2 us  [swapped(): lax.ppermute(value, axis, [(i, partner(i) % count) for i in range(count)])]
    ppermute x8 -> x11, waiting for transfers between devices: 7.95 us -> 9.49 us  [swapped(): lax.ppermute(value, axis, [(i, partner(i) % count) for i in range(count)])]
    pallas_call x2 -> x4, Pallas kernels: 9.54 us -> 9 us  [the longest x1 4.59 us: raise_start(): pl.pallas_call(functools.partial(raise_start_kernel, count), name='raise_...]
  transfers between devices with their start and end apart: 8 -> 11, of which waited for: 3 -> 5; matrix products, arithmetic and copies ran while one was open for 0% -> 0% of each run, Pallas kernels for 24% -> 20%
where the time goes in v5:
time: 49.7 us; the launch traced here: 49.5 us
  Pallas kernels  20 us (40%)
  starting transfers between devices  19.2 us (39%)
  waiting for transfers between devices  9.49 us (19%)
  between operations  0.8 us (2%)
    ppermute x11, starting transfers between devices, swapped(): lax.ppermute(value, axis, [(i, partner(i) % count) for i in range(count)])  19.2 us
    ppermute x11, waiting for transfers between devices, swapped(): lax.ppermute(value, axis, [(i, partner(i) % count) for i in range(count)])  9.49 us
    pallas_call x2, Pallas kernels, sweep_again(): pl.pallas_call(functools.partial(sweep_again_kernel, start), out_shape=(j...  5.07 us
    pallas_call x1, Pallas kernels, raise_start(): pl.pallas_call(functools.partial(raise_start_kernel, count), name='raise_...  4.59 us
    pallas_call x2, Pallas kernels, sweep_once(): pl.pallas_call(functools.partial(sweep_once_kernel, start, count, rows, c...  3.6 us
    pallas_call x1, Pallas kernels, raise_rest(): pl.pallas_call(functools.partial(raise_rest_kernel, start), name='raise_r...  3.52 us
    pallas_call x1, Pallas kernels, patch_y(): pl.pallas_call(functools.partial(patch_y_kernel, scale, lax.axis_size('gz...  1.55 us
  transfers between devices with their start and end apart: 11, of which 5 were waited for; matrix products, arithmetic and copies ran while one was open for 0% of the time, Pallas kernels for 20%

profile of v5, /device:TPU:0, one launch (start us, length us, event | category | flops | bytes accessed | tf_op | source)
XLA Modules:
  0.0 49.5 jit_solution(8189898632103833851)
XLA Ops:
  0.6 4.6 %raise_start.1 = (f32[66,200,128]{2,1,0:T(8,128)S(1)}, f32[32,1024]{1,0:T(8,128)S(1)}, s32[8,128]{1,0:T(8,128)S(1)}) custom-call(f32[64,16,1024]{2,1,0:T(8,128)} %dist.3, s32[64,16,1024]{2,1,0:T(8,128)} %par.3, s32[32,128]{1,0:T(8,128)} %bitcast.2, s32[64,16,1024]{2,1,0:T(8,128)} %occ.3), custom_call_target="tpu_custom_call" | custom-call | bytes 8388608 | tf_op jit(solution)/shard_map/raise_start/pallas_call | solution.py:239
  5.2 0.4 shard_map.63
  5.7 3.5 %raise_rest.1 = (f32[66,200,128]{2,1,0:T(8,128)S(1)}, f32[40,1024]{1,0:T(8,128)S(1)}, f32[40,1024]{1,0:T(8,128)S(1)}, f32[8,1024]{1,0:T(8,128)S(1)}) custom-call(f32[64,16,1024]{2,1,0:T(8,128)} %dist.3, s32[64,16,1024]{2,1,0:T(8,128)} %par.3, s32[32,128]{1,0:T(8,128)} %bitcast.3, s32[64,16,1024]{2,1,0:T(8,128)} %occ.3, ...), custom_call_target="tpu_custom_call", output_to_operand_aliasing={{0}: (6, {})} | custom-call | bytes 8388608 | tf_op jit(solution)/shard_map/raise_rest/pallas_call | solution.py:259
  9.2 5.1 %collective-permute-start.2 = (f32[8,1024]{1,0:T(8,128)S(1)}, f32[8,1024]{1,0:T(8,128)S(1)}, u32[]{:S(2)}, u32[]{:S(2)}) collective-permute-start(f32[8,1024]{1,0:T(8,128)S(1)} %get-tuple-element.58), channel_id=1, source_target_pairs={{0,6},{1,7},{2,4},{3,5},{4,2},{5,3},{6,0},{7,1},{8,14},{9,15},{10,... | collective-permute-start | bytes 98312 | tf_op jit(solution)/shard_map/ppermute | solution.py:515
  14.4 0.0 collective-permute-start.1
  14.4 0.6 %collective-permute-start = (f32[8,1024]{1,0:T(8,128)S(1)}, f32[8,1024]{1,0:T(8,128)S(1)}, u32[]{:S(2)}, u32[]{:S(2)}) collective-permute-start(f32[8,1024]{1,0:T(8,128)S(1)} %get-tuple-element.58), channel_id=1, source_target_pairs={{0,2},{1,3},{2,0},{3,1},{4,6},{5,7},{6,4},{7,5},{8,10},{9,11},{10,... | collective-permute-start | bytes 98312 | tf_op jit(solution)/shard_map/ppermute | solution.py:515
  15.0 1.8 %shard_map.59.once = f32[34,200,128]{2,1,0:T(8,128)S(1)} custom-call(f32[66,200,128]{2,1,0:T(8,128)S(1)} %get-tuple-element.59.field), custom_call_target="tpu_custom_call" | custom-call | bytes 8388608 | tf_op jit(solution)/shard_map/pallas_call | solution.py:303
  16.8 0.0 collective-permute-done.2
  16.8 2.4 %collective-permute-done.1 = f32[8,1024]{1,0:T(8,128)S(1)} collective-permute-done((f32[8,1024]{1,0:T(8,128)S(1)}, f32[8,1024]{1,0:T(8,128)S(1)}, u32[]{:S(2)}, u32[]{:S(2)}) %collective-permute-start.1) | collective-permute-done | bytes 32800 | tf_op jit(solution)/shard_map/ppermute | solution.py:515
  19.2 0.0 collective-permute-done
  19.2 0.1 collective-permute-start.3
  19.3 1.6 %collective-permute-start.5 = (f32[2,32,1024]{2,1,0:T(8,128)S(1)}, f32[2,32,1024]{2,1,0:T(8,128)S(1)}, u32[]{:S(2)}, u32[]{:S(2)}) collective-permute-start(f32[2,32,1024]{2,1,0:T(8,128)S(1)} %get-tuple-element.72), channel_id=1, source_target_pairs={{0,1},{1,2},{2,3},{3,4},{4,5},{5,6},{6,7},{7,0},{8,9},{9,10},{10,1... | collective-permute-start | bytes 786440 | tf_op jit(solution)/shard_map/ppermute | solution.py:515
  20.8 3.2 %collective-permute-start.7 = (f32[2,32,1024]{2,1,0:T(8,128)S(1)}, f32[2,32,1024]{2,1,0:T(8,128)S(1)}, u32[]{:S(2)}, u32[]{:S(2)}) collective-permute-start(f32[2,32,1024]{2,1,0:T(8,128)S(1)} %get-tuple-element.74), channel_id=1, source_target_pairs={{0,7},{1,0},{2,1},{3,2},{4,3},{5,4},{6,5},{7,6},{8,15},{9,8},{10,9... | collective-permute-start | bytes 786440 | tf_op jit(solution)/shard_map/ppermute | solution.py:515
  24.1 0.4 shard_map.64
  24.5 0.1 collective-permute-start.6
  24.6 4.7 %collective-permute-start.8 = (f32[2,32,1024]{2,1,0:T(8,128)S(1)}, f32[2,32,1024]{2,1,0:T(8,128)S(1)}, u32[]{:S(2)}, u32[]{:S(2)}) collective-permute-start(f32[2,32,1024]{2,1,0:T(8,128)S(1)} %get-tuple-element.75), channel_id=1, source_target_pairs={{0,7},{1,0},{2,1},{3,2},{4,3},{5,4},{6,5},{7,6},{8,15},{9,8},{10,9... | collective-permute-start | bytes 786440 | tf_op jit(solution)/shard_map/ppermute | solution.py:515
  29.3 2.5 %shard_map.60 = (f32[64,16,1024]{2,1,0:T(8,128)}, f32[4096,128]{1,0:T(8,128)S(1)}) custom-call(f32[34,200,128]{2,1,0:T(8,128)S(1)} %shard_map.59.once), custom_call_target="tpu_custom_call" | custom-call | bytes 8388608 | tf_op jit(solution)/shard_map/pallas_call | solution.py:352
  31.8 0.0 collective-permute-done.3.first
  31.9 0.5 collective-permute-start.4
  32.3 1.8 %shard_map.61.once = f32[34,200,128]{2,1,0:T(8,128)S(1)} custom-call(f32[66,200,128]{2,1,0:T(8,128)S(1)} %get-tuple-element.59.field), custom_call_target="tpu_custom_call" | custom-call | bytes 8388608 | tf_op jit(solution)/shard_map/pallas_call | solution.py:303
  34.1 2.5 %shard_map.62 = (f32[64,16,1024]{2,1,0:T(8,128)}, f32[4096,128]{1,0:T(8,128)S(1)}) custom-call(f32[34,200,128]{2,1,0:T(8,128)S(1)} %shard_map.61.once, f32[64,16,1024]{2,1,0:T(8,128)} %get-tuple-element.65.refs_0_), custom_call_target="tpu_custom_call", output_to_operand_aliasing={{0}: (1, {})} | custom-call | bytes 8388608 | tf_op jit(solution)/shard_map/pallas_call | solution.py:352
  36.7 0.0 collective-permute-done.4.second
  36.7 0.1 collective-permute-start.9
  36.8 1.4 %collective-permute-done.5.low0 = f32[2,32,1024]{2,1,0:T(8,128)S(1)} collective-permute-done((f32[2,32,1024]{2,1,0:T(8,128)S(1)}, f32[2,32,1024]{2,1,0:T(8,128)S(1)}, u32[]{:S(2)}, u32[]{:S(2)}) %collective-permute-start.5) | collective-permute-done | bytes 262176 | tf_op jit(solution)/shard_map/ppermute | solution.py:515
  38.2 3.3 %collective-permute-start.10 = (f32[8,1024]{1,0:T(8,128)S(1)}, f32[8,1024]{1,0:T(8,128)S(1)}, u32[]{:S(2)}, u32[]{:S(2)}) collective-permute-start(f32[8,1024]{1,0:T(8,128)S(1)} %get-tuple-element.77), channel_id=1, source_target_pairs={{0,7},{1,0},{2,1},{3,2},{4,3},{5,4},{6,5},{7,6},{8,15},{9,8},{10,9... | collective-permute-start | bytes 98312 | tf_op jit(solution)/shard_map/ppermute | solution.py:515
  41.5 0.8 %patch_z.1 = (f32[64,16,1024]{2,1,0:T(8,128)}, f32[4,64,1024]{2,1,0:T(8,128)S(1)}) custom-call(f32[40,1024]{1,0:T(8,128)S(1)} %collective-permute-done.3.first, f32[40,1024]{1,0:T(8,128)S(1)} %collective-permute-done.4.second, f32[4096,128]{1,0:T(8,128)S(1)} %get-tuple-element.68.slab_low, ...), custom_call_target="tpu_custom_call", output_to_operand_aliasing={{0}: (4, {})} | custom-call | bytes 1048576 | tf_op jit(solution)/shard_map/patch_z/pallas_call | solution.py:440
  42.3 0.0 collective-permute-done.7.high0
  42.3 2.2 %collective-permute-done.6.low1 = f32[2,32,1024]{2,1,0:T(8,128)S(1)} collective-permute-done((f32[2,32,1024]{2,1,0:T(8,128)S(1)}, f32[2,32,1024]{2,1,0:T(8,128)S(1)}, u32[]{:S(2)}, u32[]{:S(2)}) %collective-permute-start.6) | collective-permute-done | bytes 262176 | tf_op jit(solution)/shard_map/ppermute | solution.py:515
  44.5 2.8 %collective-permute-done.8.high1 = f32[2,32,1024]{2,1,0:T(8,128)S(1)} collective-permute-done((f32[2,32,1024]{2,1,0:T(8,128)S(1)}, f32[2,32,1024]{2,1,0:T(8,128)S(1)}, u32[]{:S(2)}, u32[]{:S(2)}) %collective-permute-start.8) | collective-permute-done | bytes 262176 | tf_op jit(solution)/shard_map/ppermute | solution.py:515
  47.3 0.0 collective-permute-done.9.clow
  47.3 0.7 %collective-permute-done.10.chigh = f32[8,1024]{1,0:T(8,128)S(1)} collective-permute-done((f32[8,1024]{1,0:T(8,128)S(1)}, f32[8,1024]{1,0:T(8,128)S(1)}, u32[]{:S(2)}, u32[]{:S(2)}) %collective-permute-start.10) | collective-permute-done | bytes 32800 | tf_op jit(solution)/shard_map/ppermute | solution.py:515
  48.0 1.5 %patch_y.1 = (f32[64,16,1024]{2,1,0:T(8,128)}, f32[1,1]{1,0:T(1,128)}) custom-call(f32[4,64,1024]{2,1,0:T(8,128)S(1)} %get-tuple-element.71.edges, f32[2,32,1024]{2,1,0:T(8,128)S(1)} %collective-permute-done.5.low0, f32[2,32,1024]{2,1,0:T(8,128)S(1)} %collective-permute-done.6.low1, ...), custom_call_target="tpu_custom_call", output_to_operand_aliasing={{0}: (8, {})} | custom-call | bytes 2097152 | tf_op jit(solution)/shard_map/patch_y/pallas_call | solution.py:497
  (5 shorter events, 0.0 us)
Async XLA Ops:
  9.2 7.6 %collective-permute-start.2 = (f32[8,1024]{1,0:T(8,128)S(1)}, f32[8,1024]{1,0:T(8,128)S(1)}, u32[]{:S(2)}, u32[]{:S(2)}) collective-permute-start(f32[8,1024]{1,0:T(8,128)S(1)} %get-tuple-element.58), channel_id=1, source_target_pairs={{0,6},{1,7},{2,4},{3,5},{4,2},{5,3},{6,0},{7,1},{8,14},{9,15},{10,... | collective-permute-start | bytes 98312 | tf_op jit(solution)/shard_map/ppermute | solution.py:515
  14.4 4.8 %collective-permute-start.1 = (f32[8,1024]{1,0:T(8,128)S(1)}, f32[8,1024]{1,0:T(8,128)S(1)}, u32[]{:S(2)}, u32[]{:S(2)}) collective-permute-start(f32[8,1024]{1,0:T(8,128)S(1)} %get-tuple-element.58), channel_id=1, source_target_pairs={{0,4},{1,5},{2,6},{3,7},{4,0},{5,1},{6,2},{7,3},{8,12},{9,13},{10,... | collective-permute-start | bytes 98312 | tf_op jit(solution)/shard_map/ppermute | solution.py:515
  14.4 4.8 %collective-permute-start = (f32[8,1024]{1,0:T(8,128)S(1)}, f32[8,1024]{1,0:T(8,128)S(1)}, u32[]{:S(2)}, u32[]{:S(2)}) collective-permute-start(f32[8,1024]{1,0:T(8,128)S(1)} %get-tuple-element.58), channel_id=1, source_target_pairs={{0,2},{1,3},{2,0},{3,1},{4,6},{5,7},{6,4},{7,5},{8,10},{9,11},{10,... | collective-permute-start | bytes 98312 | tf_op jit(solution)/shard_map/ppermute | solution.py:515
  19.2 12.6 %collective-permute-start.3 = (f32[40,1024]{1,0:T(8,128)S(1)}, f32[40,1024]{1,0:T(8,128)S(1)}, u32[]{:S(2)}, u32[]{:S(2)}) collective-permute-start(f32[40,1024]{1,0:T(8,128)S(1)} %constant_dynamic-update-slice_fusion.1), channel_id=1, source_target_pairs={{0,24},{8,16},{16,8},{24,0},{1,25},{9,17},{17,9},{25,1},{2,26},{10... | collective-permute-start | bytes 491528 | tf_op jit(solution)/shard_map/ppermute | solution.py:515
  19.3 18.9 %collective-permute-start.5 = (f32[2,32,1024]{2,1,0:T(8,128)S(1)}, f32[2,32,1024]{2,1,0:T(8,128)S(1)}, u32[]{:S(2)}, u32[]{:S(2)}) collective-permute-start(f32[2,32,1024]{2,1,0:T(8,128)S(1)} %get-tuple-element.72), channel_id=1, source_target_pairs={{0,1},{1,2},{2,3},{3,4},{4,5},{5,6},{6,7},{7,0},{8,9},{9,10},{10,1... | collective-permute-start | bytes 786440 | tf_op jit(solution)/shard_map/ppermute | solution.py:515
  20.8 21.4 %collective-permute-start.7 = (f32[2,32,1024]{2,1,0:T(8,128)S(1)}, f32[2,32,1024]{2,1,0:T(8,128)S(1)}, u32[]{:S(2)}, u32[]{:S(2)}) collective-permute-start(f32[2,32,1024]{2,1,0:T(8,128)S(1)} %get-tuple-element.74), channel_id=1, source_target_pairs={{0,7},{1,0},{2,1},{3,2},{4,3},{5,4},{6,5},{7,6},{8,15},{9,8},{10,9... | collective-permute-start | bytes 786440 | tf_op jit(solution)/shard_map/ppermute | solution.py:515
  24.5 20.0 %collective-permute-start.6 = (f32[2,32,1024]{2,1,0:T(8,128)S(1)}, f32[2,32,1024]{2,1,0:T(8,128)S(1)}, u32[]{:S(2)}, u32[]{:S(2)}) collective-permute-start(f32[2,32,1024]{2,1,0:T(8,128)S(1)} %get-tuple-element.73), channel_id=1, source_target_pairs={{0,1},{1,2},{2,3},{3,4},{4,5},{5,6},{6,7},{7,0},{8,9},{9,10},{10,1... | collective-permute-start | bytes 786440 | tf_op jit(solution)/shard_map/ppermute | solution.py:515
  24.6 22.7 %collective-permute-start.8 = (f32[2,32,1024]{2,1,0:T(8,128)S(1)}, f32[2,32,1024]{2,1,0:T(8,128)S(1)}, u32[]{:S(2)}, u32[]{:S(2)}) collective-permute-start(f32[2,32,1024]{2,1,0:T(8,128)S(1)} %get-tuple-element.75), channel_id=1, source_target_pairs={{0,7},{1,0},{2,1},{3,2},{4,3},{5,4},{6,5},{7,6},{8,15},{9,8},{10,9... | collective-permute-start | bytes 786440 | tf_op jit(solution)/shard_map/ppermute | solution.py:515
  31.9 4.8 %collective-permute-start.4 = (f32[40,1024]{1,0:T(8,128)S(1)}, f32[40,1024]{1,0:T(8,128)S(1)}, u32[]{:S(2)}, u32[]{:S(2)}) collective-permute-start(f32[40,1024]{1,0:T(8,128)S(1)} %get-tuple-element.82), channel_id=1, source_target_pairs={{0,8},{8,0},{16,24},{24,16},{1,9},{9,1},{17,25},{25,17},{2,10},{10... | collective-permute-start | bytes 491528 | tf_op jit(solution)/shard_map/ppermute | solution.py:515
  36.7 10.6 %collective-permute-start.9 = (f32[8,1024]{1,0:T(8,128)S(1)}, f32[8,1024]{1,0:T(8,128)S(1)}, u32[]{:S(2)}, u32[]{:S(2)}) collective-permute-start(f32[8,1024]{1,0:T(8,128)S(1)} %get-tuple-element.76), channel_id=1, source_target_pairs={{0,1},{1,2},{2,3},{3,4},{4,5},{5,6},{6,7},{7,0},{8,9},{9,10},{10,1... | collective-permute-start | bytes 98312 | tf_op jit(solution)/shard_map/ppermute | solution.py:515
  38.2 9.8 %collective-permute-start.10 = (f32[8,1024]{1,0:T(8,128)S(1)}, f32[8,1024]{1,0:T(8,128)S(1)}, u32[]{:S(2)}, u32[]{:S(2)}) collective-permute-start(f32[8,1024]{1,0:T(8,128)S(1)} %get-tuple-element.77), channel_id=1, source_target_pairs={{0,7},{1,0},{2,1},{3,2},{4,3},{5,4},{6,5},{7,6},{8,15},{9,8},{10,9... | collective-permute-start | bytes 98312 | tf_op jit(solution)/shard_map/ppermute | solution.py:515

commit v6 on v5

--- a/solution.py
+++ b/solution.py
@@ -96,38 +96,54 @@
     return swept_tiles(centers, others)
 
 
-def faces_kernel(start, rows, cols, field, low, high):
+def face_tiles(field, rows, cols, row, inward, z):
     planes, height, _ = field.shape
     lines = field.reshape(planes * height, LANES)
     columns = range(cols // LANES)
 
+    def read(column, y, dz=0):
+        first = (z + 1 + dz) * height + row_of(column, y, rows)
+        return lines[pl.ds(first, SUBLANES, stride=height), :]
+
+    ends = [read(c, row) for c in columns]
+    others = [(read(c, row, -1), read(c, row, 1), read(c, inward)) for c in columns]
+    return ends, swept_tiles(ends, others)
+
+
+def write_faces(field, rows, cols, top, start, out):
     def body(group, _):
-        z = pl.multiple_of(group * SUBLANES, SUBLANES)
-        at = pl.ds(z, SUBLANES)
-        for out, row, inward in ((low, 0, 1), (high, rows - 1, rows - 2)):
-
-            def read(column, y, dz=0):
-                first = (start + z + 1 + dz) * height + row_of(column, y, rows)
-                return lines[pl.ds(first, SUBLANES, stride=height), :]
-
-            ends = [read(c, row) for c in columns]
-            others = [(read(c, row, -1), read(c, row, 1), read(c, inward)) for c in columns]
-            for column, tile in enumerate(swept_tiles(ends, others)):
+        at = pl.ds(pl.multiple_of(group * SUBLANES, SUBLANES), SUBLANES)
+
+        def write(row, inward):
+            ends, swept = face_tiles(field, rows, cols, row, inward, start + group * SUBLANES)
+            for column, (end, tile) in enumerate(zip(ends, swept)):
                 x = pl.ds(column * LANES, LANES)
-                out[0, at, x] = ends[column]
+                out[0, at, x] = end
                 out[1, at, x] = tile
+
+        pl.when(top)(lambda: write(rows - 1, rows - 2))
+        pl.when(jnp.logical_not(top))(lambda: write(0, 1))
         return 0
 
-    lax.fori_loop(0, low.shape[1] // SUBLANES, body, 0)
-
-
-def faces(field, start, count, rows, cols):
+    lax.fori_loop(0, out.shape[1] // SUBLANES, body, 0)
+
+
+def faces_kernel(start, rows, cols, field, near, *far):
+    odd = (lax.axis_index("gy") & 1) == 1
+    write_faces(field, rows, cols, jnp.logical_not(odd), start, near)
+    for out in far:
+        write_faces(field, rows, cols, odd, 0, out)
+
+
+def faces(field, start, count, rows, cols, both):
     face = jax.ShapeDtypeStruct((2, count, cols), jnp.float32)
+    whole = jax.ShapeDtypeStruct((2, field.shape[0] - 2, cols), jnp.float32)
+    shapes = (face, whole) if both else (face,)
     return pl.pallas_call(
         functools.partial(faces_kernel, start, rows, cols),
-        out_shape=(face, face),
+        out_shape=shapes,
         in_specs=[VMEM],
-        out_specs=(VMEM, VMEM),
+        out_specs=(VMEM,) * len(shapes),
         compiler_params=params(8),
         cost_estimate=cost(2),
     )(field)
@@ -456,19 +472,22 @@
     )(first, second, slab_low, slab_high, out)
 
 
-def patch_y_kernel(scale, slabs, edges, low0, low1, high0, high1, clow, chigh, counts, _, out, share, buf, sem):
+def patch_y_kernel(scale, slabs, edges, near0, near1, far, clow, chigh, counts, _, out, share, buf, sem):
     depth, rows, _ = out.shape
     slab = lax.axis_index("gz")
     copies = []
-    for side, (parts, corner) in enumerate((((low0, low1), clow), ((high0, high1), chigh))):
+    odd = (lax.axis_index("gy") & 1) == 1
+    for side, corner in enumerate((clow, chigh)):
         for away in range(2):
             edge = (away, 3 - away)[side]
             row = (away, rows - 1 - away)[side]
             at = 2 * side + away
             z = 0
-            for face in parts:
+            for face in (near0, near1):
                 planes = pl.ds(z, face.shape[1])
-                reach = face[1 - away] + VOXEL
+                ours, theirs = face[1 - away], far[1 - away, planes, :]
+                is_near = odd if side == 0 else jnp.logical_not(odd)
+                reach = jnp.where(is_near, ours, theirs) + VOXEL
                 if away:
                     reach = reach + VOXEL
                 buf[at, planes, :] = jnp.minimum(edges[edge, planes, :], reach)
@@ -492,7 +511,7 @@
         cp.wait()
 
 
-def patch_y(scale, edges, lows, highs, clow, chigh, counts, out):
+def patch_y(scale, edges, near0, near1, far, clow, chigh, counts, out):
     depth, _, cols = out.shape
     return pl.pallas_call(
         functools.partial(patch_y_kernel, scale, lax.axis_size("gz")),
@@ -501,13 +520,13 @@
             jax.ShapeDtypeStruct(out.shape, out.dtype),
             jax.ShapeDtypeStruct((1, 1), jnp.float32),
         ),
-        in_specs=[VMEM] * 8 + [HBM],
+        in_specs=[VMEM] * 7 + [HBM],
         out_specs=(HBM, VMEM),
-        input_output_aliases={8: 0},
+        input_output_aliases={7: 0},
         scratch_shapes=[pltpu.VMEM((4, depth, cols), jnp.float32), pltpu.SemaphoreType.DMA((4,))],
         compiler_params=params(8),
         cost_estimate=cost(2),
-    )(edges, *lows, *highs, clow, chigh, counts, out)
+    )(edges, near0, near1, far, clow, chigh, counts, out)
 
 
 def swapped(value, axis, partner):
@@ -528,35 +547,32 @@
         pltpu.with_memory_space_constraint(a, pltpu.HBM)
         for a in (distance, parent, removed.reshape(-1, LANES), occupied)
     )
-    lows, highs = [], []
-
-    def send(field, start, count):
-        ylow, yhigh = faces(field, start, count, rows, cols)
-        lows.append(shifted(yhigh, "gy", 1))
-        highs.append(shifted(ylow, "gy", -1))
-
     early = half + READ
     field, end, total = raise_start(distance, parent, flags, occupied, early)
-    send(field, 0, half)
+    (face0,) = faces(field, 0, half, rows, cols, False)
+    near0 = swapped(face0, "gy", lambda i: i ^ 1)
     field, first, second, counts = raise_rest(
         distance, parent, flags, occupied, end, total, field, early
     )
-
-    bit = 2
-    while bit < columns:
-        masks = [m for m in (bit, 2 * bit, 3 * bit) if m < columns]
-        got = []
-        for mask in masks:
-            got.append(swapped(counts, "gy", lambda i: i ^ mask))
-        counts = sum(got, counts)
-        bit *= 4
-    send(field, half, depth - half)
+    face1, face = faces(field, half, depth - half, rows, cols, True)
+    near1 = swapped(face1, "gy", lambda i: i ^ 1)
     once0 = sweep_once(field, 0, half, rows, cols)
-    counts, once0 = tied((counts, once0))
+    once1 = sweep_once(field, half, half, rows, cols)
+
+    mask = columns // 2
+    while mask > 1:
+        got = swapped(counts, "gy", lambda i: i ^ mask)
+        if mask == 4:
+            got, once0 = tied((got, once0))
+        if mask == 2:
+            got, once1 = tied((got, once1))
+        counts = counts + got
+        mask //= 2
+    counts, face = tied((counts, face))
+    far = swapped(face, "gy", lambda i: i - 1 + 2 * (i % 2))
 
     first = first.at[2 * rows :].set(counts)
     got_first = swapped(first, "gz", lambda i: i - 1 + 2 * (i % 2))
-    once1 = sweep_once(field, half, half, rows, cols)
     lowered, half0 = sweep_again(once0, None, 0, depth, rows, cols)
     got_first, half0 = tied((got_first, half0))
     counts = counts + got_first[2 * rows :]
@@ -570,7 +586,7 @@
     lowered, edges = patch_z(got_first, got_second, half0, half1, lowered)
     total = distance.size * slabs * columns
     lowered, share = patch_y(
-        100.0 / total, edges, lows, highs, from_low, from_high, counts, lowered
+        100.0 / total, edges, near0, near1, far, from_low, from_high, counts, lowered
     )
     return (lowered, share[0, 0])
 

time: 49.7 us -> 52.2 us (1.050)
  waiting for transfers between devices: 9.49 us -> 13 us
  starting transfers between devices: 19.2 us -> 17.5 us
  Pallas kernels: 20 us -> 20.7 us
    ppermute x11 -> x9, waiting for transfers between devices: 9.49 us -> 13 us  [swapped(): lax.ppermute(value, axis, [(i, partner(i) % count) for i in range(count)])]
    ppermute x11 -> x9, starting transfers between devices: 19.2 us -> 17.5 us  [swapped(): lax.ppermute(value, axis, [(i, partner(i) % count) for i in range(count)])]
    pallas_call x2, Pallas kernels: 0.89 us -> 1.62 us  [faces(): pl.pallas_call(functools.partial(faces_kernel, start, rows, cols), out_sh...]
  transfers between devices with their start and end apart: 11 -> 9, of which waited for: 5 -> 4; matrix products, arithmetic and copies ran while one was open for 0% -> 0% of each run, Pallas kernels for 20% -> 20%
where the time goes in v6:
time: 52.2 us; the launch traced here: 52 us
  Pallas kernels  20.7 us (40%)
  starting transfers between devices  17.5 us (34%)
  waiting for transfers between devices  13 us (25%)
  between operations  0.77 us (1%)
    ppermute x9, starting transfers between devices, swapped(): lax.ppermute(value, axis, [(i, partner(i) % count) for i in range(count)])  17.5 us
    ppermute x9, waiting for transfers between devices, swapped(): lax.ppermute(value, axis, [(i, partner(i) % count) for i in range(count)])  13 us
    pallas_call x2, Pallas kernels, sweep_again(): pl.pallas_call(functools.partial(sweep_again_kernel, start), out_shape=(j...  5.07 us
    pallas_call x1, Pallas kernels, raise_start(): pl.pallas_call(functools.partial(raise_start_kernel, count), name='raise_...  4.59 us
    pallas_call x2, Pallas kernels, sweep_once(): pl.pallas_call(functools.partial(sweep_once_kernel, start, count, rows, c...  3.6 us
    pallas_call x1, Pallas kernels, raise_rest(): pl.pallas_call(functools.partial(raise_rest_kernel, start), name='raise_r...  3.52 us
    pallas_call x2, Pallas kernels, faces(): pl.pallas_call(functools.partial(faces_kernel, start, rows, cols), out_sh...  1.62 us
    pallas_call x1, Pallas kernels, patch_y(): pl.pallas_call(functools.partial(patch_y_kernel, scale, lax.axis_size('gz...  1.56 us
  transfers between devices with their start and end apart: 9, of which 4 were waited for; matrix products, arithmetic and copies ran while one was open for 0% of the time, Pallas kernels for 20%

profile of v6, /device:TPU:0, one launch (start us, length us, event | category | flops | bytes accessed | tf_op | source)
XLA Modules:
  0.0 52.0 jit_solution(6429190754224526861)
XLA Ops:
  0.6 4.6 %raise_start.1 = (f32[66,200,128]{2,1,0:T(8,128)S(1)}, f32[32,1024]{1,0:T(8,128)S(1)}, s32[8,128]{1,0:T(8,128)S(1)}) custom-call(f32[64,16,1024]{2,1,0:T(8,128)} %dist.3, s32[64,16,1024]{2,1,0:T(8,128)} %par.3, s32[32,128]{1,0:T(8,128)} %bitcast.2, s32[64,16,1024]{2,1,0:T(8,128)} %occ.3), custom_call_target="tpu_custom_call" | custom-call | bytes 8388608 | tf_op jit(solution)/shard_map/raise_start/pallas_call | solution.py:255
  5.2 0.4 shard_map.64
  5.7 3.5 %raise_rest.1 = (f32[66,200,128]{2,1,0:T(8,128)S(1)}, f32[40,1024]{1,0:T(8,128)S(1)}, f32[40,1024]{1,0:T(8,128)S(1)}, f32[8,1024]{1,0:T(8,128)S(1)}) custom-call(f32[64,16,1024]{2,1,0:T(8,128)} %dist.3, s32[64,16,1024]{2,1,0:T(8,128)} %par.3, s32[32,128]{1,0:T(8,128)} %bitcast.3, s32[64,16,1024]{2,1,0:T(8,128)} %occ.3, ...), custom_call_target="tpu_custom_call", output_to_operand_aliasing={{0}: (6, {})} | custom-call | bytes 8388608 | tf_op jit(solution)/shard_map/raise_rest/pallas_call | solution.py:275
  9.2 4.1 %collective-permute-start = (f32[8,1024]{1,0:T(8,128)S(1)}, f32[8,1024]{1,0:T(8,128)S(1)}, u32[]{:S(2)}, u32[]{:S(2)}) collective-permute-start(f32[8,1024]{1,0:T(8,128)S(1)} %get-tuple-element.60), channel_id=1, source_target_pairs={{0,4},{1,5},{2,6},{3,7},{4,0},{5,1},{6,2},{7,3},{8,12},{9,13},{10,... | collective-permute-start | bytes 98312 | tf_op jit(solution)/shard_map/ppermute | solution.py:534
  13.3 1.8 %shard_map.59.once = f32[34,200,128]{2,1,0:T(8,128)S(1)} custom-call(f32[66,200,128]{2,1,0:T(8,128)S(1)} %get-tuple-element.61.field), custom_call_target="tpu_custom_call" | custom-call | bytes 8388608 | tf_op jit(solution)/shard_map/pallas_call | solution.py:319
  15.1 0.4 collective-permute-done
  15.6 1.6 %collective-permute-start.1 = (f32[8,1024]{1,0:T(8,128)S(1)}, f32[8,1024]{1,0:T(8,128)S(1)}, u32[]{:S(2)}, u32[]{:S(2)}) collective-permute-start(f32[8,1024]{1,0:T(8,128)S(1)} %add.13), channel_id=1, source_target_pairs={{0,2},{1,3},{2,0},{3,1},{4,6},{5,7},{6,4},{7,5},{8,10},{9,11},{10,... | collective-permute-start | bytes 98312 | tf_op jit(solution)/shard_map/ppermute | solution.py:534
  17.1 1.2 %shard_map.61 = (f32[2,32,1024]{2,1,0:T(8,128)S(1)}, f32[2,64,1024]{2,1,0:T(8,128)S(1)}) custom-call(f32[66,200,128]{2,1,0:T(8,128)S(1)} %get-tuple-element.61.field), custom_call_target="tpu_custom_call" | custom-call | bytes 2097152 | tf_op jit(solution)/shard_map/pallas_call | solution.py:142
  18.3 1.8 %shard_map.60.once = f32[34,200,128]{2,1,0:T(8,128)S(1)} custom-call(f32[66,200,128]{2,1,0:T(8,128)S(1)} %get-tuple-element.61.field), custom_call_target="tpu_custom_call" | custom-call | bytes 8388608 | tf_op jit(solution)/shard_map/pallas_call | solution.py:319
  20.1 0.0 collective-permute-done.1
  20.2 0.1 collective-permute-start.2
  20.3 4.1 %collective-permute-start.6 = (f32[2,64,1024]{2,1,0:T(8,128)S(1)}, f32[2,64,1024]{2,1,0:T(8,128)S(1)}, u32[]{:S(2)}, u32[]{:S(2)}) collective-permute-start(f32[2,64,1024]{2,1,0:T(8,128)S(1)} %get-tuple-element.79), channel_id=1, source_target_pairs={{0,7},{1,2},{2,1},{3,4},{4,3},{5,6},{6,5},{7,0},{8,15},{9,10},{10,... | collective-permute-start | bytes 1572872 | tf_op jit(solution)/shard_map/ppermute | solution.py:534
  24.4 0.0 collective-permute-start.4
  24.4 2.0 %collective-permute-start.5 = (f32[2,32,1024]{2,1,0:T(8,128)S(1)}, f32[2,32,1024]{2,1,0:T(8,128)S(1)}, u32[]{:S(2)}, u32[]{:S(2)}) collective-permute-start(f32[2,32,1024]{2,1,0:T(8,128)S(1)} %get-tuple-element.78), channel_id=1, source_target_pairs={{0,1},{1,0},{2,3},{3,2},{4,5},{5,4},{6,7},{7,6},{8,9},{9,8},{10,11... | collective-permute-start | bytes 786440 | tf_op jit(solution)/shard_map/ppermute | solution.py:534
  26.4 2.5 %shard_map.62 = (f32[64,16,1024]{2,1,0:T(8,128)}, f32[4096,128]{1,0:T(8,128)S(1)}) custom-call(f32[34,200,128]{2,1,0:T(8,128)S(1)} %shard_map.59.once), custom_call_target="tpu_custom_call" | custom-call | bytes 8388608 | tf_op jit(solution)/shard_map/pallas_call | solution.py:368
  29.0 0.0 collective-permute-done.2.first
  29.0 0.8 %collective-permute-start.3 = (f32[40,1024]{1,0:T(8,128)S(1)}, f32[40,1024]{1,0:T(8,128)S(1)}, u32[]{:S(2)}, u32[]{:S(2)}) collective-permute-start(f32[40,1024]{1,0:T(8,128)S(1)} %get-tuple-element.86), channel_id=1, source_target_pairs={{0,8},{8,0},{16,24},{24,16},{1,9},{9,1},{17,25},{25,17},{2,10},{10... | collective-permute-start | bytes 491528 | tf_op jit(solution)/shard_map/ppermute | solution.py:534
  29.7 2.5 %shard_map.63 = (f32[64,16,1024]{2,1,0:T(8,128)}, f32[4096,128]{1,0:T(8,128)S(1)}) custom-call(f32[34,200,128]{2,1,0:T(8,128)S(1)} %shard_map.60.once, f32[64,16,1024]{2,1,0:T(8,128)} %get-tuple-element.71.refs_0_), custom_call_target="tpu_custom_call", output_to_operand_aliasing={{0}: (1, {})} | custom-call | bytes 8388608 | tf_op jit(solution)/shard_map/pallas_call | solution.py:368
  32.3 0.0 collective-permute-done.3.second
  32.3 0.4 collective-permute-start.7
  32.7 4.4 %collective-permute-start.8 = (f32[8,1024]{1,0:T(8,128)S(1)}, f32[8,1024]{1,0:T(8,128)S(1)}, u32[]{:S(2)}, u32[]{:S(2)}) collective-permute-start(f32[8,1024]{1,0:T(8,128)S(1)} %get-tuple-element.81), channel_id=1, source_target_pairs={{0,7},{1,0},{2,1},{3,2},{4,3},{5,4},{6,5},{7,6},{8,15},{9,8},{10,9... | collective-permute-start | bytes 98312 | tf_op jit(solution)/shard_map/ppermute | solution.py:534
  37.1 0.8 %patch_z.1 = (f32[64,16,1024]{2,1,0:T(8,128)}, f32[4,64,1024]{2,1,0:T(8,128)S(1)}) custom-call(f32[40,1024]{1,0:T(8,128)S(1)} %collective-permute-done.2.first, f32[40,1024]{1,0:T(8,128)S(1)} %collective-permute-done.3.second, f32[4096,128]{1,0:T(8,128)S(1)} %get-tuple-element.74.slab_low, ...), custom_call_target="tpu_custom_call", output_to_operand_aliasing={{0}: (4, {})} | custom-call | bytes 1048576 | tf_op jit(solution)/shard_map/patch_z/pallas_call | solution.py:456
  37.9 6.2 %collective-permute-done.4.near0 = f32[2,32,1024]{2,1,0:T(8,128)S(1)} collective-permute-done((f32[2,32,1024]{2,1,0:T(8,128)S(1)}, f32[2,32,1024]{2,1,0:T(8,128)S(1)}, u32[]{:S(2)}, u32[]{:S(2)}) %collective-permute-start.4) | collective-permute-done | bytes 262176 | tf_op jit(solution)/shard_map/ppermute | solution.py:534
  44.1 5.6 %collective-permute-done.5.near1 = f32[2,32,1024]{2,1,0:T(8,128)S(1)} collective-permute-done((f32[2,32,1024]{2,1,0:T(8,128)S(1)}, f32[2,32,1024]{2,1,0:T(8,128)S(1)}, u32[]{:S(2)}, u32[]{:S(2)}) %collective-permute-start.5) | collective-permute-done | bytes 262176 | tf_op jit(solution)/shard_map/ppermute | solution.py:534
  49.7 0.0 collective-permute-done.7.clow
  49.7 0.7 %collective-permute-done.8.chigh = f32[8,1024]{1,0:T(8,128)S(1)} collective-permute-done((f32[8,1024]{1,0:T(8,128)S(1)}, f32[8,1024]{1,0:T(8,128)S(1)}, u32[]{:S(2)}, u32[]{:S(2)}) %collective-permute-start.8) | collective-permute-done | bytes 32800 | tf_op jit(solution)/shard_map/ppermute | solution.py:534
  50.4 0.0 collective-permute-done.6.far
  50.4 1.6 %patch_y.1 = (f32[64,16,1024]{2,1,0:T(8,128)}, f32[1,1]{1,0:T(1,128)}) custom-call(f32[4,64,1024]{2,1,0:T(8,128)S(1)} %get-tuple-element.77.edges, f32[2,32,1024]{2,1,0:T(8,128)S(1)} %collective-permute-done.4.near0, f32[2,32,1024]{2,1,0:T(8,128)S(1)} %collective-permute-done.5.near1, ...), custom_call_target="tpu_custom_call", output_to_operand_aliasing={{0}: (7, {})} | custom-call | bytes 2097152 | tf_op jit(solution)/shard_map/patch_y/pallas_call | solution.py:516
  (6 shorter events, 0.0 us)
Async XLA Ops:
  9.2 6.4 %collective-permute-start = (f32[8,1024]{1,0:T(8,128)S(1)}, f32[8,1024]{1,0:T(8,128)S(1)}, u32[]{:S(2)}, u32[]{:S(2)}) collective-permute-start(f32[8,1024]{1,0:T(8,128)S(1)} %get-tuple-element.60), channel_id=1, source_target_pairs={{0,4},{1,5},{2,6},{3,7},{4,0},{5,1},{6,2},{7,3},{8,12},{9,13},{10,... | collective-permute-start | bytes 98312 | tf_op jit(solution)/shard_map/ppermute | solution.py:534
  15.6 4.6 %collective-permute-start.1 = (f32[8,1024]{1,0:T(8,128)S(1)}, f32[8,1024]{1,0:T(8,128)S(1)}, u32[]{:S(2)}, u32[]{:S(2)}) collective-permute-start(f32[8,1024]{1,0:T(8,128)S(1)} %add.13), channel_id=1, source_target_pairs={{0,2},{1,3},{2,0},{3,1},{4,6},{5,7},{6,4},{7,5},{8,10},{9,11},{10,... | collective-permute-start | bytes 98312 | tf_op jit(solution)/shard_map/ppermute | solution.py:534
  20.2 8.8 %collective-permute-start.2 = (f32[40,1024]{1,0:T(8,128)S(1)}, f32[40,1024]{1,0:T(8,128)S(1)}, u32[]{:S(2)}, u32[]{:S(2)}) collective-permute-start(f32[40,1024]{1,0:T(8,128)S(1)} %constant_dynamic-update-slice_fusion.1), channel_id=1, source_target_pairs={{0,24},{8,16},{16,8},{24,0},{1,25},{9,17},{17,9},{25,1},{2,26},{10... | collective-permute-start | bytes 491528 | tf_op jit(solution)/shard_map/ppermute | solution.py:534
  20.3 30.2 %collective-permute-start.6 = (f32[2,64,1024]{2,1,0:T(8,128)S(1)}, f32[2,64,1024]{2,1,0:T(8,128)S(1)}, u32[]{:S(2)}, u32[]{:S(2)}) collective-permute-start(f32[2,64,1024]{2,1,0:T(8,128)S(1)} %get-tuple-element.79), channel_id=1, source_target_pairs={{0,7},{1,2},{2,1},{3,4},{4,3},{5,6},{6,5},{7,0},{8,15},{9,10},{10,... | collective-permute-start | bytes 1572872 | tf_op jit(solution)/shard_map/ppermute | solution.py:534
  24.4 19.7 %collective-permute-start.4 = (f32[2,32,1024]{2,1,0:T(8,128)S(1)}, f32[2,32,1024]{2,1,0:T(8,128)S(1)}, u32[]{:S(2)}, u32[]{:S(2)}) collective-permute-start(f32[2,32,1024]{2,1,0:T(8,128)S(1)} %shard_map.64), channel_id=1, source_target_pairs={{0,1},{1,0},{2,3},{3,2},{4,5},{5,4},{6,7},{7,6},{8,9},{9,8},{10,11... | collective-permute-start | bytes 786440 | tf_op jit(solution)/shard_map/ppermute | solution.py:534
  24.4 25.3 %collective-permute-start.5 = (f32[2,32,1024]{2,1,0:T(8,128)S(1)}, f32[2,32,1024]{2,1,0:T(8,128)S(1)}, u32[]{:S(2)}, u32[]{:S(2)}) collective-permute-start(f32[2,32,1024]{2,1,0:T(8,128)S(1)} %get-tuple-element.78), channel_id=1, source_target_pairs={{0,1},{1,0},{2,3},{3,2},{4,5},{5,4},{6,7},{7,6},{8,9},{9,8},{10,11... | collective-permute-start | bytes 786440 | tf_op jit(solution)/shard_map/ppermute | solution.py:534
  29.0 3.3 %collective-permute-start.3 = (f32[40,1024]{1,0:T(8,128)S(1)}, f32[40,1024]{1,0:T(8,128)S(1)}, u32[]{:S(2)}, u32[]{:S(2)}) collective-permute-start(f32[40,1024]{1,0:T(8,128)S(1)} %get-tuple-element.86), channel_id=1, source_target_pairs={{0,8},{8,0},{16,24},{24,16},{1,9},{9,1},{17,25},{25,17},{2,10},{10... | collective-permute-start | bytes 491528 | tf_op jit(solution)/shard_map/ppermute | solution.py:534
  32.3 17.4 %collective-permute-start.7 = (f32[8,1024]{1,0:T(8,128)S(1)}, f32[8,1024]{1,0:T(8,128)S(1)}, u32[]{:S(2)}, u32[]{:S(2)}) collective-permute-start(f32[8,1024]{1,0:T(8,128)S(1)} %get-tuple-element.80), channel_id=1, source_target_pairs={{0,1},{1,2},{2,3},{3,4},{4,5},{5,6},{6,7},{7,0},{8,9},{9,10},{10,1... | collective-permute-start | bytes 98312 | tf_op jit(solution)/shard_map/ppermute | solution.py:534
  32.7 17.7 %collective-permute-start.8 = (f32[8,1024]{1,0:T(8,128)S(1)}, f32[8,1024]{1,0:T(8,128)S(1)}, u32[]{:S(2)}, u32[]{:S(2)}) collective-permute-start(f32[8,1024]{1,0:T(8,128)S(1)} %get-tuple-element.81), channel_id=1, source_target_pairs={{0,7},{1,0},{2,1},{3,2},{4,3},{5,4},{6,5},{7,6},{8,15},{9,8},{10,9... | collective-permute-start | bytes 98312 | tf_op jit(solution)/shard_map/ppermute | solution.py:534

commit v7 on v6

--- a/solution.py
+++ b/solution.py
@@ -472,50 +472,105 @@
     )(first, second, slab_low, slab_high, out)
 
 
-def patch_y_kernel(scale, slabs, edges, near0, near1, far, clow, chigh, counts, _, out, share, buf, sem):
+def merge_rows(away, edges, faces, corner, missing, buf):
+    z = 0
+    for face, first in faces:
+        planes = pl.ds(z, buf.shape[0] // len(faces))
+        reach = face[1 - away, pl.ds(first, planes.size), :] + VOXEL
+        if away:
+            reach = reach + VOXEL
+        buf[planes, :] = jnp.minimum(edges[planes, :], reach)
+        z += planes.size
+    if corner is not None:
+        for end, z in enumerate((0, buf.shape[0] - 1)):
+            offer = jnp.where(missing[end], FAR, corner[pl.ds(end, 1), :])
+            line = pl.ds(z, 1)
+            buf[line, :] = jnp.minimum(buf[line, :], offer + VOXEL + VOXEL)
+
+
+def sides(rows):
+    return (((0, 0), (1, 1)), ((rows - 1, 3), (rows - 2, 2)))
+
+
+def patch_near_kernel(edges, near0, near1, _, out, buf, sem):
+    odd = lax.axis_index("gy") & 1
+    for side, places in enumerate(sides(out.shape[1])):
+
+        @pl.when(odd == 1 - side)
+        def _():
+            copies = []
+            for away, (row, edge) in enumerate(places):
+                faces = ((near0, 0), (near1, 0))
+                merge_rows(away, edges.at[edge], faces, None, None, buf.at[away])
+                cp = pltpu.make_async_copy(buf.at[away], out.at[:, row, :], sem.at[away])
+                cp.start()
+                copies.append(cp)
+            for cp in copies:
+                cp.wait()
+
+
+def patch_far_kernel(
+    scale, slabs, edges, near0, near1, far, clow, chigh, counts, _, out, share, buf, lines, sem
+):
     depth, rows, _ = out.shape
+    odd = lax.axis_index("gy") & 1
     slab = lax.axis_index("gz")
-    copies = []
-    odd = (lax.axis_index("gy") & 1) == 1
-    for side, corner in enumerate((clow, chigh)):
-        for away in range(2):
-            edge = (away, 3 - away)[side]
-            row = (away, rows - 1 - away)[side]
-            at = 2 * side + away
-            z = 0
-            for face in (near0, near1):
-                planes = pl.ds(z, face.shape[1])
-                ours, theirs = face[1 - away], far[1 - away, planes, :]
-                is_near = odd if side == 0 else jnp.logical_not(odd)
-                reach = jnp.where(is_near, ours, theirs) + VOXEL
-                if away:
-                    reach = reach + VOXEL
-                buf[at, planes, :] = jnp.minimum(edges[edge, planes, :], reach)
-                z += face.shape[1]
-            if not away:
-                for end, z in enumerate((0, depth - 1)):
-                    missing = slab == (0, slabs - 1)[end]
-                    offer = jnp.where(missing, FAR, corner[pl.ds(end, 1), :])
-                    line = jnp.minimum(buf[at, pl.ds(z, 1), :], offer + VOXEL + VOXEL)
-                    buf[at, pl.ds(z, 1), :] = line
-            cp = pltpu.make_async_copy(buf.at[at], out.at[:, row, :], sem.at[at])
-            cp.start()
-            copies.append(cp)
+    missing = (slab == 0, slab == slabs - 1)
+    corners = (clow, chigh)
+    for side, places in enumerate(sides(rows)):
+
+        @pl.when(odd == side)
+        def _():
+            copies = []
+            for away, (row, edge) in enumerate(places):
+                corner = None if away else corners[side]
+                faces = ((far, 0), (far, depth // 2))
+                merge_rows(away, edges.at[edge], faces, corner, missing, buf.at[away])
+                cp = pltpu.make_async_copy(buf.at[away], out.at[:, row, :], sem.at[away])
+                cp.start()
+                copies.append(cp)
+            row, edge = sides(rows)[1 - side][0]
+            for end, face in enumerate((near0, near1)):
+                z, line = ((0, 0), (depth - 1, face.shape[1] - 1))[end]
+                reach = jnp.minimum(edges[edge, pl.ds(z, 1), :], face[1, pl.ds(line, 1), :] + VOXEL)
+                offer = jnp.where(missing[end], FAR, corners[1 - side][pl.ds(end, 1), :])
+                lines[end] = jnp.minimum(reach, offer + VOXEL + VOXEL)
+                cp = pltpu.make_async_copy(
+                    lines.at[end], out.at[pl.ds(z, 1), row, :], sem.at[2 + end]
+                )
+                cp.start()
+                copies.append(cp)
+            for cp in copies:
+                cp.wait()
+
     x = pl.ds(0, LANES)
     both = (counts[:, x] + clow[:, x]).astype(jnp.int32)
     row = lax.broadcasted_iota(jnp.int32, both.shape, 0)
     both = jnp.where(row == 2, both, jnp.where(row == 3, both << COUNT_BITS, 0))
     count = jnp.sum(both, axis=0, keepdims=True)
     share[...] = count[:, :1].astype(jnp.float32) * jnp.float32(scale)
-    for cp in copies:
-        cp.wait()
-
-
-def patch_y(scale, edges, near0, near1, far, clow, chigh, counts, out):
+
+
+def patch_near(edges, near0, near1, out):
     depth, _, cols = out.shape
     return pl.pallas_call(
-        functools.partial(patch_y_kernel, scale, lax.axis_size("gz")),
-        name="patch_y",
+        patch_near_kernel,
+        name="patch_near",
+        out_shape=jax.ShapeDtypeStruct(out.shape, out.dtype),
+        in_specs=[VMEM] * 3 + [HBM],
+        out_specs=HBM,
+        input_output_aliases={3: 0},
+        scratch_shapes=[pltpu.VMEM((2, depth, cols), jnp.float32), pltpu.SemaphoreType.DMA((2,))],
+        compiler_params=params(4),
+        cost_estimate=cost(1),
+    )(edges, near0, near1, out)
+
+
+def patch_far(scale, edges, near0, near1, far, clow, chigh, counts, out):
+    depth, _, cols = out.shape
+    return pl.pallas_call(
+        functools.partial(patch_far_kernel, scale, lax.axis_size("gz")),
+        name="patch_far",
         out_shape=(
             jax.ShapeDtypeStruct(out.shape, out.dtype),
             jax.ShapeDtypeStruct((1, 1), jnp.float32),
@@ -523,9 +578,13 @@
         in_specs=[VMEM] * 7 + [HBM],
         out_specs=(HBM, VMEM),
         input_output_aliases={7: 0},
-        scratch_shapes=[pltpu.VMEM((4, depth, cols), jnp.float32), pltpu.SemaphoreType.DMA((4,))],
-        compiler_params=params(8),
-        cost_estimate=cost(2),
+        scratch_shapes=[
+            pltpu.VMEM((2, depth, cols), jnp.float32),
+            pltpu.VMEM((2, 1, cols), jnp.float32),
+            pltpu.SemaphoreType.DMA((4,)),
+        ],
+        compiler_params=params(4),
+        cost_estimate=cost(1),
     )(edges, near0, near1, far, clow, chigh, counts, out)
 
 
@@ -557,22 +616,19 @@
     face1, face = faces(field, half, depth - half, rows, cols, True)
     near1 = swapped(face1, "gy", lambda i: i ^ 1)
     once0 = sweep_once(field, 0, half, rows, cols)
-    once1 = sweep_once(field, half, half, rows, cols)
 
     mask = columns // 2
     while mask > 1:
         got = swapped(counts, "gy", lambda i: i ^ mask)
-        if mask == 4:
+        if mask == 2:
             got, once0 = tied((got, once0))
-        if mask == 2:
-            got, once1 = tied((got, once1))
         counts = counts + got
         mask //= 2
-    counts, face = tied((counts, face))
     far = swapped(face, "gy", lambda i: i - 1 + 2 * (i % 2))
 
     first = first.at[2 * rows :].set(counts)
     got_first = swapped(first, "gz", lambda i: i - 1 + 2 * (i % 2))
+    once1 = sweep_once(field, half, half, rows, cols)
     lowered, half0 = sweep_again(once0, None, 0, depth, rows, cols)
     got_first, half0 = tied((got_first, half0))
     counts = counts + got_first[2 * rows :]
@@ -585,7 +641,8 @@
     from_high = shifted(clow, "gy", -1)
     lowered, edges = patch_z(got_first, got_second, half0, half1, lowered)
     total = distance.size * slabs * columns
-    lowered, share = patch_y(
+    lowered = patch_near(edges, near0, near1, lowered)
+    lowered, share = patch_far(
         100.0 / total, edges, near0, near1, far, from_low, from_high, counts, lowered
     )
     return (lowered, share[0, 0])

time: 52.2 us -> 52.8 us (1.011)
  waiting for transfers between devices: 13 us -> 12.2 us
  Pallas kernels: 20.7 us -> 21.4 us
  starting transfers between devices: 17.5 us -> 18.2 us
    ppermute x9, waiting for transfers between devices: 13 us -> 12.2 us  [swapped(): lax.ppermute(value, axis, [(i, partner(i) % count) for i in range(count)])]
    ppermute x9, starting transfers between devices: 17.5 us -> 18.2 us  [swapped(): lax.ppermute(value, axis, [(i, partner(i) % count) for i in range(count)])]
    pallas_call x1 -> x2, Pallas kernels: 1.56 us -> 2.26 us  [the longest x1 1.41 us: patch_far(): pl.pallas_call(functools.partial(patch_far_kernel, scale, lax.axis_size('...]
  transfers between devices with their start and end apart: 9 -> 9, of which waited for: 4 -> 4; matrix products, arithmetic and copies ran while one was open for 0% -> 0% of each run, Pallas kernels for 20% -> 22%
where the time goes in v7:
time: 52.8 us; the launch traced here: 52.6 us
  Pallas kernels  21.4 us (41%)
  starting transfers between devices  18.2 us (34%)
  waiting for transfers between devices  12.2 us (23%)
  between operations  0.79 us (1%)
    ppermute x9, starting transfers between devices, swapped(): lax.ppermute(value, axis, [(i, partner(i) % count) for i in range(count)])  18.2 us
    ppermute x9, waiting for transfers between devices, swapped(): lax.ppermute(value, axis, [(i, partner(i) % count) for i in range(count)])  12.2 us
    pallas_call x2, Pallas kernels, sweep_again(): pl.pallas_call(functools.partial(sweep_again_kernel, start), out_shape=(j...  5.07 us
    pallas_call x1, Pallas kernels, raise_start(): pl.pallas_call(functools.partial(raise_start_kernel, count), name='raise_...  4.59 us
    pallas_call x2, Pallas kernels, sweep_once(): pl.pallas_call(functools.partial(sweep_once_kernel, start, count, rows, c...  3.6 us
    pallas_call x1, Pallas kernels, raise_rest(): pl.pallas_call(functools.partial(raise_rest_kernel, start), name='raise_r...  3.52 us
    pallas_call x2, Pallas kernels, faces(): pl.pallas_call(functools.partial(faces_kernel, start, rows, cols), out_sh...  1.63 us
    pallas_call x1, Pallas kernels, patch_far(): pl.pallas_call(functools.partial(patch_far_kernel, scale, lax.axis_size('...  1.41 us
  transfers between devices with their start and end apart: 9, of which 4 were waited for; matrix products, arithmetic and copies ran while one was open for 0% of the time, Pallas kernels for 22%

profile of v7, /device:TPU:0, one launch (start us, length us, event | category | flops | bytes accessed | tf_op | source)
XLA Modules:
  0.0 52.6 jit_solution(11529694341360436475)
XLA Ops:
  0.6 4.6 %raise_start.1 = (f32[66,200,128]{2,1,0:T(8,128)S(1)}, f32[32,1024]{1,0:T(8,128)S(1)}, s32[8,128]{1,0:T(8,128)S(1)}) custom-call(f32[64,16,1024]{2,1,0:T(8,128)} %dist.3, s32[64,16,1024]{2,1,0:T(8,128)} %par.3, s32[32,128]{1,0:T(8,128)} %bitcast.2, s32[64,16,1024]{2,1,0:T(8,128)} %occ.3), custom_call_target="tpu_custom_call" | custom-call | bytes 8388608 | tf_op jit(solution)/shard_map/raise_start/pallas_call | solution.py:255
  5.2 0.4 shard_map.63
  5.7 3.5 %raise_rest.1 = (f32[66,200,128]{2,1,0:T(8,128)S(1)}, f32[40,1024]{1,0:T(8,128)S(1)}, f32[40,1024]{1,0:T(8,128)S(1)}, f32[8,1024]{1,0:T(8,128)S(1)}) custom-call(f32[64,16,1024]{2,1,0:T(8,128)} %dist.3, s32[64,16,1024]{2,1,0:T(8,128)} %par.3, s32[32,128]{1,0:T(8,128)} %bitcast.3, s32[64,16,1024]{2,1,0:T(8,128)} %occ.3, ...), custom_call_target="tpu_custom_call", output_to_operand_aliasing={{0}: (6, {})} | custom-call | bytes 8388608 | tf_op jit(solution)/shard_map/raise_rest/pallas_call | solution.py:275
  9.2 4.1 %collective-permute-start = (f32[8,1024]{1,0:T(8,128)S(1)}, f32[8,1024]{1,0:T(8,128)S(1)}, u32[]{:S(2)}, u32[]{:S(2)}) collective-permute-start(f32[8,1024]{1,0:T(8,128)S(1)} %get-tuple-element.56), channel_id=1, source_target_pairs={{0,4},{1,5},{2,6},{3,7},{4,0},{5,1},{6,2},{7,3},{8,12},{9,13},{10,... | collective-permute-start | bytes 98312 | tf_op jit(solution)/shard_map/ppermute | solution.py:593
  13.3 2.2 %collective-permute-done = f32[8,1024]{1,0:T(8,128)S(1)} collective-permute-done((f32[8,1024]{1,0:T(8,128)S(1)}, f32[8,1024]{1,0:T(8,128)S(1)}, u32[]{:S(2)}, u32[]{:S(2)}) %collective-permute-start) | collective-permute-done | bytes 32800 | tf_op jit(solution)/shard_map/ppermute | solution.py:593
  15.6 1.6 %collective-permute-start.1 = (f32[8,1024]{1,0:T(8,128)S(1)}, f32[8,1024]{1,0:T(8,128)S(1)}, u32[]{:S(2)}, u32[]{:S(2)}) collective-permute-start(f32[8,1024]{1,0:T(8,128)S(1)} %add.13), channel_id=1, source_target_pairs={{0,2},{1,3},{2,0},{3,1},{4,6},{5,7},{6,4},{7,5},{8,10},{9,11},{10,... | collective-permute-start | bytes 98312 | tf_op jit(solution)/shard_map/ppermute | solution.py:593
  17.1 1.8 %shard_map.59.once = f32[34,200,128]{2,1,0:T(8,128)S(1)} custom-call(f32[66,200,128]{2,1,0:T(8,128)S(1)} %get-tuple-element.57.field), custom_call_target="tpu_custom_call" | custom-call | bytes 8388608 | tf_op jit(solution)/shard_map/pallas_call | solution.py:319
  18.9 0.6 %collective-permute-done.1 = f32[8,1024]{1,0:T(8,128)S(1)} collective-permute-done((f32[8,1024]{1,0:T(8,128)S(1)}, f32[8,1024]{1,0:T(8,128)S(1)}, u32[]{:S(2)}, u32[]{:S(2)}) %collective-permute-start.1) | collective-permute-done | bytes 32800 | tf_op jit(solution)/shard_map/ppermute | solution.py:593
  19.5 0.1 collective-permute-start.2
  19.6 1.2 %shard_map.64 = (f32[2,32,1024]{2,1,0:T(8,128)S(1)}, f32[2,64,1024]{2,1,0:T(8,128)S(1)}) custom-call(f32[66,200,128]{2,1,0:T(8,128)S(1)} %get-tuple-element.57.field), custom_call_target="tpu_custom_call" | custom-call | bytes 2097152 | tf_op jit(solution)/shard_map/pallas_call | solution.py:142
  20.8 4.8 %collective-permute-start.6 = (f32[2,64,1024]{2,1,0:T(8,128)S(1)}, f32[2,64,1024]{2,1,0:T(8,128)S(1)}, u32[]{:S(2)}, u32[]{:S(2)}) collective-permute-start(f32[2,64,1024]{2,1,0:T(8,128)S(1)} %get-tuple-element.71), channel_id=1, source_target_pairs={{0,7},{1,2},{2,1},{3,4},{4,3},{5,6},{6,5},{7,0},{8,15},{9,10},{10,... | collective-permute-start | bytes 1572872 | tf_op jit(solution)/shard_map/ppermute | solution.py:593
  25.6 0.0 collective-permute-start.4
  25.6 2.0 %collective-permute-start.5 = (f32[2,32,1024]{2,1,0:T(8,128)S(1)}, f32[2,32,1024]{2,1,0:T(8,128)S(1)}, u32[]{:S(2)}, u32[]{:S(2)}) collective-permute-start(f32[2,32,1024]{2,1,0:T(8,128)S(1)} %get-tuple-element.70), channel_id=1, source_target_pairs={{0,1},{1,0},{2,3},{3,2},{4,5},{5,4},{6,7},{7,6},{8,9},{9,8},{10,11... | collective-permute-start | bytes 786440 | tf_op jit(solution)/shard_map/ppermute | solution.py:593
  27.7 2.5 %shard_map.60 = (f32[64,16,1024]{2,1,0:T(8,128)}, f32[4096,128]{1,0:T(8,128)S(1)}) custom-call(f32[34,200,128]{2,1,0:T(8,128)S(1)} %shard_map.59.once), custom_call_target="tpu_custom_call" | custom-call | bytes 8388608 | tf_op jit(solution)/shard_map/pallas_call | solution.py:368
  30.2 0.0 collective-permute-done.2.first
  30.2 0.8 %collective-permute-start.3 = (f32[40,1024]{1,0:T(8,128)S(1)}, f32[40,1024]{1,0:T(8,128)S(1)}, u32[]{:S(2)}, u32[]{:S(2)}) collective-permute-start(f32[40,1024]{1,0:T(8,128)S(1)} %get-tuple-element.78), channel_id=1, source_target_pairs={{0,8},{8,0},{16,24},{24,16},{1,9},{9,1},{17,25},{25,17},{2,10},{10... | collective-permute-start | bytes 491528 | tf_op jit(solution)/shard_map/ppermute | solution.py:593
  31.0 1.8 %shard_map.61.once = f32[34,200,128]{2,1,0:T(8,128)S(1)} custom-call(f32[66,200,128]{2,1,0:T(8,128)S(1)} %get-tuple-element.57.field), custom_call_target="tpu_custom_call" | custom-call | bytes 8388608 | tf_op jit(solution)/shard_map/pallas_call | solution.py:319
  32.8 2.5 %shard_map.62 = (f32[64,16,1024]{2,1,0:T(8,128)}, f32[4096,128]{1,0:T(8,128)S(1)}) custom-call(f32[34,200,128]{2,1,0:T(8,128)S(1)} %shard_map.61.once, f32[64,16,1024]{2,1,0:T(8,128)} %get-tuple-element.63.refs_0_), custom_call_target="tpu_custom_call", output_to_operand_aliasing={{0}: (1, {})} | custom-call | bytes 8388608 | tf_op jit(solution)/shard_map/pallas_call | solution.py:368
  35.4 0.0 collective-permute-done.3.second
  35.4 0.4 collective-permute-start.7
  35.8 4.4 %collective-permute-start.8 = (f32[8,1024]{1,0:T(8,128)S(1)}, f32[8,1024]{1,0:T(8,128)S(1)}, u32[]{:S(2)}, u32[]{:S(2)}) collective-permute-start(f32[8,1024]{1,0:T(8,128)S(1)} %get-tuple-element.73), channel_id=1, source_target_pairs={{0,7},{1,0},{2,1},{3,2},{4,3},{5,4},{6,5},{7,6},{8,15},{9,8},{10,9... | collective-permute-start | bytes 98312 | tf_op jit(solution)/shard_map/ppermute | solution.py:593
  40.2 0.8 %patch_z.1 = (f32[64,16,1024]{2,1,0:T(8,128)}, f32[4,64,1024]{2,1,0:T(8,128)S(1)}) custom-call(f32[40,1024]{1,0:T(8,128)S(1)} %collective-permute-done.2.first, f32[40,1024]{1,0:T(8,128)S(1)} %collective-permute-done.3.second, f32[4096,128]{1,0:T(8,128)S(1)} %get-tuple-element.66.slab_low, ...), custom_call_target="tpu_custom_call", output_to_operand_aliasing={{0}: (4, {})} | custom-call | bytes 1048576 | tf_op jit(solution)/shard_map/patch_z/pallas_call | solution.py:456
  41.0 3.7 %collective-permute-done.4.near0 = f32[2,32,1024]{2,1,0:T(8,128)S(1)} collective-permute-done((f32[2,32,1024]{2,1,0:T(8,128)S(1)}, f32[2,32,1024]{2,1,0:T(8,128)S(1)}, u32[]{:S(2)}, u32[]{:S(2)}) %collective-permute-start.4) | collective-permute-done | bytes 262176 | tf_op jit(solution)/shard_map/ppermute | solution.py:593
  44.7 5.6 %collective-permute-done.5.near1 = f32[2,32,1024]{2,1,0:T(8,128)S(1)} collective-permute-done((f32[2,32,1024]{2,1,0:T(8,128)S(1)}, f32[2,32,1024]{2,1,0:T(8,128)S(1)}, u32[]{:S(2)}, u32[]{:S(2)}) %collective-permute-start.5) | collective-permute-done | bytes 262176 | tf_op jit(solution)/shard_map/ppermute | solution.py:593
  50.3 0.8 %patch_near.1._ = f32[64,16,1024]{2,1,0:T(8,128)} custom-call(f32[4,64,1024]{2,1,0:T(8,128)S(1)} %get-tuple-element.69.edges, f32[2,32,1024]{2,1,0:T(8,128)S(1)} %collective-permute-done.4.near0, f32[2,32,1024]{2,1,0:T(8,128)S(1)} %collective-permute-done.5.near1, f32[64,16,1024]{2,1,0:T(8,128)} %get-tuple-element.75._), custom_call_target="tpu_custom_call", output_to_operand_aliasing={{}: (3, {})} | custom-call | bytes 1048576 | tf_op jit(solution)/shard_map/patch_near/pallas_call | solution.py:556
  51.2 0.0 collective-permute-done.7.clow
  51.2 0.0 collective-permute-done.8.chigh
  51.2 0.0 collective-permute-done.6.far
  51.2 1.4 %patch_far.1 = (f32[64,16,1024]{2,1,0:T(8,128)}, f32[1,1]{1,0:T(1,128)}) custom-call(f32[4,64,1024]{2,1,0:T(8,128)S(1)} %get-tuple-element.69.edges, f32[2,32,1024]{2,1,0:T(8,128)S(1)} %collective-permute-done.4.near0, f32[2,32,1024]{2,1,0:T(8,128)S(1)} %collective-permute-done.5.near1, ...), custom_call_target="tpu_custom_call", output_to_operand_aliasing={{0}: (7, {})} | custom-call | bytes 1048576 | tf_op jit(solution)/shard_map/patch_far/pallas_call | solution.py:571
  (5 shorter events, 0.0 us)
Async XLA Ops:
  9.2 6.4 %collective-permute-start = (f32[8,1024]{1,0:T(8,128)S(1)}, f32[8,1024]{1,0:T(8,128)S(1)}, u32[]{:S(2)}, u32[]{:S(2)}) collective-permute-start(f32[8,1024]{1,0:T(8,128)S(1)} %get-tuple-element.56), channel_id=1, source_target_pairs={{0,4},{1,5},{2,6},{3,7},{4,0},{5,1},{6,2},{7,3},{8,12},{9,13},{10,... | collective-permute-start | bytes 98312 | tf_op jit(solution)/shard_map/ppermute | solution.py:593
  15.6 3.9 %collective-permute-start.1 = (f32[8,1024]{1,0:T(8,128)S(1)}, f32[8,1024]{1,0:T(8,128)S(1)}, u32[]{:S(2)}, u32[]{:S(2)}) collective-permute-start(f32[8,1024]{1,0:T(8,128)S(1)} %add.13), channel_id=1, source_target_pairs={{0,2},{1,3},{2,0},{3,1},{4,6},{5,7},{6,4},{7,5},{8,10},{9,11},{10,... | collective-permute-start | bytes 98312 | tf_op jit(solution)/shard_map/ppermute | solution.py:593
  19.5 10.7 %collective-permute-start.2 = (f32[40,1024]{1,0:T(8,128)S(1)}, f32[40,1024]{1,0:T(8,128)S(1)}, u32[]{:S(2)}, u32[]{:S(2)}) collective-permute-start(f32[40,1024]{1,0:T(8,128)S(1)} %get-tuple-element.80), channel_id=1, source_target_pairs={{0,24},{8,16},{16,8},{24,0},{1,25},{9,17},{17,9},{25,1},{2,26},{10... | collective-permute-start | bytes 491528 | tf_op jit(solution)/shard_map/ppermute | solution.py:593
  20.8 30.4 %collective-permute-start.6 = (f32[2,64,1024]{2,1,0:T(8,128)S(1)}, f32[2,64,1024]{2,1,0:T(8,128)S(1)}, u32[]{:S(2)}, u32[]{:S(2)}) collective-permute-start(f32[2,64,1024]{2,1,0:T(8,128)S(1)} %get-tuple-element.71), channel_id=1, source_target_pairs={{0,7},{1,2},{2,1},{3,4},{4,3},{5,6},{6,5},{7,0},{8,15},{9,10},{10,... | collective-permute-start | bytes 1572872 | tf_op jit(solution)/shard_map/ppermute | solution.py:593
  25.6 19.1 %collective-permute-start.4 = (f32[2,32,1024]{2,1,0:T(8,128)S(1)}, f32[2,32,1024]{2,1,0:T(8,128)S(1)}, u32[]{:S(2)}, u32[]{:S(2)}) collective-permute-start(f32[2,32,1024]{2,1,0:T(8,128)S(1)} %shard_map.63), channel_id=1, source_target_pairs={{0,1},{1,0},{2,3},{3,2},{4,5},{5,4},{6,7},{7,6},{8,9},{9,8},{10,11... | collective-permute-start | bytes 786440 | tf_op jit(solution)/shard_map/ppermute | solution.py:593
  25.6 24.7 %collective-permute-start.5 = (f32[2,32,1024]{2,1,0:T(8,128)S(1)}, f32[2,32,1024]{2,1,0:T(8,128)S(1)}, u32[]{:S(2)}, u32[]{:S(2)}) collective-permute-start(f32[2,32,1024]{2,1,0:T(8,128)S(1)} %get-tuple-element.70), channel_id=1, source_target_pairs={{0,1},{1,0},{2,3},{3,2},{4,5},{5,4},{6,7},{7,6},{8,9},{9,8},{10,11... | collective-permute-start | bytes 786440 | tf_op jit(solution)/shard_map/ppermute | solution.py:593
  30.2 5.2 %collective-permute-start.3 = (f32[40,1024]{1,0:T(8,128)S(1)}, f32[40,1024]{1,0:T(8,128)S(1)}, u32[]{:S(2)}, u32[]{:S(2)}) collective-permute-start(f32[40,1024]{1,0:T(8,128)S(1)} %get-tuple-element.78), channel_id=1, source_target_pairs={{0,8},{8,0},{16,24},{24,16},{1,9},{9,1},{17,25},{25,17},{2,10},{10... | collective-permute-start | bytes 491528 | tf_op jit(solution)/shard_map/ppermute | solution.py:593
  35.4 15.8 %collective-permute-start.7 = (f32[8,1024]{1,0:T(8,128)S(1)}, f32[8,1024]{1,0:T(8,128)S(1)}, u32[]{:S(2)}, u32[]{:S(2)}) collective-permute-start(f32[8,1024]{1,0:T(8,128)S(1)} %get-tuple-element.72), channel_id=1, source_target_pairs={{0,1},{1,2},{2,3},{3,4},{4,5},{5,6},{6,7},{7,0},{8,9},{9,10},{10,1... | collective-permute-start | bytes 98312 | tf_op jit(solution)/shard_map/ppermute | solution.py:593
  35.8 15.4 %collective-permute-start.8 = (f32[8,1024]{1,0:T(8,128)S(1)}, f32[8,1024]{1,0:T(8,128)S(1)}, u32[]{:S(2)}, u32[]{:S(2)}) collective-permute-start(f32[8,1024]{1,0:T(8,128)S(1)} %get-tuple-element.73), channel_id=1, source_target_pairs={{0,7},{1,0},{2,1},{3,2},{4,3},{5,4},{6,5},{7,6},{8,15},{9,8},{10,9... | collective-permute-start | bytes 98312 | tf_op jit(solution)/shard_map/ppermute | solution.py:593

commit v8 on v7

--- a/solution.py
+++ b/solution.py
@@ -130,9 +130,9 @@
 
 def faces_kernel(start, rows, cols, field, near, *far):
     odd = (lax.axis_index("gy") & 1) == 1
-    write_faces(field, rows, cols, jnp.logical_not(odd), start, near)
+    write_faces(field, rows, cols, odd, start, near)
     for out in far:
-        write_faces(field, rows, cols, odd, 0, out)
+        write_faces(field, rows, cols, jnp.logical_not(odd), 0, out)
 
 
 def faces(field, start, count, rows, cols, both):
@@ -496,7 +496,7 @@
     odd = lax.axis_index("gy") & 1
     for side, places in enumerate(sides(out.shape[1])):
 
-        @pl.when(odd == 1 - side)
+        @pl.when(odd == side)
         def _():
             copies = []
             for away, (row, edge) in enumerate(places):
@@ -519,7 +519,7 @@
     corners = (clow, chigh)
     for side, places in enumerate(sides(rows)):
 
-        @pl.when(odd == side)
+        @pl.when(odd == 1 - side)
         def _():
             copies = []
             for away, (row, edge) in enumerate(places):
@@ -593,6 +593,10 @@
     return lax.ppermute(value, axis, [(i, partner(i) % count) for i in range(count)])
 
 
+def after_odd(i):
+    return i - 1 + 2 * (i % 2)
+
+
 def shifted(value, axis, by):
     return swapped(value, axis, lambda i: i + by)
 
@@ -609,34 +613,36 @@
     early = half + READ
     field, end, total = raise_start(distance, parent, flags, occupied, early)
     (face0,) = faces(field, 0, half, rows, cols, False)
-    near0 = swapped(face0, "gy", lambda i: i ^ 1)
+    near0 = swapped(face0, "gy", after_odd)
     field, first, second, counts = raise_rest(
         distance, parent, flags, occupied, end, total, field, early
     )
+
+    got_first = swapped(first, "gz", after_odd)
     face1, face = faces(field, half, depth - half, rows, cols, True)
-    near1 = swapped(face1, "gy", lambda i: i ^ 1)
+    near1 = swapped(face1, "gy", after_odd)
+    far = swapped(face, "gy", lambda i: i ^ 1)
     once0 = sweep_once(field, 0, half, rows, cols)
-
+    got_first, once0 = tied((got_first, once0))
+    second = second.at[2 * rows :].add(got_first[2 * rows :])
+    got_second = swapped(second, "gz", lambda i: i ^ 1)
+    once1 = sweep_once(field, half, half, rows, cols)
+    got_second, once1 = tied((got_second, once1))
+    counts = second[2 * rows :] + got_second[2 * rows :]
+    lowered, half0 = sweep_again(once0, None, 0, depth, rows, cols)
+    lowered, half1 = sweep_again(once1, lowered, half, depth, rows, cols)
+
+    more = jnp.zeros_like(counts)
     mask = columns // 2
     while mask > 1:
-        got = swapped(counts, "gy", lambda i: i ^ mask)
+        counts = counts + more
+        more = swapped(counts, "gy", lambda i: i ^ mask)
+        if mask == 4:
+            more, half0 = tied((more, half0))
         if mask == 2:
-            got, once0 = tied((got, once0))
-        counts = counts + got
+            more, half1 = tied((more, half1))
         mask //= 2
-    far = swapped(face, "gy", lambda i: i - 1 + 2 * (i % 2))
-
-    first = first.at[2 * rows :].set(counts)
-    got_first = swapped(first, "gz", lambda i: i - 1 + 2 * (i % 2))
-    once1 = sweep_once(field, half, half, rows, cols)
-    lowered, half0 = sweep_again(once0, None, 0, depth, rows, cols)
-    got_first, half0 = tied((got_first, half0))
-    counts = counts + got_first[2 * rows :]
-    second = second.at[2 * rows :].set(counts)
-    got_second = swapped(second, "gz", lambda i: i ^ 1)
-    lowered, half1 = sweep_again(once1, lowered, half, depth, rows, cols)
-    got_second, half1 = tied((got_second, half1))
-    clow, chigh, counts = corners(got_first, got_second, counts, got_second[2 * rows :])
+    clow, chigh, counts = corners(got_first, got_second, counts, more)
     from_low = shifted(chigh, "gy", 1)
     from_high = shifted(clow, "gy", -1)
     lowered, edges = patch_z(got_first, got_second, half0, half1, lowered)

time: 52.8 us -> 47.9 us (0.907)
  waiting for transfers between devices: 12.2 us -> 7.51 us
  starting transfers between devices: 18.2 us -> 17.4 us
  Pallas kernels: 21.4 us -> 22 us
    ppermute x9, waiting for transfers between devices: 12.2 us -> 7.51 us  [swapped(): lax.ppermute(value, axis, [(i, partner(i) % count) for i in range(count)])]
    ppermute x9, starting transfers between devices: 18.2 us -> 17.4 us  [swapped(): lax.ppermute(value, axis, [(i, partner(i) % count) for i in range(count)])]
    pallas_call x1, Pallas kernels: 3.52 us -> 4.13 us  [raise_rest(): pl.pallas_call(functools.partial(raise_rest_kernel, start), name='raise_r...]
  transfers between devices with their start and end apart: 9 -> 9, of which waited for: 4 -> 2; matrix products, arithmetic and copies ran while one was open for 0% -> 0% of each run, Pallas kernels for 22% -> 24%
where the time goes in v8:
time: 47.9 us; the launch traced here: 47.8 us
  Pallas kernels  22 us (46%)
  starting transfers between devices  17.4 us (36%)
  waiting for transfers between devices  7.51 us (16%)
  between operations  0.79 us (2%)
    ppermute x9, starting transfers between devices, swapped(): lax.ppermute(value, axis, [(i, partner(i) % count) for i in range(count)])  17.4 us
    ppermute x9, waiting for transfers between devices, swapped(): lax.ppermute(value, axis, [(i, partner(i) % count) for i in range(count)])  7.51 us
    pallas_call x2, Pallas kernels, sweep_again(): pl.pallas_call(functools.partial(sweep_again_kernel, start), out_shape=(j...  5.07 us
    pallas_call x1, Pallas kernels, raise_start(): pl.pallas_call(functools.partial(raise_start_kernel, count), name='raise_...  4.59 us
    pallas_call x1, Pallas kernels, raise_rest(): pl.pallas_call(functools.partial(raise_rest_kernel, start), name='raise_r...  4.13 us
    pallas_call x2, Pallas kernels, sweep_once(): pl.pallas_call(functools.partial(sweep_once_kernel, start, count, rows, c...  3.6 us
    pallas_call x2, Pallas kernels, faces(): pl.pallas_call(functools.partial(faces_kernel, start, rows, cols), out_sh...  1.62 us
    pallas_call x1, Pallas kernels, patch_far(): pl.pallas_call(functools.partial(patch_far_kernel, scale, lax.axis_size('...  1.4 us
  transfers between devices with their start and end apart: 9, of which 2 were waited for; matrix products, arithmetic and copies ran while one was open for 0% of the time, Pallas kernels for 24%

profile of v8, /device:TPU:0, one launch (start us, length us, event | category | flops | bytes accessed | tf_op | source)
XLA Modules:
  0.0 47.8 jit_solution(7397404329293981336)
XLA Ops:
  0.6 4.6 %raise_start.1 = (f32[66,200,128]{2,1,0:T(8,128)S(1)}, f32[32,1024]{1,0:T(8,128)S(1)}, s32[8,128]{1,0:T(8,128)S(1)}) custom-call(f32[64,16,1024]{2,1,0:T(8,128)} %dist.3, s32[64,16,1024]{2,1,0:T(8,128)} %par.3, s32[32,128]{1,0:T(8,128)} %bitcast.2, s32[64,16,1024]{2,1,0:T(8,128)} %occ.3), custom_call_target="tpu_custom_call" | custom-call | bytes 8388608 | tf_op jit(solution)/shard_map/raise_start/pallas_call | solution.py:255
  5.2 0.4 shard_map.63
  5.7 4.1 %raise_rest.1 = (f32[66,200,128]{2,1,0:T(8,128)S(1)}, f32[40,1024]{1,0:T(8,128)S(1)}, f32[40,1024]{1,0:T(8,128)S(1)}, f32[8,1024]{1,0:T(8,128)}) custom-call(f32[64,16,1024]{2,1,0:T(8,128)} %dist.3, s32[64,16,1024]{2,1,0:T(8,128)} %par.3, s32[32,128]{1,0:T(8,128)} %bitcast.3, s32[64,16,1024]{2,1,0:T(8,128)} %occ.3, ...), custom_call_target="tpu_custom_call", output_to_operand_aliasing={{0}: (6, {})} | custom-call | bytes 8388608 | tf_op jit(solution)/shard_map/raise_rest/pallas_call | solution.py:275
  9.8 2.5 %collective-permute-start = (f32[40,1024]{1,0:T(8,128)S(1)}, f32[40,1024]{1,0:T(8,128)S(1)}, u32[]{:S(2)}, u32[]{:S(2)}) collective-permute-start(f32[40,1024]{1,0:T(8,128)S(1)} %get-tuple-element.44), channel_id=1, source_target_pairs={{0,24},{8,16},{16,8},{24,0},{1,25},{9,17},{17,9},{25,1},{2,26},{10... | collective-permute-start | bytes 491528 | tf_op jit(solution)/shard_map/ppermute | solution.py:593
  12.3 1.2 %shard_map.64 = (f32[2,32,1024]{2,1,0:T(8,128)S(1)}, f32[2,64,1024]{2,1,0:T(8,128)S(1)}) custom-call(f32[66,200,128]{2,1,0:T(8,128)S(1)} %get-tuple-element.45.field), custom_call_target="tpu_custom_call" | custom-call | bytes 2097152 | tf_op jit(solution)/shard_map/pallas_call | solution.py:142
  13.5 1.6 %collective-permute-start.6 = (f32[2,64,1024]{2,1,0:T(8,128)S(1)}, f32[2,64,1024]{2,1,0:T(8,128)S(1)}, u32[]{:S(2)}, u32[]{:S(2)}) collective-permute-start(f32[2,64,1024]{2,1,0:T(8,128)S(1)} %get-tuple-element.60), channel_id=1, source_target_pairs={{0,1},{1,0},{2,3},{3,2},{4,5},{5,4},{6,7},{7,6},{8,9},{9,8},{10,11... | collective-permute-start | bytes 1572872 | tf_op jit(solution)/shard_map/ppermute | solution.py:593
  15.1 1.8 %shard_map.59.once = f32[34,200,128]{2,1,0:T(8,128)S(1)} custom-call(f32[66,200,128]{2,1,0:T(8,128)S(1)} %get-tuple-element.45.field), custom_call_target="tpu_custom_call" | custom-call | bytes 8388608 | tf_op jit(solution)/shard_map/pallas_call | solution.py:319
  16.9 0.0 collective-permute-done.first
  16.9 0.5 collective-permute-start.1
  17.4 5.1 %collective-permute-start.4 = (f32[2,32,1024]{2,1,0:T(8,128)S(1)}, f32[2,32,1024]{2,1,0:T(8,128)S(1)}, u32[]{:S(2)}, u32[]{:S(2)}) collective-permute-start(f32[2,32,1024]{2,1,0:T(8,128)S(1)} %shard_map.63), channel_id=1, source_target_pairs={{0,7},{1,2},{2,1},{3,4},{4,3},{5,6},{6,5},{7,0},{8,15},{9,10},{10,... | collective-permute-start | bytes 786440 | tf_op jit(solution)/shard_map/ppermute | solution.py:593
  22.5 0.0 collective-permute-start.5
  22.5 1.8 %shard_map.60.once = f32[34,200,128]{2,1,0:T(8,128)S(1)} custom-call(f32[66,200,128]{2,1,0:T(8,128)S(1)} %get-tuple-element.45.field), custom_call_target="tpu_custom_call" | custom-call | bytes 8388608 | tf_op jit(solution)/shard_map/pallas_call | solution.py:319
  24.3 0.0 collective-permute-done.1.second
  24.4 1.0 %collective-permute-start.2 = (f32[8,1024]{1,0:T(8,128)S(1)}, f32[8,1024]{1,0:T(8,128)S(1)}, u32[]{:S(2)}, u32[]{:S(2)}) collective-permute-start(f32[8,1024]{1,0:T(8,128)S(1)} %slice_add_fusion), channel_id=1, source_target_pairs={{0,4},{1,5},{2,6},{3,7},{4,0},{5,1},{6,2},{7,3},{8,12},{9,13},{10,... | collective-permute-start | bytes 98312 | tf_op jit(solution)/shard_map/ppermute | solution.py:593
  25.4 2.5 %shard_map.61 = (f32[64,16,1024]{2,1,0:T(8,128)}, f32[4096,128]{1,0:T(8,128)S(1)}) custom-call(f32[34,200,128]{2,1,0:T(8,128)S(1)} %shard_map.59.once), custom_call_target="tpu_custom_call" | custom-call | bytes 8388608 | tf_op jit(solution)/shard_map/pallas_call | solution.py:368
  27.9 7.3 %collective-permute-done.2 = f32[8,1024]{1,0:T(8,128)S(1)} collective-permute-done((f32[8,1024]{1,0:T(8,128)S(1)}, f32[8,1024]{1,0:T(8,128)S(1)}, u32[]{:S(2)}, u32[]{:S(2)}) %collective-permute-start.2) | collective-permute-done | bytes 32800 | tf_op jit(solution)/shard_map/ppermute | solution.py:593
  35.2 2.0 %collective-permute-start.3 = (f32[8,1024]{1,0:T(8,128)S(1)}, f32[8,1024]{1,0:T(8,128)S(1)}, u32[]{:S(2)}, u32[]{:S(2)}) collective-permute-start(f32[8,1024]{1,0:T(8,128)S(1)} %add.15.counts), channel_id=1, source_target_pairs={{0,2},{1,3},{2,0},{3,1},{4,6},{5,7},{6,4},{7,5},{8,10},{9,11},{10,... | collective-permute-start | bytes 98312 | tf_op jit(solution)/shard_map/ppermute | solution.py:593
  37.1 2.5 %shard_map.62 = (f32[64,16,1024]{2,1,0:T(8,128)}, f32[4096,128]{1,0:T(8,128)S(1)}) custom-call(f32[34,200,128]{2,1,0:T(8,128)S(1)} %shard_map.60.once, f32[64,16,1024]{2,1,0:T(8,128)} %get-tuple-element.54.refs_0_), custom_call_target="tpu_custom_call", output_to_operand_aliasing={{0}: (1, {})} | custom-call | bytes 8388608 | tf_op jit(solution)/shard_map/pallas_call | solution.py:368
  39.7 0.0 collective-permute-done.3.more
  39.7 1.2 %collective-permute-start.7 = (f32[8,1024]{1,0:T(8,128)S(1)}, f32[8,1024]{1,0:T(8,128)S(1)}, u32[]{:S(2)}, u32[]{:S(2)}) collective-permute-start(f32[8,1024]{1,0:T(8,128)S(1)} %get-tuple-element.62), channel_id=1, source_target_pairs={{0,1},{1,2},{2,3},{3,4},{4,5},{5,6},{6,7},{7,0},{8,9},{9,10},{10,1... | collective-permute-start | bytes 98312 | tf_op jit(solution)/shard_map/ppermute | solution.py:593
  40.9 3.6 %collective-permute-start.8 = (f32[8,1024]{1,0:T(8,128)S(1)}, f32[8,1024]{1,0:T(8,128)S(1)}, u32[]{:S(2)}, u32[]{:S(2)}) collective-permute-start(f32[8,1024]{1,0:T(8,128)S(1)} %get-tuple-element.63), channel_id=1, source_target_pairs={{0,7},{1,0},{2,1},{3,2},{4,3},{5,4},{6,5},{7,6},{8,15},{9,8},{10,9... | collective-permute-start | bytes 98312 | tf_op jit(solution)/shard_map/ppermute | solution.py:593
  44.5 0.8 %patch_z.1 = (f32[64,16,1024]{2,1,0:T(8,128)}, f32[4,64,1024]{2,1,0:T(8,128)S(1)}) custom-call(f32[40,1024]{1,0:T(8,128)S(1)} %collective-permute-done.first, f32[40,1024]{1,0:T(8,128)S(1)} %collective-permute-done.1.second, f32[4096,128]{1,0:T(8,128)S(1)} %get-tuple-element.51.slab_low, ...), custom_call_target="tpu_custom_call", output_to_operand_aliasing={{0}: (4, {})} | custom-call | bytes 1048576 | tf_op jit(solution)/shard_map/patch_z/pallas_call | solution.py:456
  45.2 0.0 collective-permute-done.4.near0
  45.2 0.0 collective-permute-done.5.near1
  45.3 0.9 %patch_near.1._ = f32[64,16,1024]{2,1,0:T(8,128)} custom-call(f32[4,64,1024]{2,1,0:T(8,128)S(1)} %get-tuple-element.58.edges, f32[2,32,1024]{2,1,0:T(8,128)S(1)} %collective-permute-done.4.near0, f32[2,32,1024]{2,1,0:T(8,128)S(1)} %collective-permute-done.5.near1, f32[64,16,1024]{2,1,0:T(8,128)} %get-tuple-element.65._), custom_call_target="tpu_custom_call", output_to_operand_aliasing={{}: (3, {})} | custom-call | bytes 1048576 | tf_op jit(solution)/shard_map/patch_near/pallas_call | solution.py:556
  46.1 0.2 collective-permute-done.7.clow
  46.4 0.0 collective-permute-done.8.chigh
  46.4 0.0 collective-permute-done.6.far
  46.4 1.4 %patch_far.1 = (f32[64,16,1024]{2,1,0:T(8,128)}, f32[1,1]{1,0:T(1,128)}) custom-call(f32[4,64,1024]{2,1,0:T(8,128)S(1)} %get-tuple-element.58.edges, f32[2,32,1024]{2,1,0:T(8,128)S(1)} %collective-permute-done.4.near0, f32[2,32,1024]{2,1,0:T(8,128)S(1)} %collective-permute-done.5.near1, ...), custom_call_target="tpu_custom_call", output_to_operand_aliasing={{0}: (7, {})} | custom-call | bytes 1048576 | tf_op jit(solution)/shard_map/patch_far/pallas_call | solution.py:571
  (5 shorter events, 0.1 us)
Async XLA Ops:
  9.8 7.1 %collective-permute-start = (f32[40,1024]{1,0:T(8,128)S(1)}, f32[40,1024]{1,0:T(8,128)S(1)}, u32[]{:S(2)}, u32[]{:S(2)}) collective-permute-start(f32[40,1024]{1,0:T(8,128)S(1)} %get-tuple-element.44), channel_id=1, source_target_pairs={{0,24},{8,16},{16,8},{24,0},{1,25},{9,17},{17,9},{25,1},{2,26},{10... | collective-permute-start | bytes 491528 | tf_op jit(solution)/shard_map/ppermute | solution.py:593
  13.5 32.9 %collective-permute-start.6 = (f32[2,64,1024]{2,1,0:T(8,128)S(1)}, f32[2,64,1024]{2,1,0:T(8,128)S(1)}, u32[]{:S(2)}, u32[]{:S(2)}) collective-permute-start(f32[2,64,1024]{2,1,0:T(8,128)S(1)} %get-tuple-element.60), channel_id=1, source_target_pairs={{0,1},{1,0},{2,3},{3,2},{4,5},{5,4},{6,7},{7,6},{8,9},{9,8},{10,11... | collective-permute-start | bytes 1572872 | tf_op jit(solution)/shard_map/ppermute | solution.py:593
  16.9 7.4 %collective-permute-start.1 = (f32[40,1024]{1,0:T(8,128)S(1)}, f32[40,1024]{1,0:T(8,128)S(1)}, u32[]{:S(2)}, u32[]{:S(2)}) collective-permute-start(f32[40,1024]{1,0:T(8,128)S(1)} %fusion), channel_id=1, source_target_pairs={{0,8},{8,0},{16,24},{24,16},{1,9},{9,1},{17,25},{25,17},{2,10},{10... | collective-permute-start | bytes 491528 | tf_op jit(solution)/shard_map/ppermute | solution.py:593
  17.4 27.9 %collective-permute-start.4 = (f32[2,32,1024]{2,1,0:T(8,128)S(1)}, f32[2,32,1024]{2,1,0:T(8,128)S(1)}, u32[]{:S(2)}, u32[]{:S(2)}) collective-permute-start(f32[2,32,1024]{2,1,0:T(8,128)S(1)} %shard_map.63), channel_id=1, source_target_pairs={{0,7},{1,2},{2,1},{3,4},{4,3},{5,6},{6,5},{7,0},{8,15},{9,10},{10,... | collective-permute-start | bytes 786440 | tf_op jit(solution)/shard_map/ppermute | solution.py:593
  22.5 22.7 %collective-permute-start.5 = (f32[2,32,1024]{2,1,0:T(8,128)S(1)}, f32[2,32,1024]{2,1,0:T(8,128)S(1)}, u32[]{:S(2)}, u32[]{:S(2)}) collective-permute-start(f32[2,32,1024]{2,1,0:T(8,128)S(1)} %get-tuple-element.59), channel_id=1, source_target_pairs={{0,7},{1,2},{2,1},{3,4},{4,3},{5,6},{6,5},{7,0},{8,15},{9,10},{10,... | collective-permute-start | bytes 786440 | tf_op jit(solution)/shard_map/ppermute | solution.py:593
  24.4 10.8 %collective-permute-start.2 = (f32[8,1024]{1,0:T(8,128)S(1)}, f32[8,1024]{1,0:T(8,128)S(1)}, u32[]{:S(2)}, u32[]{:S(2)}) collective-permute-start(f32[8,1024]{1,0:T(8,128)S(1)} %slice_add_fusion), channel_id=1, source_target_pairs={{0,4},{1,5},{2,6},{3,7},{4,0},{5,1},{6,2},{7,3},{8,12},{9,13},{10,... | collective-permute-start | bytes 98312 | tf_op jit(solution)/shard_map/ppermute | solution.py:593
  35.2 4.5 %collective-permute-start.3 = (f32[8,1024]{1,0:T(8,128)S(1)}, f32[8,1024]{1,0:T(8,128)S(1)}, u32[]{:S(2)}, u32[]{:S(2)}) collective-permute-start(f32[8,1024]{1,0:T(8,128)S(1)} %add.15.counts), channel_id=1, source_target_pairs={{0,2},{1,3},{2,0},{3,1},{4,6},{5,7},{6,4},{7,5},{8,10},{9,11},{10,... | collective-permute-start | bytes 98312 | tf_op jit(solution)/shard_map/ppermute | solution.py:593
  39.7 6.7 %collective-permute-start.7 = (f32[8,1024]{1,0:T(8,128)S(1)}, f32[8,1024]{1,0:T(8,128)S(1)}, u32[]{:S(2)}, u32[]{:S(2)}) collective-permute-start(f32[8,1024]{1,0:T(8,128)S(1)} %get-tuple-element.62), channel_id=1, source_target_pairs={{0,1},{1,2},{2,3},{3,4},{4,5},{5,6},{6,7},{7,0},{8,9},{9,10},{10,1... | collective-permute-start | bytes 98312 | tf_op jit(solution)/shard_map/ppermute | solution.py:593
  40.9 5.5 %collective-permute-start.8 = (f32[8,1024]{1,0:T(8,128)S(1)}, f32[8,1024]{1,0:T(8,128)S(1)}, u32[]{:S(2)}, u32[]{:S(2)}) collective-permute-start(f32[8,1024]{1,0:T(8,128)S(1)} %get-tuple-element.63), channel_id=1, source_target_pairs={{0,7},{1,0},{2,1},{3,2},{4,3},{5,4},{6,5},{7,6},{8,15},{9,8},{10,9... | collective-permute-start | bytes 98312 | tf_op jit(solution)/shard_map/ppermute | solution.py:593
